TPU v7x, 32 devices: a whole 2x2x4 slice. The times are simulated.
32 devices in a mesh: gx: 4 (over y, core), gy: 8 (over z, x).
Axes of the slice: x: 2, y: 2, z: 4, core: 2. Of those that a mesh axis runs over, the one named last changes fastest.
Arguments:
- offsets: float32 [2, 8, 64, 128], P(None, 'gx', 'gy'), may hold values from 0 to 1
- masses: float32 [8, 64, 128], P('gx', 'gy'), may hold values from 0.01 to 0.04
- counts: int32 [8, 64], P('gx', 'gy'), may hold values from 1 to 128, as said below
- source: float32 [8, 64, 128], P('gx', 'gy'), may hold values from -6 to 6
Outputs:
- density: float32 [8, 64, 128], P('gx', 'gy')
- pressure: float32 [8, 64, 128], P('gx', 'gy')
- residual: float32 [8, 64, 128], P('gx', 'gy')
- peaks: float32 [5], replicated
Inputs may be any that keep to these rules, and one draw needn't show every extreme that they name: `counts`: each cell's occupied slots come first; some cell holds 128 particles.
All inputs are finite; a program needn't handle non-finite values.
Results may differ from a plain program's by a relative error of at most 0.0003.
Values sent between devices are 32-bit elements; how exact they have to be, the bound alone decides.
No kernel may reach another device: no remote copies, remote signals or barrier semaphores. Data moves between devices by JAX's collectives and lax.ppermute only.
A program may use at most 64 MiB of HBM per device.

v0:
```python
import jax
import jax.numpy as jnp
from jax import lax
from jax.experimental import pallas as pl
from jax.experimental.pallas import tpu as pltpu
from jax.sharding import PartitionSpec as P

ITERS = 5
BASE_STIFF = 0.5
PAIR_SCALE = 0.05
STEPS = [(sx, sy) for sx in (-1, 0, 1) for sy in (-1, 0, 1)]
DEPTH = 1
CHUNK = 32
SHIFTS = (1.0, 0.15, 0.55, 0.8, 0.3)
SCALE = 0.3
GRAM = [(i, j) for i in range(ITERS + 1) for j in range(i, ITERS + 1)]
GRAM_ROWS = -(-len(GRAM) // 8) * 8
LIMIT = pltpu.CompilerParams(vmem_limit_bytes=56 * 1024 * 1024)


def extended(block, axis, dim, width):
    count = lax.axis_size(axis)
    size = block.shape[dim]
    lows, highs = [], []
    hop, left = 1, width
    while left > 0:
        take = min(size, left)
        up = [(i, i + hop) for i in range(count - hop)]
        down = [(i + hop, i) for i in range(count - hop)]
        tail = lax.slice_in_dim(block, size - take, size, axis=dim)
        head = lax.slice_in_dim(block, 0, take, axis=dim)
        lows.insert(0, lax.ppermute(tail, axis, up))
        highs.append(lax.ppermute(head, axis, down))
        hop, left = hop + 1, left - take
    return jnp.concatenate(lows + [block] + highs, axis=dim)


def ghosted(block, width):
    rank = block.ndim
    return extended(extended(block, "gx", rank - 3, width), "gy", rank - 2, width)


def combined(part, combine):
    for axis in ("gx", "gy"):
        count = lax.axis_size(axis)
        window = 1
        while window < count:
            radix = next(k for k in (4, 2, 3, count // window) if (count // window) % k == 0)
            got = [part]
            for k in range(1, radix):
                pairs = [(i, (i + k * window) % count) for i in range(count)]
                got.append(lax.ppermute(part, axis, pairs))
            part = got[0]
            for other in got[1:]:
                part = combine(part, other)
            window *= radix
    return part


def column(row):
    slots = row.shape[-1]
    return jnp.broadcast_to(row, (slots, slots)).T


def folded(parts):
    return jnp.sum(jnp.concatenate(parts, axis=0).T, axis=0, keepdims=True)


def loop_cells(rows, cols, visit):
    def outer(r, carry):
        def inner(c, carry):
            visit(r, c)
            return carry
        return lax.fori_loop(0, cols, inner, carry)
    lax.fori_loop(0, rows, outer, 0)


def setup_kernel(f_ref, dens_ref, w_ref, aux_ref, u_ref, full_ref):
    _, rows_all, cols_all, slots = f_ref.shape
    halo = DEPTH + 2
    rows, cols = rows_all - 2 * halo, cols_all - 2 * halo

    def field(k, r, c):
        return f_ref[k, r, pl.ds(c, 1), :]

    def falloff(xc, yc, r, c, sx, sy):
        dx = (sx + field(0, r + sx, c + sy)) - xc
        dy = (sy + field(1, r + sx, c + sy)) - yc
        return jnp.maximum(1.0 - (dx * dx + dy * dy), 0.0)

    def density(r0, c0):
        r, c = r0 + 1, c0 + 1
        xc, yc = column(field(0, r, c)), column(field(1, r, c))
        parts = []
        for s in range(0, slots, CHUNK):
            acc = jnp.zeros((CHUNK, slots), jnp.float32)
            for sx, sy in STEPS:
                f = falloff(xc[s:s + CHUNK], yc[s:s + CHUNK], r, c, sx, sy)
                acc = acc + f * f * f * field(2, r + sx, c + sy)
            parts.append(acc)
        full_ref[r, pl.ds(c, 1), :] = 1.0 + folded(parts)

    loop_cells(rows_all - 2, cols_all - 2, density)

    def weights(r0, c0):
        r, c = r0 + 2, c0 + 2
        cell = r0 * (cols + 2 * DEPTH) + c0
        xc, yc = column(field(0, r, c)), column(field(1, r, c))
        dc = column(full_ref[r, pl.ds(c, 1), :])
        parts = []
        for s in range(0, slots, CHUNK):
            acc = jnp.zeros((CHUNK, slots), jnp.float32)
            for k, (sx, sy) in enumerate(STEPS):
                f = falloff(xc[s:s + CHUNK], yc[s:s + CHUNK], r, c, sx, sy)
                near = full_ref[r + sx, pl.ds(c + sy, 1), :]
                weight = f * f * (2.0 * PAIR_SCALE) / (dc[s:s + CHUNK] + near)
                w_ref[cell, k, s:s + CHUNK, :] = weight
                live = jnp.where(field(2, r + sx, c + sy) > 0.0, 1.0, 0.0)
                acc = acc + weight * live
            parts.append(acc)
        occupied = jnp.where(field(2, r, c) > 0.0, 1.0, 0.0)
        diagonal = BASE_STIFF + occupied * folded(parts)
        aux_ref[0, r0, pl.ds(c0, 1), :] = diagonal
        aux_ref[1, r0, pl.ds(c0, 1), :] = occupied / diagonal
        u_ref[r0, pl.ds(c0, 1), :] = field(3, r, c) / diagonal

    loop_cells(rows + 2 * DEPTH, cols + 2 * DEPTH, weights)
    dens_ref[...] = full_ref[halo:halo + rows, halo:halo + cols, :]


def product(w_ref, aux_ref, u_ref, out_ref, reach, shift):
    rows, cols, slots = out_ref.shape
    skip = DEPTH - reach
    span = aux_ref.shape[2]

    def visit(r, c):
        cell = (r + skip) * span + (c + skip)
        acc = jnp.zeros((slots, slots), jnp.float32)
        for k, (sx, sy) in enumerate(STEPS):
            acc = acc + w_ref[cell, k] * u_ref[r + 1 + sx, pl.ds(c + 1 + sy, 1), :]
        summed = jnp.sum(acc.T, axis=0, keepdims=True)
        own = u_ref[r + 1, pl.ds(c + 1, 1), :]
        out_ref[r, pl.ds(c, 1), :] = (
            (1.0 - shift) * own - summed * aux_ref[1, r + skip, pl.ds(c + skip, 1), :]
        ) * (1.0 / SCALE)

    loop_cells(rows, cols, visit)


def own_part(ref, rows, cols):
    edge = (ref.shape[-3] - rows) // 2
    if edge == 0:
        return ref[...]
    return ref[..., edge:edge + rows, edge:edge + cols, :]


def products_kernel(first, count, last, *refs):
    w_ref, aux_ref, u_ref = refs[:3]
    earlier = refs[3:3 + (first + 1 if last else 0)]
    tail = refs[3 + len(earlier):]
    outs = tail[:count]
    grids = tail[count + (1 if last else 0):]
    rows, cols, slots = outs[0].shape
    source = u_ref
    for n in range(count):
        reach = count - 1 - n
        target = outs[n] if reach == 0 else grids[n]
        product(w_ref, aux_ref, source, target, reach, SHIFTS[first + n])
        if reach:
            outs[n][...] = own_part(target, rows, cols)
        source = target
    if last:
        gram_ref = tail[count]
        diagonal = own_part(aux_ref, rows, cols)[0]
        basis = [own_part(r, rows, cols) for r in earlier] + [r[...] for r in outs]
        lines = []
        for i, j in GRAM:
            term = basis[i] * basis[j] * diagonal
            lines.append(jnp.sum(jnp.sum(term, axis=0), axis=0, keepdims=True))
        lines += [jnp.zeros((1, slots), jnp.float32)] * (GRAM_ROWS - len(GRAM))
        gram_ref[...] = jnp.concatenate(lines, axis=0)


def solve_kernel(gram_ref, aux_ref, *refs):
    basis_refs = refs[:ITERS + 1]
    pressure_ref, residual_ref, peak_ref = refs[ITERS + 1:]
    rows, cols, slots = pressure_ref.shape
    totals = jnp.sum(gram_ref[...], axis=1, keepdims=True)
    gram = {}
    for n, (i, j) in enumerate(GRAM):
        gram[i, j] = gram[j, i] = totals[n:n + 1, :]
    zero = jnp.zeros((1, 1), jnp.float32)

    def mapped(v):
        out = [None] * (len(v) + 1)
        for k in range(len(v) + 1):
            term = SHIFTS[k] * v[k] if k < len(v) else zero
            out[k] = term + (SCALE * v[k - 1] if k else zero)
        return out

    def inner(a, b):
        total = zero
        for i, ai in enumerate(a):
            line = zero
            for j, bj in enumerate(b):
                line = line + gram[i, j] * bj
            total = total + ai * line
        return total

    def added(a, b, scale):
        size = max(len(a), len(b))
        pad = lambda v: v + [zero] * (size - len(v))
        return [x + scale * y for x, y in zip(pad(a), pad(b))]

    diagonal = own_part(aux_ref, rows, cols)[0]
    basis = [own_part(r, rows, cols) for r in basis_refs]

    def expand(coefs):
        total = None
        for k, coef in enumerate(coefs):
            term = coef.reshape(1, 1, 1) * basis[k]
            total = term if total is None else total + term
        return total

    z = [jnp.ones((1, 1), jnp.float32)]
    p = list(z)
    x = []
    rz = inner(z, z)
    tops = []
    for step in range(ITERS):
        image = mapped(p)
        size = rz / inner(p, image)
        x = added(x, p, size)
        z = added(z, image, -size)
        residual = diagonal * expand(z)
        tops.append(jnp.max(jnp.max(jnp.abs(residual), axis=0), axis=0, keepdims=True))
        if step + 1 < ITERS:
            following = inner(z, z)
            p = added(z, p, following / rz)
            rz = following
    pressure_ref[...] = expand(x)
    residual_ref[...] = residual
    tops += [jnp.zeros((1, slots), jnp.float32)] * (8 - len(tops))
    peak = jnp.max(jnp.concatenate(tops, axis=0), axis=1, keepdims=True)
    peak_ref[...] = jnp.broadcast_to(peak, (8, slots))


def body(offsets, masses, counts, source):
    _, rows, cols, slots = offsets.shape
    f32 = jnp.float32
    live = jnp.arange(slots, dtype=jnp.int32)[None, None, :] < counts[:, :, None]
    fields = jnp.concatenate(
        [offsets, jnp.where(live, masses, 0.0)[None], jnp.where(live, source, 0.0)[None]]
    )
    padded = ghosted(fields, DEPTH + 2)
    span_r, span_c = rows + 2 * DEPTH, cols + 2 * DEPTH
    own = jax.ShapeDtypeStruct((rows, cols, slots), f32)
    density, weight, aux, vector = pl.pallas_call(
        setup_kernel,
        out_shape=(
            own,
            WEIGHT_SPACE((span_r * span_c, len(STEPS), slots, slots), f32),
            jax.ShapeDtypeStruct((2, span_r, span_c, slots), f32),
            jax.ShapeDtypeStruct((span_r, span_c, slots), f32),
        ),
        scratch_shapes=[pltpu.VMEM(padded.shape[1:], f32)],
        compiler_params=LIMIT,
        name="setup",
    )(padded)
    basis = [vector]
    wide = vector
    reach = DEPTH
    while len(basis) <= ITERS:
        if reach == 0:
            reach = min(DEPTH + 1, ITERS + 1 - len(basis))
            wide = ghosted(basis[-1], reach)
        first = len(basis) - 1
        count = reach
        last = first + count == ITERS
        outs = [own] * count
        if last:
            outs.append(jax.ShapeDtypeStruct((GRAM_ROWS, slots), f32))
        grids = [
            pltpu.VMEM((rows + 2 * e, cols + 2 * e, slots), f32) for e in range(count - 1, 0, -1)
        ]
        got = pl.pallas_call(
            lambda *refs, a=first, n=count, z=last: products_kernel(a, n, z, *refs),
            out_shape=tuple(outs),
            scratch_shapes=grids,
            compiler_params=LIMIT,
            name=f"products_{first}",
        )(weight, aux, wide, *(basis if last else []))
        basis += list(got[:count])
        if last:
            gram = got[count]
        reach = 0
    gram = combined(gram, jnp.add)
    pressure, residual, peak = pl.pallas_call(
        solve_kernel,
        out_shape=(own, own, jax.ShapeDtypeStruct((8, slots), f32)),
        compiler_params=LIMIT,
        name="solve",
    )(gram, aux, *basis)
    peak = combined(peak, jnp.maximum)
    return density, pressure, residual, peak[:ITERS, 0]


WEIGHT_SPACE = jax.ShapeDtypeStruct


def solution(mesh):
    in_specs = (P(None, "gx", "gy", None), P("gx", "gy", None), P("gx", "gy"), P("gx", "gy", None))
    out_specs = (P("gx", "gy", None), P("gx", "gy", None), P("gx", "gy", None), P())
    return jax.shard_map(body, mesh=mesh, in_specs=in_specs, out_specs=out_specs, check_vma=False)
```

profile of v0, /device:TPU:0, one launch (start us, length us, event | category | flops | bytes accessed | tf_op | source)
XLA Modules:
  0.0 195.6 jit_solution(17804236168625608090)
XLA Ops:
  2.2 4.9 %collective-permute-start = (f32[4,1,8,128]{3,2,1,0:T(8,128)S(1)}, f32[4,1,8,128]{3,2,1,0:T(8,128)S(1)}, u32[]{:S(2)}, u32[]{:S(2)}) collective-permute-start(f32[4,1,8,128]{3,2,1,0:T(8,128)S(1)} %get-tuple-element.31), channel_id=1, source_target_pairs={{0,16},{8,24},{1,17},{9,25},{2,18},{10,26},{3,19},{11,27},{4,20},{... | collective-permute-start | bytes 49160 | tf_op jit(solution)/shard_map/ppermute | solution.py:32
  7.1 1.3 collective-permute-start.2
  8.4 3.0 %collective-permute-start.1 = (f32[4,2,8,128]{3,2,1,0:T(8,128)S(1)}, f32[4,2,8,128]{3,2,1,0:T(8,128)S(1)}, u32[]{:S(2)}, u32[]{:S(2)}) collective-permute-start(f32[4,2,8,128]{3,2,1,0:T(8,128)S(1)} %pad_maximum_fusion.3), channel_id=1, source_target_pairs={{0,8},{8,16},{16,24},{1,9},{9,17},{17,25},{2,10},{10,18},{18,26},{... | collective-permute-start | bytes 98312 | tf_op jit(solution)/shard_map/ppermute | solution.py:32
  11.4 1.3 collective-permute-start.3
  13.5 3.6 %collective-permute-done.3 = f32[4,1,8,128]{3,2,1,0:T(8,128)S(1)} collective-permute-done((f32[4,1,8,128]{3,2,1,0:T(8,128)S(1)}, f32[4,1,8,128]{3,2,1,0:T(8,128)S(1)}, u32[]{:S(2)}, u32[]{:S(2)}) %collective-permute-start.3) | collective-permute-done | bytes 16416 | tf_op jit(solution)/shard_map/ppermute | solution.py:33
  17.1 3.4 %collective-permute-start.4 = (f32[4,8,3,128]{3,2,1,0:T(4,128)S(1)}, f32[4,8,3,128]{3,2,1,0:T(4,128)S(1)}, u32[]{:S(2)}, u32[]{:S(2)}) collective-permute-start(f32[4,8,3,128]{3,2,1,0:T(4,128)S(1)} %get-tuple-element.28), channel_id=1, source_target_pairs={{0,1},{1,2},{2,3},{3,4},{4,5},{5,6},{6,7},{8,9},{9,10},{10,11},{11... | collective-permute-start | bytes 147464 | tf_op jit(solution)/shard_map/ppermute | solution.py:32
  20.5 1.3 collective-permute-start.5
  22.3 4.3 %collective-permute-done.5 = f32[4,8,3,128]{3,2,1,0:T(4,128)S(1)} collective-permute-done((f32[4,8,3,128]{3,2,1,0:T(4,128)S(1)}, f32[4,8,3,128]{3,2,1,0:T(4,128)S(1)}, u32[]{:S(2)}, u32[]{:S(2)}) %collective-permute-start.5) | collective-permute-done | bytes 49184 | tf_op jit(solution)/shard_map/ppermute | solution.py:33
  27.4 53.0 %setup.1 = (f32[2,8,128]{2,1,0:T(8,128)}, f32[40,9,128,128]{3,2,1,0:T(8,128)}, f32[2,4,10,128]{3,2,1,0:T(8,128)}, f32[4,10,128]{2,1,0:T(8,128)}) custom-call(f32[4,8,14,128]{3,2,1,0:T(8,128)} %pad_maximum_fusion.f_ref), custom_call_target="tpu_custom_call" | custom-call | tf_op jit(solution)/shard_map/setup/pallas_call | solution.py:258
  80.4 10.3 %products_0.1.refs_4_.refs_1_ = f32[2,8,128]{2,1,0:T(8,128)} custom-call(f32[40,9,128,128]{3,2,1,0:T(8,128)} %get-tuple-element.17.refs_0_, f32[2,4,10,128]{3,2,1,0:T(8,128)} %get-tuple-element.18.refs_1_.aux_ref, f32[4,10,128]{2,1,0:T(8,128)} %get-tuple-element.19.refs_2_.refs_3_.refs_0_), custom_call_target="tpu_custom_call" | custom-call | tf_op jit(solution)/shard_map/products_0/pallas_call | solution.py:286
  92.0 3.0 %collective-permute-start.6 = (f32[2,8,128]{2,1,0:T(8,128)}, f32[2,8,128]{2,1,0:T(8,128)S(1)}, u32[]{:S(2)}, u32[]{:S(2)}) collective-permute-start(f32[2,8,128]{2,1,0:T(8,128)} %products_0.1.refs_4_.refs_1_), channel_id=1, source_target_pairs={{0,8},{8,16},{16,24},{1,9},{9,17},{17,25},{2,10},{10,18},{18,26},{... | collective-permute-start | bytes 24584 | tf_op jit(solution)/shard_map/ppermute | solution.py:32
  96.8 4.3 %collective-permute-start.8 = (f32[6,2,128]{2,1,0:T(2,128)S(1)}, f32[6,2,128]{2,1,0:T(2,128)S(1)}, u32[]{:S(2)}, u32[]{:S(2)}) collective-permute-start(f32[6,2,128]{2,1,0:T(2,128)S(1)} %get-tuple-element.34), channel_id=1, source_target_pairs={{0,1},{1,2},{2,3},{3,4},{4,5},{5,6},{6,7},{8,9},{9,10},{10,11},{11... | collective-permute-start | bytes 18440 | tf_op jit(solution)/shard_map/ppermute | solution.py:32
  102.5 4.2 %collective-permute-done.9 = f32[6,2,128]{2,1,0:T(2,128)S(1)} collective-permute-done((f32[6,2,128]{2,1,0:T(2,128)S(1)}, f32[6,2,128]{2,1,0:T(2,128)S(1)}, u32[]{:S(2)}, u32[]{:S(2)}) %collective-permute-start.9) | collective-permute-done | bytes 6176 | tf_op jit(solution)/shard_map/ppermute | solution.py:33
  106.7 1.3 pad_maximum_fusion.1.refs_2_
  108.0 15.2 %products_1.1 = (f32[2,8,128]{2,1,0:T(8,128)}, f32[2,8,128]{2,1,0:T(8,128)}) custom-call(f32[40,9,128,128]{3,2,1,0:T(8,128)} %get-tuple-element.17.refs_0_, f32[2,4,10,128]{3,2,1,0:T(8,128)} %get-tuple-element.18.refs_1_.aux_ref, f32[6,12,128]{2,1,0:T(8,128)} %pad_maximum_fusion.1.refs_2_), custom_call_target="tpu_custom_call" | custom-call | tf_op jit(solution)/shard_map/products_1/pallas_call | solution.py:286
  126.5 3.6 %collective-permute-done.11 = f32[2,8,128]{2,1,0:T(8,128)S(1)} collective-permute-done((f32[2,8,128]{2,1,0:T(8,128)}, f32[2,8,128]{2,1,0:T(8,128)S(1)}, u32[]{:S(2)}, u32[]{:S(2)}) %collective-permute-start.11) | collective-permute-done | bytes 8224 | tf_op jit(solution)/shard_map/ppermute | solution.py:33
  130.1 3.4 %collective-permute-start.12 = (f32[6,2,128]{2,1,0:T(2,128)S(1)}, f32[6,2,128]{2,1,0:T(2,128)S(1)}, u32[]{:S(2)}, u32[]{:S(2)}) collective-permute-start(f32[6,2,128]{2,1,0:T(2,128)S(1)} %get-tuple-element.32), channel_id=1, source_target_pairs={{0,1},{1,2},{2,3},{3,4},{4,5},{5,6},{6,7},{8,9},{9,10},{10,11},{11... | collective-permute-start | bytes 18440 | tf_op jit(solution)/shard_map/ppermute | solution.py:32
  134.9 4.2 %collective-permute-done.13 = f32[6,2,128]{2,1,0:T(2,128)S(1)} collective-permute-done((f32[6,2,128]{2,1,0:T(2,128)S(1)}, f32[6,2,128]{2,1,0:T(2,128)S(1)}, u32[]{:S(2)}, u32[]{:S(2)}) %collective-permute-start.13) | collective-permute-done | bytes 6176 | tf_op jit(solution)/shard_map/ppermute | solution.py:33
  139.7 15.3 %products_3.1 = (f32[2,8,128]{2,1,0:T(8,128)}, f32[2,8,128]{2,1,0:T(8,128)}, f32[24,128]{1,0:T(8,128)}) custom-call(f32[40,9,128,128]{3,2,1,0:T(8,128)} %get-tuple-element.17.refs_0_, f32[2,4,10,128]{3,2,1,0:T(8,128)} %get-tuple-element.18.refs_1_.aux_ref, f32[6,12,128]{2,1,0:T(8,128)} %pad_maximum_fusion.2.refs_2_, ...), custom_call_target="tpu_custom_call" | custom-call | tf_op jit(solution)/shard_map/products_3/pallas_call | solution.py:286
  155.0 2.6 %collective-permute-start.15 = (f32[24,128]{1,0:T(8,128)}, f32[24,128]{1,0:T(8,128)S(1)}, u32[]{:S(2)}, u32[]{:S(2)}) collective-permute-start(f32[24,128]{1,0:T(8,128)} %get-tuple-element.22), channel_id=1, source_target_pairs={{0,16},{8,24},{16,0},{24,8},{1,17},{9,25},{17,1},{25,9},{2,18},{10... | collective-permute-start | bytes 36872 | tf_op jit(solution)/shard_map/ppermute | solution.py:52
  157.6 2.0 %collective-permute-done.15 = f32[24,128]{1,0:T(8,128)S(1)} collective-permute-done((f32[24,128]{1,0:T(8,128)}, f32[24,128]{1,0:T(8,128)S(1)}, u32[]{:S(2)}, u32[]{:S(2)}) %collective-permute-start.15) | collective-permute-done | bytes 12320 | tf_op jit(solution)/shard_map/ppermute | solution.py:52
  159.6 1.3 collective-permute-done.14
  161.6 3.5 %collective-permute-start.19 = (f32[24,128]{1,0:T(8,128)S(1)}, f32[24,128]{1,0:T(8,128)S(1)}, u32[]{:S(2)}, u32[]{:S(2)}) collective-permute-start(f32[24,128]{1,0:T(8,128)S(1)} %add_add_fusion.1), channel_id=1, source_target_pairs={{0,3},{1,4},{2,5},{3,6},{4,7},{5,0},{6,1},{7,2},{8,11},{9,12},{10,... | collective-permute-start | bytes 36872 | tf_op jit(solution)/shard_map/ppermute | solution.py:52
  165.7 1.4 collective-permute-done.19
  167.1 3.5 %collective-permute-done.18 = f32[24,128]{1,0:T(8,128)S(1)} collective-permute-done((f32[24,128]{1,0:T(8,128)S(1)}, f32[24,128]{1,0:T(8,128)S(1)}, u32[]{:S(2)}, u32[]{:S(2)}) %collective-permute-start.18) | collective-permute-done | bytes 12320 | tf_op jit(solution)/shard_map/ppermute | solution.py:52
  172.5 3.9 %collective-permute-done.20 = f32[24,128]{1,0:T(8,128)S(1)} collective-permute-done((f32[24,128]{1,0:T(8,128)S(1)}, f32[24,128]{1,0:T(8,128)S(1)}, u32[]{:S(2)}, u32[]{:S(2)}) %collective-permute-start.20) | collective-permute-done | bytes 12320 | tf_op jit(solution)/shard_map/ppermute | solution.py:52
  177.0 1.8 solve.1
  180.4 2.3 %collective-permute-done.22 = f32[8,128]{1,0:T(8,128)S(1)} collective-permute-done((f32[8,128]{1,0:T(8,128)}, f32[8,128]{1,0:T(8,128)S(1)}, u32[]{:S(2)}, u32[]{:S(2)}) %collective-permute-start.22) | collective-permute-done | bytes 4128 | tf_op jit(solution)/shard_map/ppermute | solution.py:52
  184.0 3.1 %collective-permute-start.24 = (f32[8,128]{1,0:T(8,128)S(1)}, f32[8,128]{1,0:T(8,128)S(1)}, u32[]{:S(2)}, u32[]{:S(2)}) collective-permute-start(f32[8,128]{1,0:T(8,128)S(1)} %maximum_maximum_fusion.1), channel_id=1, source_target_pairs={{0,1},{1,2},{2,3},{3,4},{4,5},{5,6},{6,7},{7,0},{8,9},{9,10},{10,1... | collective-permute-start | bytes 12296 | tf_op jit(solution)/shard_map/ppermute | solution.py:52
  187.1 1.6 collective-permute-done.26
  188.8 1.6 collective-permute-done.24
  191.2 3.8 %collective-permute-done.27 = f32[8,128]{1,0:T(8,128)S(1)} collective-permute-done((f32[8,128]{1,0:T(8,128)S(1)}, f32[8,128]{1,0:T(8,128)S(1)}, u32[]{:S(2)}, u32[]{:S(2)}) %collective-permute-start.27) | collective-permute-done | bytes 4128 | tf_op jit(solution)/shard_map/ppermute | solution.py:52
  (53 shorter events, 21.4 us)
Async XLA Ops:
  2.2 10.5 %collective-permute-start = (f32[4,1,8,128]{3,2,1,0:T(8,128)S(1)}, f32[4,1,8,128]{3,2,1,0:T(8,128)S(1)}, u32[]{:S(2)}, u32[]{:S(2)}) collective-permute-start(f32[4,1,8,128]{3,2,1,0:T(8,128)S(1)} %get-tuple-element.31), channel_id=1, source_target_pairs={{0,16},{8,24},{1,17},{9,25},{2,18},{10,26},{3,19},{11,27},{4,20},{... | collective-permute-start | bytes 49160 | tf_op jit(solution)/shard_map/ppermute | solution.py:32
  7.1 6.4 %collective-permute-start.2 = (f32[4,2,8,128]{3,2,1,0:T(8,128)S(1)}, f32[4,2,8,128]{3,2,1,0:T(8,128)S(1)}, u32[]{:S(2)}, u32[]{:S(2)}) collective-permute-start(f32[4,2,8,128]{3,2,1,0:T(8,128)S(1)} %pad_maximum_fusion.3), channel_id=1, source_target_pairs={{8,0},{16,8},{24,16},{9,1},{17,9},{25,17},{10,2},{18,10},{26,18},{... | collective-permute-start | bytes 98312 | tf_op jit(solution)/shard_map/ppermute | solution.py:33
  8.4 4.4 %collective-permute-start.1 = (f32[4,2,8,128]{3,2,1,0:T(8,128)S(1)}, f32[4,2,8,128]{3,2,1,0:T(8,128)S(1)}, u32[]{:S(2)}, u32[]{:S(2)}) collective-permute-start(f32[4,2,8,128]{3,2,1,0:T(8,128)S(1)} %pad_maximum_fusion.3), channel_id=1, source_target_pairs={{0,8},{8,16},{16,24},{1,9},{9,17},{17,25},{2,10},{10,18},{18,26},{... | collective-permute-start | bytes 98312 | tf_op jit(solution)/shard_map/ppermute | solution.py:32
  11.4 5.6 %collective-permute-start.3 = (f32[4,1,8,128]{3,2,1,0:T(8,128)S(1)}, f32[4,1,8,128]{3,2,1,0:T(8,128)S(1)}, u32[]{:S(2)}, u32[]{:S(2)}) collective-permute-start(f32[4,1,8,128]{3,2,1,0:T(8,128)S(1)} %get-tuple-element.30), channel_id=1, source_target_pairs={{16,0},{24,8},{17,1},{25,9},{18,2},{26,10},{19,3},{27,11},{20,4},{... | collective-permute-start | bytes 49160 | tf_op jit(solution)/shard_map/ppermute | solution.py:33
  17.1 5.3 %collective-permute-start.4 = (f32[4,8,3,128]{3,2,1,0:T(4,128)S(1)}, f32[4,8,3,128]{3,2,1,0:T(4,128)S(1)}, u32[]{:S(2)}, u32[]{:S(2)}) collective-permute-start(f32[4,8,3,128]{3,2,1,0:T(4,128)S(1)} %get-tuple-element.28), channel_id=1, source_target_pairs={{0,1},{1,2},{2,3},{3,4},{4,5},{5,6},{6,7},{8,9},{9,10},{10,11},{11... | collective-permute-start | bytes 147464 | tf_op jit(solution)/shard_map/ppermute | solution.py:32
  20.5 6.2 %collective-permute-start.5 = (f32[4,8,3,128]{3,2,1,0:T(4,128)S(1)}, f32[4,8,3,128]{3,2,1,0:T(4,128)S(1)}, u32[]{:S(2)}, u32[]{:S(2)}) collective-permute-start(f32[4,8,3,128]{3,2,1,0:T(4,128)S(1)} %get-tuple-element.29), channel_id=1, source_target_pairs={{1,0},{2,1},{3,2},{4,3},{5,4},{6,5},{7,6},{9,8},{10,9},{11,10},{12... | collective-permute-start | bytes 147464 | tf_op jit(solution)/shard_map/ppermute | solution.py:33
  90.7 4.3 %collective-permute-start.7 = (f32[2,8,128]{2,1,0:T(8,128)}, f32[2,8,128]{2,1,0:T(8,128)S(1)}, u32[]{:S(2)}, u32[]{:S(2)}) collective-permute-start(f32[2,8,128]{2,1,0:T(8,128)} %products_0.1.refs_4_.refs_1_), channel_id=1, source_target_pairs={{8,0},{16,8},{24,16},{9,1},{17,9},{25,17},{10,2},{18,10},{26,18},{... | collective-permute-start | bytes 24584 | tf_op jit(solution)/shard_map/ppermute | solution.py:33
  92.0 4.1 %collective-permute-start.6 = (f32[2,8,128]{2,1,0:T(8,128)}, f32[2,8,128]{2,1,0:T(8,128)S(1)}, u32[]{:S(2)}, u32[]{:S(2)}) collective-permute-start(f32[2,8,128]{2,1,0:T(8,128)} %products_0.1.refs_4_.refs_1_), channel_id=1, source_target_pairs={{0,8},{8,16},{16,24},{1,9},{9,17},{17,25},{2,10},{10,18},{18,26},{... | collective-permute-start | bytes 24584 | tf_op jit(solution)/shard_map/ppermute | solution.py:32
  96.8 5.7 %collective-permute-start.8 = (f32[6,2,128]{2,1,0:T(2,128)S(1)}, f32[6,2,128]{2,1,0:T(2,128)S(1)}, u32[]{:S(2)}, u32[]{:S(2)}) collective-permute-start(f32[6,2,128]{2,1,0:T(2,128)S(1)} %get-tuple-element.34), channel_id=1, source_target_pairs={{0,1},{1,2},{2,3},{3,4},{4,5},{5,6},{6,7},{8,9},{9,10},{10,11},{11... | collective-permute-start | bytes 18440 | tf_op jit(solution)/shard_map/ppermute | solution.py:32
  101.1 5.5 %collective-permute-start.9 = (f32[6,2,128]{2,1,0:T(2,128)S(1)}, f32[6,2,128]{2,1,0:T(2,128)S(1)}, u32[]{:S(2)}, u32[]{:S(2)}) collective-permute-start(f32[6,2,128]{2,1,0:T(2,128)S(1)} %get-tuple-element.35), channel_id=1, source_target_pairs={{1,0},{2,1},{3,2},{4,3},{5,4},{6,5},{7,6},{9,8},{10,9},{11,10},{12... | collective-permute-start | bytes 18440 | tf_op jit(solution)/shard_map/ppermute | solution.py:33
  123.2 2.6 %collective-permute-start.10 = (f32[2,8,128]{2,1,0:T(8,128)}, f32[2,8,128]{2,1,0:T(8,128)S(1)}, u32[]{:S(2)}, u32[]{:S(2)}) collective-permute-start(f32[2,8,128]{2,1,0:T(8,128)} %get-tuple-element.20.refs_6_.refs_3_), channel_id=1, source_target_pairs={{0,8},{8,16},{16,24},{1,9},{9,17},{17,25},{2,10},{10,18},{18,26},{... | collective-permute-start | bytes 24584 | tf_op jit(solution)/shard_map/ppermute | solution.py:32
  124.5 5.7 %collective-permute-start.11 = (f32[2,8,128]{2,1,0:T(8,128)}, f32[2,8,128]{2,1,0:T(8,128)S(1)}, u32[]{:S(2)}, u32[]{:S(2)}) collective-permute-start(f32[2,8,128]{2,1,0:T(8,128)} %get-tuple-element.20.refs_6_.refs_3_), channel_id=1, source_target_pairs={{8,0},{16,8},{24,16},{9,1},{17,9},{25,17},{10,2},{18,10},{26,18},{... | collective-permute-start | bytes 24584 | tf_op jit(solution)/shard_map/ppermute | solution.py:33
  130.1 4.7 %collective-permute-start.12 = (f32[6,2,128]{2,1,0:T(2,128)S(1)}, f32[6,2,128]{2,1,0:T(2,128)S(1)}, u32[]{:S(2)}, u32[]{:S(2)}) collective-permute-start(f32[6,2,128]{2,1,0:T(2,128)S(1)} %get-tuple-element.32), channel_id=1, source_target_pairs={{0,1},{1,2},{2,3},{3,4},{4,5},{5,6},{6,7},{8,9},{9,10},{10,11},{11... | collective-permute-start | bytes 18440 | tf_op jit(solution)/shard_map/ppermute | solution.py:32
  133.5 5.5 %collective-permute-start.13 = (f32[6,2,128]{2,1,0:T(2,128)S(1)}, f32[6,2,128]{2,1,0:T(2,128)S(1)}, u32[]{:S(2)}, u32[]{:S(2)}) collective-permute-start(f32[6,2,128]{2,1,0:T(2,128)S(1)} %get-tuple-element.33), channel_id=1, source_target_pairs={{1,0},{2,1},{3,2},{4,3},{5,4},{6,5},{7,6},{9,8},{10,9},{11,10},{12... | collective-permute-start | bytes 18440 | tf_op jit(solution)/shard_map/ppermute | solution.py:33
  155.0 2.6 %collective-permute-start.16 = (f32[24,128]{1,0:T(8,128)}, f32[24,128]{1,0:T(8,128)S(1)}, u32[]{:S(2)}, u32[]{:S(2)}) collective-permute-start(f32[24,128]{1,0:T(8,128)} %get-tuple-element.22), channel_id=1, source_target_pairs={{0,24},{8,0},{16,8},{24,16},{1,25},{9,1},{17,9},{25,17},{2,26},{10... | collective-permute-start | bytes 36872 | tf_op jit(solution)/shard_map/ppermute | solution.py:52
  155.0 4.6 %collective-permute-start.15 = (f32[24,128]{1,0:T(8,128)}, f32[24,128]{1,0:T(8,128)S(1)}, u32[]{:S(2)}, u32[]{:S(2)}) collective-permute-start(f32[24,128]{1,0:T(8,128)} %get-tuple-element.22), channel_id=1, source_target_pairs={{0,16},{8,24},{16,0},{24,8},{1,17},{9,25},{17,1},{25,9},{2,18},{10... | collective-permute-start | bytes 36872 | tf_op jit(solution)/shard_map/ppermute | solution.py:52
  157.6 3.3 %collective-permute-start.14 = (f32[24,128]{1,0:T(8,128)}, f32[24,128]{1,0:T(8,128)S(1)}, u32[]{:S(2)}, u32[]{:S(2)}) collective-permute-start(f32[24,128]{1,0:T(8,128)} %get-tuple-element.22), channel_id=1, source_target_pairs={{0,8},{8,16},{16,24},{24,0},{1,9},{9,17},{17,25},{25,1},{2,10},{10... | collective-permute-start | bytes 36872 | tf_op jit(solution)/shard_map/ppermute | solution.py:52
  161.6 5.5 %collective-permute-start.19 = (f32[24,128]{1,0:T(8,128)S(1)}, f32[24,128]{1,0:T(8,128)S(1)}, u32[]{:S(2)}, u32[]{:S(2)}) collective-permute-start(f32[24,128]{1,0:T(8,128)S(1)} %add_add_fusion.1), channel_id=1, source_target_pairs={{0,3},{1,4},{2,5},{3,6},{4,7},{5,0},{6,1},{7,2},{8,11},{9,12},{10,... | collective-permute-start | bytes 36872 | tf_op jit(solution)/shard_map/ppermute | solution.py:52
  165.1 5.5 %collective-permute-start.18 = (f32[24,128]{1,0:T(8,128)S(1)}, f32[24,128]{1,0:T(8,128)S(1)}, u32[]{:S(2)}, u32[]{:S(2)}) collective-permute-start(f32[24,128]{1,0:T(8,128)S(1)} %add_add_fusion.1), channel_id=1, source_target_pairs={{0,2},{1,3},{2,4},{3,5},{4,6},{5,7},{6,0},{7,1},{8,10},{9,11},{10,... | collective-permute-start | bytes 36872 | tf_op jit(solution)/shard_map/ppermute | solution.py:52
  165.4 6.4 %collective-permute-start.17 = (f32[24,128]{1,0:T(8,128)S(1)}, f32[24,128]{1,0:T(8,128)S(1)}, u32[]{:S(2)}, u32[]{:S(2)}) collective-permute-start(f32[24,128]{1,0:T(8,128)S(1)} %add_add_fusion.1), channel_id=1, source_target_pairs={{0,1},{1,2},{2,3},{3,4},{4,5},{5,6},{6,7},{7,0},{8,9},{9,10},{10,1... | collective-permute-start | bytes 36872 | tf_op jit(solution)/shard_map/ppermute | solution.py:52
  171.8 4.6 %collective-permute-start.20 = (f32[24,128]{1,0:T(8,128)S(1)}, f32[24,128]{1,0:T(8,128)S(1)}, u32[]{:S(2)}, u32[]{:S(2)}) collective-permute-start(f32[24,128]{1,0:T(8,128)S(1)} %add_add_fusion), channel_id=1, source_target_pairs={{0,4},{1,5},{2,6},{3,7},{4,0},{5,1},{6,2},{7,3},{8,12},{9,13},{10,... | collective-permute-start | bytes 36872 | tf_op jit(solution)/shard_map/ppermute | solution.py:52
  178.8 1.5 collective-permute-start.23
  178.8 3.8 %collective-permute-start.22 = (f32[8,128]{1,0:T(8,128)}, f32[8,128]{1,0:T(8,128)S(1)}, u32[]{:S(2)}, u32[]{:S(2)}) collective-permute-start(f32[8,128]{1,0:T(8,128)} %get-tuple-element.27), channel_id=1, source_target_pairs={{0,16},{8,24},{16,0},{24,8},{1,17},{9,25},{17,1},{25,9},{2,18},{10... | collective-permute-start | bytes 12296 | tf_op jit(solution)/shard_map/ppermute | solution.py:52
  179.4 3.3 %collective-permute-start.21 = (f32[8,128]{1,0:T(8,128)}, f32[8,128]{1,0:T(8,128)S(1)}, u32[]{:S(2)}, u32[]{:S(2)}) collective-permute-start(f32[8,128]{1,0:T(8,128)} %get-tuple-element.27), channel_id=1, source_target_pairs={{0,8},{8,16},{16,24},{24,0},{1,9},{9,17},{17,25},{25,1},{2,10},{10... | collective-permute-start | bytes 12296 | tf_op jit(solution)/shard_map/ppermute | solution.py:52
  183.4 5.4 %collective-permute-start.26 = (f32[8,128]{1,0:T(8,128)S(1)}, f32[8,128]{1,0:T(8,128)S(1)}, u32[]{:S(2)}, u32[]{:S(2)}) collective-permute-start(f32[8,128]{1,0:T(8,128)S(1)} %maximum_maximum_fusion.1), channel_id=1, source_target_pairs={{0,3},{1,4},{2,5},{3,6},{4,7},{5,0},{6,1},{7,2},{8,11},{9,12},{10,... | collective-permute-start | bytes 12296 | tf_op jit(solution)/shard_map/ppermute | solution.py:52
  183.4 5.4 %collective-permute-start.25 = (f32[8,128]{1,0:T(8,128)S(1)}, f32[8,128]{1,0:T(8,128)S(1)}, u32[]{:S(2)}, u32[]{:S(2)}) collective-permute-start(f32[8,128]{1,0:T(8,128)S(1)} %maximum_maximum_fusion.1), channel_id=1, source_target_pairs={{0,2},{1,3},{2,4},{3,5},{4,6},{5,7},{6,0},{7,1},{8,10},{9,11},{10,... | collective-permute-start | bytes 12296 | tf_op jit(solution)/shard_map/ppermute | solution.py:52
  184.0 6.4 %collective-permute-start.24 = (f32[8,128]{1,0:T(8,128)S(1)}, f32[8,128]{1,0:T(8,128)S(1)}, u32[]{:S(2)}, u32[]{:S(2)}) collective-permute-start(f32[8,128]{1,0:T(8,128)S(1)} %maximum_maximum_fusion.1), channel_id=1, source_target_pairs={{0,1},{1,2},{2,3},{3,4},{4,5},{5,6},{6,7},{7,0},{8,9},{9,10},{10,1... | collective-permute-start | bytes 12296 | tf_op jit(solution)/shard_map/ppermute | solution.py:52
  190.4 4.5 %collective-permute-start.27 = (f32[8,128]{1,0:T(8,128)S(1)}, f32[8,128]{1,0:T(8,128)S(1)}, u32[]{:S(2)}, u32[]{:S(2)}) collective-permute-start(f32[8,128]{1,0:T(8,128)S(1)} %maximum_maximum_fusion), channel_id=1, source_target_pairs={{0,4},{1,5},{2,6},{3,7},{4,0},{5,1},{6,2},{7,3},{8,12},{9,13},{10,... | collective-permute-start | bytes 12296 | tf_op jit(solution)/shard_map/ppermute | solution.py:52
where the time goes:
time: 197 us; the launch traced here: 196 us
  Pallas kernels  95.6 us (49%)
  starting transfers between devices  45.1 us (23%)
  waiting for transfers between devices  44.9 us (23%)
  other arithmetic  7.73 us (4%)
    pallas_call x1, Pallas kernels, body(): pl.pallas_call(setup_kernel, out_shape=(own, WEIGHT_SPACE((span_r * span_...  53 us
    pallas_call x3, Pallas kernels, body(): pl.pallas_call(lambda *refs, a=first, n=count, z=last: products_kernel(a,...  40.8 us
    ppermute x14, waiting for transfers between devices, combined(): got.append(lax.ppermute(part, axis, pairs))  23.4 us
    ppermute x7, starting transfers between devices, extended(): lows.insert(0, lax.ppermute(tail, axis, up))  23.4 us
    ppermute x7, waiting for transfers between devices, extended(): highs.append(lax.ppermute(head, axis, down))  19.9 us
    ppermute x14, starting transfers between devices, combined(): got.append(lax.ppermute(part, axis, pairs))  12.7 us
    ppermute x7, starting transfers between devices, extended(): highs.append(lax.ppermute(head, axis, down))  9.03 us
  transfers between devices with their start and end apart: 28, of which 18 were waited for; matrix products, arithmetic and copies ran while one was open for 1% of the time, Pallas kernels for 0%

commit v1 on v0

--- a/solution.py
+++ b/solution.py
@@ -15,7 +15,7 @@
 SCALE = 0.3
 GRAM = [(i, j) for i in range(ITERS + 1) for j in range(i, ITERS + 1)]
 GRAM_ROWS = -(-len(GRAM) // 8) * 8
-LIMIT = pltpu.CompilerParams(vmem_limit_bytes=56 * 1024 * 1024)
+LIMIT = pltpu.CompilerParams(vmem_limit_bytes=12 * 1024 * 1024)
 
 
 def extended(block, axis, dim, width):
@@ -267,6 +267,7 @@
         compiler_params=LIMIT,
         name="setup",
     )(padded)
+    kept = weight
     basis = [vector]
     wide = vector
     reach = DEPTH
@@ -289,7 +290,7 @@
             scratch_shapes=grids,
             compiler_params=LIMIT,
             name=f"products_{first}",
-        )(weight, aux, wide, *(basis if last else []))
+        )(kept, aux, wide, *(basis if last else []))
         basis += list(got[:count])
         if last:
             gram = got[count]

time: 197 us -> 156 us (0.79)
  Pallas kernels: 95.6 us -> 60.9 us
  other arithmetic: 7.73 us -> 2.36 us
    pallas_call x3, Pallas kernels: 40.8 us -> 15.7 us  [body(): pl.pallas_call(lambda *refs, a=first, n=count, z=last: products_kernel(a,...]
    pallas_call x1, Pallas kernels: 53 us -> 44.3 us  [body(): pl.pallas_call(setup_kernel, out_shape=(own, WEIGHT_SPACE((span_r * span_...]
    concatenate x3, other arithmetic: 2.69 us -> 0.08 us  [extended(): return jnp.concatenate(lows + [block] + highs, axis=dim)]
  transfers between devices with their start and end apart: 28 -> 28, of which waited for: 18 -> 20; matrix products, arithmetic and copies ran while one was open for 1% -> 0% of each run, Pallas kernels for 0% -> 0%
where the time goes in v1:
time: 156 us; the launch traced here: 155 us
  Pallas kernels  60.9 us (39%)
  starting transfers between devices  45.3 us (29%)
  waiting for transfers between devices  44.8 us (29%)
  other arithmetic  2.36 us (2%)
    pallas_call x1, Pallas kernels, body(): pl.pallas_call(setup_kernel, out_shape=(own, WEIGHT_SPACE((span_r * span_...  44.3 us
    ppermute x7, starting transfers between devices, extended(): lows.insert(0, lax.ppermute(tail, axis, up))  23.4 us
    ppermute x14, waiting for transfers between devices, combined(): got.append(lax.ppermute(part, axis, pairs))  23 us
    ppermute x7, waiting for transfers between devices, extended(): highs.append(lax.ppermute(head, axis, down))  20.3 us
    pallas_call x3, Pallas kernels, body(): pl.pallas_call(lambda *refs, a=first, n=count, z=last: products_kernel(a,...  15.7 us
    ppermute x14, starting transfers between devices, combined(): got.append(lax.ppermute(part, axis, pairs))  12.8 us
    ppermute x7, starting transfers between devices, extended(): highs.append(lax.ppermute(head, axis, down))  9.04 us
  transfers between devices with their start and end apart: 28, of which 20 were waited for; matrix products, arithmetic and copies ran while one was open for 0% of the time, Pallas kernels for 0%

profile of v1, /device:TPU:0, one launch (start us, length us, event | category | flops | bytes accessed | tf_op | source)
XLA Modules:
  0.0 154.9 jit_solution(7377192210397691407)
XLA Ops:
  2.2 4.9 %collective-permute-start = (f32[4,1,8,128]{3,2,1,0:T(8,128)S(1)}, f32[4,1,8,128]{3,2,1,0:T(8,128)S(1)}, u32[]{:S(2)}, u32[]{:S(2)}) collective-permute-start(f32[4,1,8,128]{3,2,1,0:T(8,128)S(1)} %get-tuple-element.31), channel_id=1, source_target_pairs={{0,16},{8,24},{1,17},{9,25},{2,18},{10,26},{3,19},{11,27},{4,20},{... | collective-permute-start | bytes 49160 | tf_op jit(solution)/shard_map/ppermute | solution.py:32
  7.1 1.3 collective-permute-start.2
  8.4 3.0 %collective-permute-start.1 = (f32[4,2,8,128]{3,2,1,0:T(8,128)S(1)}, f32[4,2,8,128]{3,2,1,0:T(8,128)S(1)}, u32[]{:S(2)}, u32[]{:S(2)}) collective-permute-start(f32[4,2,8,128]{3,2,1,0:T(8,128)S(1)} %pad_maximum_fusion.3), channel_id=1, source_target_pairs={{0,8},{8,16},{16,24},{1,9},{9,17},{17,25},{2,10},{10,18},{18,26},{... | collective-permute-start | bytes 98312 | tf_op jit(solution)/shard_map/ppermute | solution.py:32
  11.4 1.3 collective-permute-start.3
  13.5 3.6 %collective-permute-done.3 = f32[4,1,8,128]{3,2,1,0:T(8,128)S(1)} collective-permute-done((f32[4,1,8,128]{3,2,1,0:T(8,128)S(1)}, f32[4,1,8,128]{3,2,1,0:T(8,128)S(1)}, u32[]{:S(2)}, u32[]{:S(2)}) %collective-permute-start.3) | collective-permute-done | bytes 16416 | tf_op jit(solution)/shard_map/ppermute | solution.py:33
  17.1 3.4 %collective-permute-start.4 = (f32[4,8,3,128]{3,2,1,0:T(4,128)S(1)}, f32[4,8,3,128]{3,2,1,0:T(4,128)S(1)}, u32[]{:S(2)}, u32[]{:S(2)}) collective-permute-start(f32[4,8,3,128]{3,2,1,0:T(4,128)S(1)} %get-tuple-element.28), channel_id=1, source_target_pairs={{0,1},{1,2},{2,3},{3,4},{4,5},{5,6},{6,7},{8,9},{9,10},{10,11},{11... | collective-permute-start | bytes 147464 | tf_op jit(solution)/shard_map/ppermute | solution.py:32
  20.5 1.3 collective-permute-start.5
  22.3 4.3 %collective-permute-done.5 = f32[4,8,3,128]{3,2,1,0:T(4,128)S(1)} collective-permute-done((f32[4,8,3,128]{3,2,1,0:T(4,128)S(1)}, f32[4,8,3,128]{3,2,1,0:T(4,128)S(1)}, u32[]{:S(2)}, u32[]{:S(2)}) %collective-permute-start.5) | collective-permute-done | bytes 49184 | tf_op jit(solution)/shard_map/ppermute | solution.py:33
  26.7 44.3 %setup.1 = (f32[2,8,128]{2,1,0:T(8,128)}, f32[40,9,128,128]{3,2,1,0:T(8,128)S(1)}, f32[2,4,10,128]{3,2,1,0:T(8,128)S(1)}, f32[4,10,128]{2,1,0:T(8,128)S(1)}) custom-call(f32[4,8,14,128]{3,2,1,0:T(8,128)S(1)} %pad_maximum_fusion.f_ref), custom_call_target="tpu_custom_call" | custom-call | tf_op jit(solution)/shard_map/setup/pallas_call | solution.py:258
  70.9 2.0 %products_0.1.refs_4_.refs_1_ = f32[2,8,128]{2,1,0:T(8,128)S(1)} custom-call(f32[40,9,128,128]{3,2,1,0:T(8,128)S(1)} %get-tuple-element.17.refs_0_, f32[2,4,10,128]{3,2,1,0:T(8,128)S(1)} %get-tuple-element.18.refs_1_.aux_ref, f32[4,10,128]{2,1,0:T(8,128)S(1)} %get-tuple-element.19.refs_2_.refs_3_.refs_0_), custom_call_target="tpu_custom_call" | custom-call | tf_op jit(solution)/shard_map/products_0/pallas_call | solution.py:287
  72.9 1.3 collective-permute-start.7
  74.2 3.0 %collective-permute-start.6 = (f32[2,8,128]{2,1,0:T(8,128)S(1)}, f32[2,8,128]{2,1,0:T(8,128)S(1)}, u32[]{:S(2)}, u32[]{:S(2)}) collective-permute-start(f32[2,8,128]{2,1,0:T(8,128)S(1)} %products_0.1.refs_4_.refs_1_), channel_id=1, source_target_pairs={{0,8},{8,16},{16,24},{1,9},{9,17},{17,25},{2,10},{10,18},{18,26},{... | collective-permute-start | bytes 24584 | tf_op jit(solution)/shard_map/ppermute | solution.py:32
  78.0 4.3 %collective-permute-start.8 = (f32[6,2,128]{2,1,0:T(2,128)S(1)}, f32[6,2,128]{2,1,0:T(2,128)S(1)}, u32[]{:S(2)}, u32[]{:S(2)}) collective-permute-start(f32[6,2,128]{2,1,0:T(2,128)S(1)} %get-tuple-element.34), channel_id=1, source_target_pairs={{0,1},{1,2},{2,3},{3,4},{4,5},{5,6},{6,7},{8,9},{9,10},{10,11},{11... | collective-permute-start | bytes 18440 | tf_op jit(solution)/shard_map/ppermute | solution.py:32
  82.4 1.3 collective-permute-start.9
  83.7 4.2 %collective-permute-done.9 = f32[6,2,128]{2,1,0:T(2,128)S(1)} collective-permute-done((f32[6,2,128]{2,1,0:T(2,128)S(1)}, f32[6,2,128]{2,1,0:T(2,128)S(1)}, u32[]{:S(2)}, u32[]{:S(2)}) %collective-permute-start.9) | collective-permute-done | bytes 6176 | tf_op jit(solution)/shard_map/ppermute | solution.py:33
  87.9 6.9 %products_1.1 = (f32[2,8,128]{2,1,0:T(8,128)S(1)}, f32[2,8,128]{2,1,0:T(8,128)S(1)}) custom-call(f32[40,9,128,128]{3,2,1,0:T(8,128)S(1)} %get-tuple-element.17.refs_0_, f32[2,4,10,128]{3,2,1,0:T(8,128)S(1)} %get-tuple-element.18.refs_1_.aux_ref, f32[6,12,128]{2,1,0:T(8,128)S(1)} %pad_maximum_fusion.1.refs_2_), custom_call_target="tpu_custom_call" | custom-call | tf_op jit(solution)/shard_map/products_1/pallas_call | solution.py:287
  97.4 4.1 %collective-permute-done.11 = f32[2,8,128]{2,1,0:T(8,128)S(1)} collective-permute-done((f32[2,8,128]{2,1,0:T(8,128)S(1)}, f32[2,8,128]{2,1,0:T(8,128)S(1)}, u32[]{:S(2)}, u32[]{:S(2)}) %collective-permute-start.11) | collective-permute-done | bytes 8224 | tf_op jit(solution)/shard_map/ppermute | solution.py:33
  101.5 3.4 %collective-permute-start.12 = (f32[6,2,128]{2,1,0:T(2,128)S(1)}, f32[6,2,128]{2,1,0:T(2,128)S(1)}, u32[]{:S(2)}, u32[]{:S(2)}) collective-permute-start(f32[6,2,128]{2,1,0:T(2,128)S(1)} %get-tuple-element.32), channel_id=1, source_target_pairs={{0,1},{1,2},{2,3},{3,4},{4,5},{5,6},{6,7},{8,9},{9,10},{10,11},{11... | collective-permute-start | bytes 18440 | tf_op jit(solution)/shard_map/ppermute | solution.py:32
  106.3 4.2 %collective-permute-done.13 = f32[6,2,128]{2,1,0:T(2,128)S(1)} collective-permute-done((f32[6,2,128]{2,1,0:T(2,128)S(1)}, f32[6,2,128]{2,1,0:T(2,128)S(1)}, u32[]{:S(2)}, u32[]{:S(2)}) %collective-permute-start.13) | collective-permute-done | bytes 6176 | tf_op jit(solution)/shard_map/ppermute | solution.py:33
  110.5 6.9 %products_3.1 = (f32[2,8,128]{2,1,0:T(8,128)S(1)}, f32[2,8,128]{2,1,0:T(8,128)S(1)}, f32[24,128]{1,0:T(8,128)S(1)}) custom-call(f32[40,9,128,128]{3,2,1,0:T(8,128)S(1)} %get-tuple-element.17.refs_0_, f32[2,4,10,128]{3,2,1,0:T(8,128)S(1)} %get-tuple-element.18.refs_1_.aux_ref, f32[6,12,128]{2,1,0:T(8,128)S(1)} %pad_maximum_fusion.2.refs_2_, ...), custom_call_target="tpu_custom_call" | custom-call | tf_op jit(solution)/shard_map/products_3/pallas_call | solution.py:287
  117.5 2.6 %collective-permute-start.15 = (f32[24,128]{1,0:T(8,128)S(1)}, f32[24,128]{1,0:T(8,128)S(1)}, u32[]{:S(2)}, u32[]{:S(2)}) collective-permute-start(f32[24,128]{1,0:T(8,128)S(1)} %get-tuple-element.22), channel_id=1, source_target_pairs={{0,16},{8,24},{16,0},{24,8},{1,17},{9,25},{17,1},{25,9},{2,18},{10... | collective-permute-start | bytes 36872 | tf_op jit(solution)/shard_map/ppermute | solution.py:52
  120.1 1.8 %collective-permute-done.15 = f32[24,128]{1,0:T(8,128)S(1)} collective-permute-done((f32[24,128]{1,0:T(8,128)S(1)}, f32[24,128]{1,0:T(8,128)S(1)}, u32[]{:S(2)}, u32[]{:S(2)}) %collective-permute-start.15) | collective-permute-done | bytes 12320 | tf_op jit(solution)/shard_map/ppermute | solution.py:52
  121.9 1.3 collective-permute-done.14
  123.2 3.5 %collective-permute-start.19 = (f32[24,128]{1,0:T(8,128)S(1)}, f32[24,128]{1,0:T(8,128)S(1)}, u32[]{:S(2)}, u32[]{:S(2)}) collective-permute-start(f32[24,128]{1,0:T(8,128)S(1)} %add_add_fusion.1), channel_id=1, source_target_pairs={{0,3},{1,4},{2,5},{3,6},{4,7},{5,0},{6,1},{7,2},{8,11},{9,12},{10,... | collective-permute-start | bytes 36872 | tf_op jit(solution)/shard_map/ppermute | solution.py:52
  127.3 1.4 collective-permute-done.19
  128.7 3.5 %collective-permute-done.18 = f32[24,128]{1,0:T(8,128)S(1)} collective-permute-done((f32[24,128]{1,0:T(8,128)S(1)}, f32[24,128]{1,0:T(8,128)S(1)}, u32[]{:S(2)}, u32[]{:S(2)}) %collective-permute-start.18) | collective-permute-done | bytes 12320 | tf_op jit(solution)/shard_map/ppermute | solution.py:52
  134.1 3.8 %collective-permute-done.20 = f32[24,128]{1,0:T(8,128)S(1)} collective-permute-done((f32[24,128]{1,0:T(8,128)S(1)}, f32[24,128]{1,0:T(8,128)S(1)}, u32[]{:S(2)}, u32[]{:S(2)}) %collective-permute-start.20) | collective-permute-done | bytes 12320 | tf_op jit(solution)/shard_map/ppermute | solution.py:52
  140.2 2.3 %collective-permute-done.22 = f32[8,128]{1,0:T(8,128)S(1)} collective-permute-done((f32[8,128]{1,0:T(8,128)S(1)}, f32[8,128]{1,0:T(8,128)S(1)}, u32[]{:S(2)}, u32[]{:S(2)}) %collective-permute-start.22) | collective-permute-done | bytes 4128 | tf_op jit(solution)/shard_map/ppermute | solution.py:52
  143.2 3.2 %collective-permute-start.24 = (f32[8,128]{1,0:T(8,128)S(1)}, f32[8,128]{1,0:T(8,128)S(1)}, u32[]{:S(2)}, u32[]{:S(2)}) collective-permute-start(f32[8,128]{1,0:T(8,128)S(1)} %maximum_maximum_fusion.1), channel_id=1, source_target_pairs={{0,1},{1,2},{2,3},{3,4},{4,5},{5,6},{6,7},{7,0},{8,9},{9,10},{10,1... | collective-permute-start | bytes 12296 | tf_op jit(solution)/shard_map/ppermute | solution.py:52
  146.4 1.6 %collective-permute-done.26 = f32[8,128]{1,0:T(8,128)S(1)} collective-permute-done((f32[8,128]{1,0:T(8,128)S(1)}, f32[8,128]{1,0:T(8,128)S(1)}, u32[]{:S(2)}, u32[]{:S(2)}) %collective-permute-start.26) | collective-permute-done | bytes 4128 | tf_op jit(solution)/shard_map/ppermute | solution.py:52
  148.0 1.7 %collective-permute-done.24 = f32[8,128]{1,0:T(8,128)S(1)} collective-permute-done((f32[8,128]{1,0:T(8,128)S(1)}, f32[8,128]{1,0:T(8,128)S(1)}, u32[]{:S(2)}, u32[]{:S(2)}) %collective-permute-start.24) | collective-permute-done | bytes 4128 | tf_op jit(solution)/shard_map/ppermute | solution.py:52
  150.3 3.9 %collective-permute-done.27 = f32[8,128]{1,0:T(8,128)S(1)} collective-permute-done((f32[8,128]{1,0:T(8,128)S(1)}, f32[8,128]{1,0:T(8,128)S(1)}, u32[]{:S(2)}, u32[]{:S(2)}) %collective-permute-start.27) | collective-permute-done | bytes 4128 | tf_op jit(solution)/shard_map/ppermute | solution.py:52
  (53 shorter events, 14.7 us)
Async XLA Ops:
  2.2 10.5 %collective-permute-start = (f32[4,1,8,128]{3,2,1,0:T(8,128)S(1)}, f32[4,1,8,128]{3,2,1,0:T(8,128)S(1)}, u32[]{:S(2)}, u32[]{:S(2)}) collective-permute-start(f32[4,1,8,128]{3,2,1,0:T(8,128)S(1)} %get-tuple-element.31), channel_id=1, source_target_pairs={{0,16},{8,24},{1,17},{9,25},{2,18},{10,26},{3,19},{11,27},{4,20},{... | collective-permute-start | bytes 49160 | tf_op jit(solution)/shard_map/ppermute | solution.py:32
  7.1 6.4 %collective-permute-start.2 = (f32[4,2,8,128]{3,2,1,0:T(8,128)S(1)}, f32[4,2,8,128]{3,2,1,0:T(8,128)S(1)}, u32[]{:S(2)}, u32[]{:S(2)}) collective-permute-start(f32[4,2,8,128]{3,2,1,0:T(8,128)S(1)} %pad_maximum_fusion.3), channel_id=1, source_target_pairs={{8,0},{16,8},{24,16},{9,1},{17,9},{25,17},{10,2},{18,10},{26,18},{... | collective-permute-start | bytes 98312 | tf_op jit(solution)/shard_map/ppermute | solution.py:33
  8.4 4.4 %collective-permute-start.1 = (f32[4,2,8,128]{3,2,1,0:T(8,128)S(1)}, f32[4,2,8,128]{3,2,1,0:T(8,128)S(1)}, u32[]{:S(2)}, u32[]{:S(2)}) collective-permute-start(f32[4,2,8,128]{3,2,1,0:T(8,128)S(1)} %pad_maximum_fusion.3), channel_id=1, source_target_pairs={{0,8},{8,16},{16,24},{1,9},{9,17},{17,25},{2,10},{10,18},{18,26},{... | collective-permute-start | bytes 98312 | tf_op jit(solution)/shard_map/ppermute | solution.py:32
  11.4 5.6 %collective-permute-start.3 = (f32[4,1,8,128]{3,2,1,0:T(8,128)S(1)}, f32[4,1,8,128]{3,2,1,0:T(8,128)S(1)}, u32[]{:S(2)}, u32[]{:S(2)}) collective-permute-start(f32[4,1,8,128]{3,2,1,0:T(8,128)S(1)} %get-tuple-element.30), channel_id=1, source_target_pairs={{16,0},{24,8},{17,1},{25,9},{18,2},{26,10},{19,3},{27,11},{20,4},{... | collective-permute-start | bytes 49160 | tf_op jit(solution)/shard_map/ppermute | solution.py:33
  17.1 5.3 %collective-permute-start.4 = (f32[4,8,3,128]{3,2,1,0:T(4,128)S(1)}, f32[4,8,3,128]{3,2,1,0:T(4,128)S(1)}, u32[]{:S(2)}, u32[]{:S(2)}) collective-permute-start(f32[4,8,3,128]{3,2,1,0:T(4,128)S(1)} %get-tuple-element.28), channel_id=1, source_target_pairs={{0,1},{1,2},{2,3},{3,4},{4,5},{5,6},{6,7},{8,9},{9,10},{10,11},{11... | collective-permute-start | bytes 147464 | tf_op jit(solution)/shard_map/ppermute | solution.py:32
  20.5 6.2 %collective-permute-start.5 = (f32[4,8,3,128]{3,2,1,0:T(4,128)S(1)}, f32[4,8,3,128]{3,2,1,0:T(4,128)S(1)}, u32[]{:S(2)}, u32[]{:S(2)}) collective-permute-start(f32[4,8,3,128]{3,2,1,0:T(4,128)S(1)} %get-tuple-element.29), channel_id=1, source_target_pairs={{1,0},{2,1},{3,2},{4,3},{5,4},{6,5},{7,6},{9,8},{10,9},{11,10},{12... | collective-permute-start | bytes 147464 | tf_op jit(solution)/shard_map/ppermute | solution.py:33
  72.9 4.3 %collective-permute-start.7 = (f32[2,8,128]{2,1,0:T(8,128)S(1)}, f32[2,8,128]{2,1,0:T(8,128)S(1)}, u32[]{:S(2)}, u32[]{:S(2)}) collective-permute-start(f32[2,8,128]{2,1,0:T(8,128)S(1)} %products_0.1.refs_4_.refs_1_), channel_id=1, source_target_pairs={{8,0},{16,8},{24,16},{9,1},{17,9},{25,17},{10,2},{18,10},{26,18},{... | collective-permute-start | bytes 24584 | tf_op jit(solution)/shard_map/ppermute | solution.py:33
  74.2 3.8 %collective-permute-start.6 = (f32[2,8,128]{2,1,0:T(8,128)S(1)}, f32[2,8,128]{2,1,0:T(8,128)S(1)}, u32[]{:S(2)}, u32[]{:S(2)}) collective-permute-start(f32[2,8,128]{2,1,0:T(8,128)S(1)} %products_0.1.refs_4_.refs_1_), channel_id=1, source_target_pairs={{0,8},{8,16},{16,24},{1,9},{9,17},{17,25},{2,10},{10,18},{18,26},{... | collective-permute-start | bytes 24584 | tf_op jit(solution)/shard_map/ppermute | solution.py:32
  78.0 5.7 %collective-permute-start.8 = (f32[6,2,128]{2,1,0:T(2,128)S(1)}, f32[6,2,128]{2,1,0:T(2,128)S(1)}, u32[]{:S(2)}, u32[]{:S(2)}) collective-permute-start(f32[6,2,128]{2,1,0:T(2,128)S(1)} %get-tuple-element.34), channel_id=1, source_target_pairs={{0,1},{1,2},{2,3},{3,4},{4,5},{5,6},{6,7},{8,9},{9,10},{10,11},{11... | collective-permute-start | bytes 18440 | tf_op jit(solution)/shard_map/ppermute | solution.py:32
  82.4 5.5 %collective-permute-start.9 = (f32[6,2,128]{2,1,0:T(2,128)S(1)}, f32[6,2,128]{2,1,0:T(2,128)S(1)}, u32[]{:S(2)}, u32[]{:S(2)}) collective-permute-start(f32[6,2,128]{2,1,0:T(2,128)S(1)} %get-tuple-element.35), channel_id=1, source_target_pairs={{1,0},{2,1},{3,2},{4,3},{5,4},{6,5},{7,6},{9,8},{10,9},{11,10},{12... | collective-permute-start | bytes 18440 | tf_op jit(solution)/shard_map/ppermute | solution.py:33
  94.8 2.6 %collective-permute-start.10 = (f32[2,8,128]{2,1,0:T(8,128)S(1)}, f32[2,8,128]{2,1,0:T(8,128)S(1)}, u32[]{:S(2)}, u32[]{:S(2)}) collective-permute-start(f32[2,8,128]{2,1,0:T(8,128)S(1)} %get-tuple-element.20.refs_6_.refs_3_), channel_id=1, source_target_pairs={{0,8},{8,16},{16,24},{1,9},{9,17},{17,25},{2,10},{10,18},{18,26},{... | collective-permute-start | bytes 24584 | tf_op jit(solution)/shard_map/ppermute | solution.py:32
  96.1 5.4 %collective-permute-start.11 = (f32[2,8,128]{2,1,0:T(8,128)S(1)}, f32[2,8,128]{2,1,0:T(8,128)S(1)}, u32[]{:S(2)}, u32[]{:S(2)}) collective-permute-start(f32[2,8,128]{2,1,0:T(8,128)S(1)} %get-tuple-element.20.refs_6_.refs_3_), channel_id=1, source_target_pairs={{8,0},{16,8},{24,16},{9,1},{17,9},{25,17},{10,2},{18,10},{26,18},{... | collective-permute-start | bytes 24584 | tf_op jit(solution)/shard_map/ppermute | solution.py:33
  101.5 4.7 %collective-permute-start.12 = (f32[6,2,128]{2,1,0:T(2,128)S(1)}, f32[6,2,128]{2,1,0:T(2,128)S(1)}, u32[]{:S(2)}, u32[]{:S(2)}) collective-permute-start(f32[6,2,128]{2,1,0:T(2,128)S(1)} %get-tuple-element.32), channel_id=1, source_target_pairs={{0,1},{1,2},{2,3},{3,4},{4,5},{5,6},{6,7},{8,9},{9,10},{10,11},{11... | collective-permute-start | bytes 18440 | tf_op jit(solution)/shard_map/ppermute | solution.py:32
  105.0 5.5 %collective-permute-start.13 = (f32[6,2,128]{2,1,0:T(2,128)S(1)}, f32[6,2,128]{2,1,0:T(2,128)S(1)}, u32[]{:S(2)}, u32[]{:S(2)}) collective-permute-start(f32[6,2,128]{2,1,0:T(2,128)S(1)} %get-tuple-element.33), channel_id=1, source_target_pairs={{1,0},{2,1},{3,2},{4,3},{5,4},{6,5},{7,6},{9,8},{10,9},{11,10},{12... | collective-permute-start | bytes 18440 | tf_op jit(solution)/shard_map/ppermute | solution.py:33
  117.4 2.7 %collective-permute-start.16 = (f32[24,128]{1,0:T(8,128)S(1)}, f32[24,128]{1,0:T(8,128)S(1)}, u32[]{:S(2)}, u32[]{:S(2)}) collective-permute-start(f32[24,128]{1,0:T(8,128)S(1)} %get-tuple-element.22), channel_id=1, source_target_pairs={{0,24},{8,0},{16,8},{24,16},{1,25},{9,1},{17,9},{25,17},{2,26},{10... | collective-permute-start | bytes 36872 | tf_op jit(solution)/shard_map/ppermute | solution.py:52
  117.5 4.4 %collective-permute-start.15 = (f32[24,128]{1,0:T(8,128)S(1)}, f32[24,128]{1,0:T(8,128)S(1)}, u32[]{:S(2)}, u32[]{:S(2)}) collective-permute-start(f32[24,128]{1,0:T(8,128)S(1)} %get-tuple-element.22), channel_id=1, source_target_pairs={{0,16},{8,24},{16,0},{24,8},{1,17},{9,25},{17,1},{25,9},{2,18},{10... | collective-permute-start | bytes 36872 | tf_op jit(solution)/shard_map/ppermute | solution.py:52
  120.1 3.1 %collective-permute-start.14 = (f32[24,128]{1,0:T(8,128)S(1)}, f32[24,128]{1,0:T(8,128)S(1)}, u32[]{:S(2)}, u32[]{:S(2)}) collective-permute-start(f32[24,128]{1,0:T(8,128)S(1)} %get-tuple-element.22), channel_id=1, source_target_pairs={{0,8},{8,16},{16,24},{24,0},{1,9},{9,17},{17,25},{25,1},{2,10},{10... | collective-permute-start | bytes 36872 | tf_op jit(solution)/shard_map/ppermute | solution.py:52
  123.2 5.5 %collective-permute-start.19 = (f32[24,128]{1,0:T(8,128)S(1)}, f32[24,128]{1,0:T(8,128)S(1)}, u32[]{:S(2)}, u32[]{:S(2)}) collective-permute-start(f32[24,128]{1,0:T(8,128)S(1)} %add_add_fusion.1), channel_id=1, source_target_pairs={{0,3},{1,4},{2,5},{3,6},{4,7},{5,0},{6,1},{7,2},{8,11},{9,12},{10,... | collective-permute-start | bytes 36872 | tf_op jit(solution)/shard_map/ppermute | solution.py:52
  126.7 5.5 %collective-permute-start.18 = (f32[24,128]{1,0:T(8,128)S(1)}, f32[24,128]{1,0:T(8,128)S(1)}, u32[]{:S(2)}, u32[]{:S(2)}) collective-permute-start(f32[24,128]{1,0:T(8,128)S(1)} %add_add_fusion.1), channel_id=1, source_target_pairs={{0,2},{1,3},{2,4},{3,5},{4,6},{5,7},{6,0},{7,1},{8,10},{9,11},{10,... | collective-permute-start | bytes 36872 | tf_op jit(solution)/shard_map/ppermute | solution.py:52
  127.0 6.4 %collective-permute-start.17 = (f32[24,128]{1,0:T(8,128)S(1)}, f32[24,128]{1,0:T(8,128)S(1)}, u32[]{:S(2)}, u32[]{:S(2)}) collective-permute-start(f32[24,128]{1,0:T(8,128)S(1)} %add_add_fusion.1), channel_id=1, source_target_pairs={{0,1},{1,2},{2,3},{3,4},{4,5},{5,6},{6,7},{7,0},{8,9},{9,10},{10,1... | collective-permute-start | bytes 36872 | tf_op jit(solution)/shard_map/ppermute | solution.py:52
  133.4 4.6 %collective-permute-start.20 = (f32[24,128]{1,0:T(8,128)S(1)}, f32[24,128]{1,0:T(8,128)S(1)}, u32[]{:S(2)}, u32[]{:S(2)}) collective-permute-start(f32[24,128]{1,0:T(8,128)S(1)} %add_add_fusion), channel_id=1, source_target_pairs={{0,4},{1,5},{2,6},{3,7},{4,0},{5,1},{6,2},{7,3},{8,12},{9,13},{10,... | collective-permute-start | bytes 36872 | tf_op jit(solution)/shard_map/ppermute | solution.py:52
  138.9 1.3 collective-permute-start.23
  138.9 3.6 %collective-permute-start.22 = (f32[8,128]{1,0:T(8,128)S(1)}, f32[8,128]{1,0:T(8,128)S(1)}, u32[]{:S(2)}, u32[]{:S(2)}) collective-permute-start(f32[8,128]{1,0:T(8,128)S(1)} %get-tuple-element.27), channel_id=1, source_target_pairs={{0,16},{8,24},{16,0},{24,8},{1,17},{9,25},{17,1},{25,9},{2,18},{10... | collective-permute-start | bytes 12296 | tf_op jit(solution)/shard_map/ppermute | solution.py:52
  139.5 3.0 %collective-permute-start.21 = (f32[8,128]{1,0:T(8,128)S(1)}, f32[8,128]{1,0:T(8,128)S(1)}, u32[]{:S(2)}, u32[]{:S(2)}) collective-permute-start(f32[8,128]{1,0:T(8,128)S(1)} %get-tuple-element.27), channel_id=1, source_target_pairs={{0,8},{8,16},{16,24},{24,0},{1,9},{9,17},{17,25},{25,1},{2,10},{10... | collective-permute-start | bytes 12296 | tf_op jit(solution)/shard_map/ppermute | solution.py:52
  142.6 5.4 %collective-permute-start.26 = (f32[8,128]{1,0:T(8,128)S(1)}, f32[8,128]{1,0:T(8,128)S(1)}, u32[]{:S(2)}, u32[]{:S(2)}) collective-permute-start(f32[8,128]{1,0:T(8,128)S(1)} %maximum_maximum_fusion.1), channel_id=1, source_target_pairs={{0,3},{1,4},{2,5},{3,6},{4,7},{5,0},{6,1},{7,2},{8,11},{9,12},{10,... | collective-permute-start | bytes 12296 | tf_op jit(solution)/shard_map/ppermute | solution.py:52
  142.6 5.5 %collective-permute-start.25 = (f32[8,128]{1,0:T(8,128)S(1)}, f32[8,128]{1,0:T(8,128)S(1)}, u32[]{:S(2)}, u32[]{:S(2)}) collective-permute-start(f32[8,128]{1,0:T(8,128)S(1)} %maximum_maximum_fusion.1), channel_id=1, source_target_pairs={{0,2},{1,3},{2,4},{3,5},{4,6},{5,7},{6,0},{7,1},{8,10},{9,11},{10,... | collective-permute-start | bytes 12296 | tf_op jit(solution)/shard_map/ppermute | solution.py:52
  143.2 6.5 %collective-permute-start.24 = (f32[8,128]{1,0:T(8,128)S(1)}, f32[8,128]{1,0:T(8,128)S(1)}, u32[]{:S(2)}, u32[]{:S(2)}) collective-permute-start(f32[8,128]{1,0:T(8,128)S(1)} %maximum_maximum_fusion.1), channel_id=1, source_target_pairs={{0,1},{1,2},{2,3},{3,4},{4,5},{5,6},{6,7},{7,0},{8,9},{9,10},{10,1... | collective-permute-start | bytes 12296 | tf_op jit(solution)/shard_map/ppermute | solution.py:52
  149.7 4.5 %collective-permute-start.27 = (f32[8,128]{1,0:T(8,128)S(1)}, f32[8,128]{1,0:T(8,128)S(1)}, u32[]{:S(2)}, u32[]{:S(2)}) collective-permute-start(f32[8,128]{1,0:T(8,128)S(1)} %maximum_maximum_fusion), channel_id=1, source_target_pairs={{0,4},{1,5},{2,6},{3,7},{4,0},{5,1},{6,2},{7,3},{8,12},{9,13},{10,... | collective-permute-start | bytes 12296 | tf_op jit(solution)/shard_map/ppermute | solution.py:52

commit v2 on v1

--- a/solution.py
+++ b/solution.py
@@ -1,5 +1,8 @@
+import functools
+
 import jax
 import jax.numpy as jnp
+import numpy as np
 from jax import lax
 from jax.experimental import pallas as pl
 from jax.experimental.pallas import tpu as pltpu
@@ -10,7 +13,8 @@
 PAIR_SCALE = 0.05
 STEPS = [(sx, sy) for sx in (-1, 0, 1) for sy in (-1, 0, 1)]
 DEPTH = 1
-CHUNK = 32
+SPLIT_ROWS = 32
+DEAD = -1.0e6
 SHIFTS = (1.0, 0.15, 0.55, 0.8, 0.3)
 SCALE = 0.3
 GRAM = [(i, j) for i in range(ITERS + 1) for j in range(i, ITERS + 1)]
@@ -48,7 +52,11 @@
             radix = next(k for k in (4, 2, 3, count // window) if (count // window) % k == 0)
             got = [part]
             for k in range(1, radix):
-                pairs = [(i, (i + k * window) % count) for i in range(count)]
+                group = radix * window
+                pairs = [
+                    (i, i // group * group + (i % group + k * window) % group)
+                    for i in range(count)
+                ]
                 got.append(lax.ppermute(part, axis, pairs))
             part = got[0]
             for other in got[1:]:
@@ -62,69 +70,104 @@
     return jnp.broadcast_to(row, (slots, slots)).T
 
 
-def folded(parts):
-    return jnp.sum(jnp.concatenate(parts, axis=0).T, axis=0, keepdims=True)
-
-
-def loop_cells(rows, cols, visit):
+def loop_cells(row_from, row_to, col_from, col_to, visit):
     def outer(r, carry):
         def inner(c, carry):
             visit(r, c)
             return carry
-        return lax.fori_loop(0, cols, inner, carry)
-    lax.fori_loop(0, rows, outer, 0)
-
-
-def setup_kernel(f_ref, dens_ref, w_ref, aux_ref, u_ref, full_ref):
+        return lax.fori_loop(col_from, col_to, inner, carry, unroll=min(2, col_to - col_from))
+    lax.fori_loop(row_from, row_to, outer, 0)
+
+
+def split_tables(slots):
+    pairs = ((0, 0), (0, 1), (1, 0), (1, 1), (0, 2), (2, 0))
+    left = [(0, 1.0), (1, 1.0), (2, 1.0), (3, 1.0), (3, 1.0), (3, 1.0)]
+    right = [(3, 1.0), (3, 1.0), (3, 1.0), (0, 1.0), (1, 1.0), (2, 1.0)]
+    for _ in range(2):
+        left += [(p, 2.0) for p, _ in pairs]
+        right += [(q, 1.0) for _, q in pairs]
+    table = np.zeros((8, SPLIT_ROWS, slots), np.float32)
+    for row, ((p, x), (q, y)) in enumerate(zip(left, right)):
+        table[p, row], table[4 + q, row] = x, y
+    return table
+
+
+def setup_kernel(f_ref, table_ref, dens_ref, w_ref, aux_ref, u_ref, full_ref, inv_ref, a_ref, b_ref):
     _, rows_all, cols_all, slots = f_ref.shape
     halo = DEPTH + 2
     rows, cols = rows_all - 2 * halo, cols_all - 2 * halo
+    span = cols + 2 * DEPTH
+    kind = lax.broadcasted_iota(jnp.int32, (SPLIT_ROWS, slots), 0)
 
     def field(k, r, c):
         return f_ref[k, r, pl.ds(c, 1), :]
 
-    def falloff(xc, yc, r, c, sx, sy):
-        dx = (sx + field(0, r + sx, c + sy)) - xc
-        dy = (sy + field(1, r + sx, c + sy)) - yc
-        return jnp.maximum(1.0 - (dx * dx + dy * dy), 0.0)
-
-    def density(r0, c0):
-        r, c = r0 + 1, c0 + 1
-        xc, yc = column(field(0, r, c)), column(field(1, r, c))
-        parts = []
-        for s in range(0, slots, CHUNK):
-            acc = jnp.zeros((CHUNK, slots), jnp.float32)
-            for sx, sy in STEPS:
-                f = falloff(xc[s:s + CHUNK], yc[s:s + CHUNK], r, c, sx, sy)
-                acc = acc + f * f * f * field(2, r + sx, c + sy)
-            parts.append(acc)
-        full_ref[r, pl.ds(c, 1), :] = 1.0 + folded(parts)
-
-    loop_cells(rows_all - 2, cols_all - 2, density)
-
-    def weights(r0, c0):
-        r, c = r0 + 2, c0 + 2
-        cell = r0 * (cols + 2 * DEPTH) + c0
-        xc, yc = column(field(0, r, c)), column(field(1, r, c))
-        dc = column(full_ref[r, pl.ds(c, 1), :])
-        parts = []
-        for s in range(0, slots, CHUNK):
-            acc = jnp.zeros((CHUNK, slots), jnp.float32)
-            for k, (sx, sy) in enumerate(STEPS):
-                f = falloff(xc[s:s + CHUNK], yc[s:s + CHUNK], r, c, sx, sy)
-                near = full_ref[r + sx, pl.ds(c + sy, 1), :]
-                weight = f * f * (2.0 * PAIR_SCALE) / (dc[s:s + CHUNK] + near)
-                w_ref[cell, k, s:s + CHUNK, :] = weight
-                live = jnp.where(field(2, r + sx, c + sy) > 0.0, 1.0, 0.0)
-                acc = acc + weight * live
-            parts.append(acc)
+    def factors(r, c):
+        x = field(0, r, c) + (jnp.float32(r) - 0.5 * rows_all)
+        y = field(1, r, c) + (jnp.float32(c) - 0.5 * cols_all)
+        own = 0.5 - (x * x + y * y)
+        near = jnp.where(field(2, r, c) > 0.0, own, DEAD)
+        x, y = (jnp.broadcast_to(v, kind.shape) for v in (x, y))
+
+        def parts(first, base):
+            value = jnp.where(kind < 6, first, jnp.where(kind < 12, x, y))
+            high = value.astype(jnp.bfloat16).astype(jnp.float32)
+            rest = value - high
+            middle = rest.astype(jnp.bfloat16).astype(jnp.float32)
+            low = rest - middle
+            total = (
+                high * table_ref[base] + middle * table_ref[base + 1]
+                + low * table_ref[base + 2] + table_ref[base + 3]
+            )
+            return total.astype(jnp.bfloat16)
+
+        a_ref[r * cols_all + c] = parts(own, 0)
+        b_ref[r * cols_all + c] = parts(near, 4)
+
+    loop_cells(0, rows_all, 0, cols_all, factors)
+
+    def density(keep, r, c):
+        acc = jnp.zeros((slots, slots), jnp.float32)
+        left = a_ref[r * cols_all + c]
+        cell = (r - 2) * span + (c - 2)
+        for k, (sx, sy) in enumerate(STEPS):
+            f = lax.dot_general(
+                left, b_ref[(r + sx) * cols_all + c + sy], (((0,), (0,)), ((), ())),
+                preferred_element_type=jnp.float32,
+            )
+            f = jnp.maximum(f, 0.0)
+            square = f * f
+            if keep:
+                w_ref[cell, k] = square
+            acc = acc + square * (f * field(2, r + sx, c + sy))
+        value = 1.0 + jnp.sum(acc.T, axis=0, keepdims=True)
+        full_ref[r, pl.ds(c, 1), :] = value
+        inv_ref[r, pl.ds(c, 1), :] = value * (1.0 / (2.0 * PAIR_SCALE))
+
+    kept, edge = functools.partial(density, True), functools.partial(density, False)
+    loop_cells(2, rows_all - 2, 2, cols_all - 2, kept)
+    for r in (1, rows_all - 2):
+        loop_cells(r, r + 1, 1, cols_all - 1, edge)
+    for c in (1, cols_all - 2):
+        loop_cells(2, rows_all - 2, c, c + 1, edge)
+
+    def weights(r, c):
+        r0, c0 = r - 2, c - 2
+        cell = r0 * span + c0
+        dc = column(inv_ref[r, pl.ds(c, 1), :])
+        acc = jnp.zeros((slots, slots), jnp.float32)
+        for k, (sx, sy) in enumerate(STEPS):
+            near = inv_ref[r + sx, pl.ds(c + sy, 1), :]
+            weight = w_ref[cell, k] * pl.reciprocal(dc + near)
+            w_ref[cell, k] = weight
+            acc = acc + weight
         occupied = jnp.where(field(2, r, c) > 0.0, 1.0, 0.0)
-        diagonal = BASE_STIFF + occupied * folded(parts)
+        diagonal = BASE_STIFF + occupied * jnp.sum(acc.T, axis=0, keepdims=True)
         aux_ref[0, r0, pl.ds(c0, 1), :] = diagonal
         aux_ref[1, r0, pl.ds(c0, 1), :] = occupied / diagonal
         u_ref[r0, pl.ds(c0, 1), :] = field(3, r, c) / diagonal
 
-    loop_cells(rows + 2 * DEPTH, cols + 2 * DEPTH, weights)
+    loop_cells(2, rows_all - 2, 2, cols_all - 2, weights)
     dens_ref[...] = full_ref[halo:halo + rows, halo:halo + cols, :]
 
 
@@ -144,7 +187,7 @@
             (1.0 - shift) * own - summed * aux_ref[1, r + skip, pl.ds(c + skip, 1), :]
         ) * (1.0 / SCALE)
 
-    loop_cells(rows, cols, visit)
+    loop_cells(0, rows, 0, cols, visit)
 
 
 def own_part(ref, rows, cols):
@@ -253,6 +296,7 @@
         [offsets, jnp.where(live, masses, 0.0)[None], jnp.where(live, source, 0.0)[None]]
     )
     padded = ghosted(fields, DEPTH + 2)
+    cells = padded.shape[1] * padded.shape[2]
     span_r, span_c = rows + 2 * DEPTH, cols + 2 * DEPTH
     own = jax.ShapeDtypeStruct((rows, cols, slots), f32)
     density, weight, aux, vector = pl.pallas_call(
@@ -263,10 +307,15 @@
             jax.ShapeDtypeStruct((2, span_r, span_c, slots), f32),
             jax.ShapeDtypeStruct((span_r, span_c, slots), f32),
         ),
-        scratch_shapes=[pltpu.VMEM(padded.shape[1:], f32)],
+        scratch_shapes=[
+            pltpu.VMEM(padded.shape[1:], f32),
+            pltpu.VMEM(padded.shape[1:], f32),
+            pltpu.VMEM((cells, SPLIT_ROWS, slots), jnp.bfloat16),
+            pltpu.VMEM((cells, SPLIT_ROWS, slots), jnp.bfloat16),
+        ],
         compiler_params=LIMIT,
         name="setup",
-    )(padded)
+    )(padded, jnp.asarray(split_tables(slots)))
     kept = weight
     basis = [vector]
     wide = vector

time: 156 us -> 132 us (0.85)
  Pallas kernels: 60.9 us -> 39.2 us
  waiting for transfers between devices: 44.8 us -> 42.3 us
    pallas_call x1, Pallas kernels: 44.3 us -> 27.9 us  [body(): pl.pallas_call(setup_kernel, out_shape=(own, WEIGHT_SPACE((span_r * span_...]
    pallas_call x3, Pallas kernels: 15.7 us -> 10.5 us  [body(): pl.pallas_call(lambda *refs, a=first, n=count, z=last: products_kernel(a,...]
    ppermute x14, waiting for transfers between devices: 23 us -> 20.6 us  [combined(): got.append(lax.ppermute(part, axis, pairs))]
  transfers between devices with their start and end apart: 28 -> 28, of which waited for: 20 -> 19; matrix products, arithmetic and copies ran while one was open for 0% -> 1% of each run, Pallas kernels for 0% -> 0%
where the time goes in v2:
time: 132 us
  starting transfers between devices  45.1 us (34%)
  waiting for transfers between devices  42.3 us (32%)
  Pallas kernels  39.2 us (30%)
  other arithmetic  2.36 us (2%)
  local copies, waits for them, and re-layouts  1.59 us (1%)
    pallas_call x1, Pallas kernels, body(): pl.pallas_call(setup_kernel, out_shape=(own, WEIGHT_SPACE((span_r * span_...  27.9 us
    ppermute x7, starting transfers between devices, extended(): lows.insert(0, lax.ppermute(tail, axis, up))  23.4 us
    ppermute x14, waiting for transfers between devices, combined(): got.append(lax.ppermute(part, axis, pairs))  20.6 us
    ppermute x7, waiting for transfers between devices, extended(): highs.append(lax.ppermute(head, axis, down))  20.3 us
    ppermute x14, starting transfers between devices, combined(): got.append(lax.ppermute(part, axis, pairs))  12.7 us
    pallas_call x3, Pallas kernels, body(): pl.pallas_call(lambda *refs, a=first, n=count, z=last: products_kernel(a,...  10.5 us
    ppermute x7, starting transfers between devices, extended(): highs.append(lax.ppermute(head, axis, down))  9.04 us
  transfers between devices with their start and end apart: 28, of which 19 were waited for; matrix products, arithmetic and copies ran while one was open for 1% of the time, Pallas kernels for 0%

profile of v2, /device:TPU:0, one launch (start us, length us, event | category | flops | bytes accessed | tf_op | source)
XLA Modules:
  0.0 131.5 jit_solution(9757426896494632819)
XLA Ops:
  2.2 4.9 %collective-permute-start = (f32[4,1,8,128]{3,2,1,0:T(8,128)S(1)}, f32[4,1,8,128]{3,2,1,0:T(8,128)S(1)}, u32[]{:S(2)}, u32[]{:S(2)}) collective-permute-start(f32[4,1,8,128]{3,2,1,0:T(8,128)S(1)} %get-tuple-element.31), channel_id=1, source_target_pairs={{0,16},{8,24},{1,17},{9,25},{2,18},{10,26},{3,19},{11,27},{4,20},{... | collective-permute-start | bytes 49160 | tf_op jit(solution)/shard_map/ppermute | solution.py:36
  7.1 1.3 collective-permute-start.2
  8.4 3.0 %collective-permute-start.1 = (f32[4,2,8,128]{3,2,1,0:T(8,128)S(1)}, f32[4,2,8,128]{3,2,1,0:T(8,128)S(1)}, u32[]{:S(2)}, u32[]{:S(2)}) collective-permute-start(f32[4,2,8,128]{3,2,1,0:T(8,128)S(1)} %pad_maximum_fusion.3), channel_id=1, source_target_pairs={{0,8},{8,16},{16,24},{1,9},{9,17},{17,25},{2,10},{10,18},{18,26},{... | collective-permute-start | bytes 98312 | tf_op jit(solution)/shard_map/ppermute | solution.py:36
  11.4 1.3 collective-permute-start.3
  13.5 3.6 %collective-permute-done.3 = f32[4,1,8,128]{3,2,1,0:T(8,128)S(1)} collective-permute-done((f32[4,1,8,128]{3,2,1,0:T(8,128)S(1)}, f32[4,1,8,128]{3,2,1,0:T(8,128)S(1)}, u32[]{:S(2)}, u32[]{:S(2)}) %collective-permute-start.3) | collective-permute-done | bytes 16416 | tf_op jit(solution)/shard_map/ppermute | solution.py:37
  17.1 3.4 %collective-permute-start.4 = (f32[4,8,3,128]{3,2,1,0:T(4,128)S(1)}, f32[4,8,3,128]{3,2,1,0:T(4,128)S(1)}, u32[]{:S(2)}, u32[]{:S(2)}) collective-permute-start(f32[4,8,3,128]{3,2,1,0:T(4,128)S(1)} %get-tuple-element.28), channel_id=1, source_target_pairs={{0,1},{1,2},{2,3},{3,4},{4,5},{5,6},{6,7},{8,9},{9,10},{10,11},{11... | collective-permute-start | bytes 147464 | tf_op jit(solution)/shard_map/ppermute | solution.py:36
  20.5 1.3 collective-permute-start.5
  22.3 4.3 %collective-permute-done.5 = f32[4,8,3,128]{3,2,1,0:T(4,128)S(1)} collective-permute-done((f32[4,8,3,128]{3,2,1,0:T(4,128)S(1)}, f32[4,8,3,128]{3,2,1,0:T(4,128)S(1)}, u32[]{:S(2)}, u32[]{:S(2)}) %collective-permute-start.5) | collective-permute-done | bytes 49184 | tf_op jit(solution)/shard_map/ppermute | solution.py:37
  27.6 27.9 %setup.1 = (f32[2,8,128]{2,1,0:T(8,128)}, f32[40,9,128,128]{3,2,1,0:T(8,128)S(1)}, f32[2,4,10,128]{3,2,1,0:T(8,128)S(1)}, f32[4,10,128]{2,1,0:T(8,128)S(1)}) custom-call(f32[4,8,14,128]{3,2,1,0:T(8,128)S(1)} %pad_maximum_fusion.f_ref, f32[8,32,128]{2,1,0:T(8,128)S(1)} %copy-done), custom_call_target="tpu_custom_call" | custom-call | tf_op jit(solution)/shard_map/setup/pallas_call | solution.py:302
  55.4 1.3 products_0.1.refs_4_.refs_1_
  56.7 1.3 collective-permute-start.7
  58.0 3.0 %collective-permute-start.6 = (f32[2,8,128]{2,1,0:T(8,128)S(1)}, f32[2,8,128]{2,1,0:T(8,128)S(1)}, u32[]{:S(2)}, u32[]{:S(2)}) collective-permute-start(f32[2,8,128]{2,1,0:T(8,128)S(1)} %products_0.1.refs_4_.refs_1_), channel_id=1, source_target_pairs={{0,8},{8,16},{16,24},{1,9},{9,17},{17,25},{2,10},{10,18},{18,26},{... | collective-permute-start | bytes 24584 | tf_op jit(solution)/shard_map/ppermute | solution.py:36
  61.9 4.3 %collective-permute-start.8 = (f32[6,2,128]{2,1,0:T(2,128)S(1)}, f32[6,2,128]{2,1,0:T(2,128)S(1)}, u32[]{:S(2)}, u32[]{:S(2)}) collective-permute-start(f32[6,2,128]{2,1,0:T(2,128)S(1)} %get-tuple-element.34), channel_id=1, source_target_pairs={{0,1},{1,2},{2,3},{3,4},{4,5},{5,6},{6,7},{8,9},{9,10},{10,11},{11... | collective-permute-start | bytes 18440 | tf_op jit(solution)/shard_map/ppermute | solution.py:36
  66.3 1.3 collective-permute-start.9
  67.6 4.2 %collective-permute-done.9 = f32[6,2,128]{2,1,0:T(2,128)S(1)} collective-permute-done((f32[6,2,128]{2,1,0:T(2,128)S(1)}, f32[6,2,128]{2,1,0:T(2,128)S(1)}, u32[]{:S(2)}, u32[]{:S(2)}) %collective-permute-start.9) | collective-permute-done | bytes 6176 | tf_op jit(solution)/shard_map/ppermute | solution.py:37
  71.8 4.6 %products_1.1 = (f32[2,8,128]{2,1,0:T(8,128)S(1)}, f32[2,8,128]{2,1,0:T(8,128)S(1)}) custom-call(f32[40,9,128,128]{3,2,1,0:T(8,128)S(1)} %get-tuple-element.17.refs_0_, f32[2,4,10,128]{3,2,1,0:T(8,128)S(1)} %get-tuple-element.18.refs_1_.aux_ref, f32[6,12,128]{2,1,0:T(8,128)S(1)} %pad_maximum_fusion.1.refs_2_), custom_call_target="tpu_custom_call" | custom-call | tf_op jit(solution)/shard_map/products_1/pallas_call | solution.py:336
  79.0 4.1 %collective-permute-done.11 = f32[2,8,128]{2,1,0:T(8,128)S(1)} collective-permute-done((f32[2,8,128]{2,1,0:T(8,128)S(1)}, f32[2,8,128]{2,1,0:T(8,128)S(1)}, u32[]{:S(2)}, u32[]{:S(2)}) %collective-permute-start.11) | collective-permute-done | bytes 8224 | tf_op jit(solution)/shard_map/ppermute | solution.py:37
  83.1 3.4 %collective-permute-start.12 = (f32[6,2,128]{2,1,0:T(2,128)S(1)}, f32[6,2,128]{2,1,0:T(2,128)S(1)}, u32[]{:S(2)}, u32[]{:S(2)}) collective-permute-start(f32[6,2,128]{2,1,0:T(2,128)S(1)} %get-tuple-element.32), channel_id=1, source_target_pairs={{0,1},{1,2},{2,3},{3,4},{4,5},{5,6},{6,7},{8,9},{9,10},{10,11},{11... | collective-permute-start | bytes 18440 | tf_op jit(solution)/shard_map/ppermute | solution.py:36
  87.9 4.2 %collective-permute-done.13 = f32[6,2,128]{2,1,0:T(2,128)S(1)} collective-permute-done((f32[6,2,128]{2,1,0:T(2,128)S(1)}, f32[6,2,128]{2,1,0:T(2,128)S(1)}, u32[]{:S(2)}, u32[]{:S(2)}) %collective-permute-start.13) | collective-permute-done | bytes 6176 | tf_op jit(solution)/shard_map/ppermute | solution.py:37
  92.1 4.6 %products_3.1 = (f32[2,8,128]{2,1,0:T(8,128)S(1)}, f32[2,8,128]{2,1,0:T(8,128)S(1)}, f32[24,128]{1,0:T(8,128)S(1)}) custom-call(f32[40,9,128,128]{3,2,1,0:T(8,128)S(1)} %get-tuple-element.17.refs_0_, f32[2,4,10,128]{3,2,1,0:T(8,128)S(1)} %get-tuple-element.18.refs_1_.aux_ref, f32[6,12,128]{2,1,0:T(8,128)S(1)} %pad_maximum_fusion.2.refs_2_, ...), custom_call_target="tpu_custom_call" | custom-call | tf_op jit(solution)/shard_map/products_3/pallas_call | solution.py:336
  96.7 2.6 %collective-permute-start.15 = (f32[24,128]{1,0:T(8,128)S(1)}, f32[24,128]{1,0:T(8,128)S(1)}, u32[]{:S(2)}, u32[]{:S(2)}) collective-permute-start(f32[24,128]{1,0:T(8,128)S(1)} %get-tuple-element.22), channel_id=1, source_target_pairs={{0,16},{8,24},{16,0},{24,8},{1,17},{9,25},{17,1},{25,9},{2,18},{10... | collective-permute-start | bytes 36872 | tf_op jit(solution)/shard_map/ppermute | solution.py:60
  99.3 1.8 %collective-permute-done.15 = f32[24,128]{1,0:T(8,128)S(1)} collective-permute-done((f32[24,128]{1,0:T(8,128)S(1)}, f32[24,128]{1,0:T(8,128)S(1)}, u32[]{:S(2)}, u32[]{:S(2)}) %collective-permute-start.15) | collective-permute-done | bytes 12320 | tf_op jit(solution)/shard_map/ppermute | solution.py:60
  101.1 1.3 %collective-permute-done.14 = f32[24,128]{1,0:T(8,128)S(1)} collective-permute-done((f32[24,128]{1,0:T(8,128)S(1)}, f32[24,128]{1,0:T(8,128)S(1)}, u32[]{:S(2)}, u32[]{:S(2)}) %collective-permute-start.14) | collective-permute-done | bytes 12320 | tf_op jit(solution)/shard_map/ppermute | solution.py:60
  102.5 3.5 %collective-permute-start.19 = (f32[24,128]{1,0:T(8,128)S(1)}, f32[24,128]{1,0:T(8,128)S(1)}, u32[]{:S(2)}, u32[]{:S(2)}) collective-permute-start(f32[24,128]{1,0:T(8,128)S(1)} %add_add_fusion.1), channel_id=1, source_target_pairs={{0,3},{1,0},{2,1},{3,2},{4,7},{5,4},{6,5},{7,6},{8,11},{9,8},{10,9... | collective-permute-start | bytes 36872 | tf_op jit(solution)/shard_map/ppermute | solution.py:60
  107.3 2.3 %collective-permute-done.18 = f32[24,128]{1,0:T(8,128)S(1)} collective-permute-done((f32[24,128]{1,0:T(8,128)S(1)}, f32[24,128]{1,0:T(8,128)S(1)}, u32[]{:S(2)}, u32[]{:S(2)}) %collective-permute-start.18) | collective-permute-done | bytes 12320 | tf_op jit(solution)/shard_map/ppermute | solution.py:60
  109.6 1.4 %collective-permute-done.17 = f32[24,128]{1,0:T(8,128)S(1)} collective-permute-done((f32[24,128]{1,0:T(8,128)S(1)}, f32[24,128]{1,0:T(8,128)S(1)}, u32[]{:S(2)}, u32[]{:S(2)}) %collective-permute-start.17) | collective-permute-done | bytes 12320 | tf_op jit(solution)/shard_map/ppermute | solution.py:60
  112.3 3.3 %collective-permute-done.20 = f32[24,128]{1,0:T(8,128)S(1)} collective-permute-done((f32[24,128]{1,0:T(8,128)S(1)}, f32[24,128]{1,0:T(8,128)S(1)}, u32[]{:S(2)}, u32[]{:S(2)}) %collective-permute-start.20) | collective-permute-done | bytes 12320 | tf_op jit(solution)/shard_map/ppermute | solution.py:60
  117.9 2.3 %collective-permute-done.22 = f32[8,128]{1,0:T(8,128)S(1)} collective-permute-done((f32[8,128]{1,0:T(8,128)S(1)}, f32[8,128]{1,0:T(8,128)S(1)}, u32[]{:S(2)}, u32[]{:S(2)}) %collective-permute-start.22) | collective-permute-done | bytes 4128 | tf_op jit(solution)/shard_map/ppermute | solution.py:60
  120.3 1.5 %collective-permute-start.25 = (f32[8,128]{1,0:T(8,128)S(1)}, f32[8,128]{1,0:T(8,128)S(1)}, u32[]{:S(2)}, u32[]{:S(2)}) collective-permute-start(f32[8,128]{1,0:T(8,128)S(1)} %maximum_maximum_fusion.1), channel_id=1, source_target_pairs={{0,2},{1,3},{2,0},{3,1},{4,6},{5,7},{6,4},{7,5},{8,10},{9,11},{10,... | collective-permute-start | bytes 12296 | tf_op jit(solution)/shard_map/ppermute | solution.py:60
  121.8 1.9 %collective-permute-start.24 = (f32[8,128]{1,0:T(8,128)S(1)}, f32[8,128]{1,0:T(8,128)S(1)}, u32[]{:S(2)}, u32[]{:S(2)}) collective-permute-start(f32[8,128]{1,0:T(8,128)S(1)} %maximum_maximum_fusion.1), channel_id=1, source_target_pairs={{0,1},{1,2},{2,3},{3,0},{4,5},{5,6},{6,7},{7,4},{8,9},{9,10},{10,1... | collective-permute-start | bytes 12296 | tf_op jit(solution)/shard_map/ppermute | solution.py:60
  124.0 2.4 %collective-permute-done.24 = f32[8,128]{1,0:T(8,128)S(1)} collective-permute-done((f32[8,128]{1,0:T(8,128)S(1)}, f32[8,128]{1,0:T(8,128)S(1)}, u32[]{:S(2)}, u32[]{:S(2)}) %collective-permute-start.24) | collective-permute-done | bytes 4128 | tf_op jit(solution)/shard_map/ppermute | solution.py:60
  126.6 4.2 %collective-permute-done.27 = f32[8,128]{1,0:T(8,128)S(1)} collective-permute-done((f32[8,128]{1,0:T(8,128)S(1)}, f32[8,128]{1,0:T(8,128)S(1)}, u32[]{:S(2)}, u32[]{:S(2)}) %collective-permute-start.27) | collective-permute-done | bytes 4128 | tf_op jit(solution)/shard_map/ppermute | solution.py:60
  (55 shorter events, 14.8 us)
Async XLA Ops:
  2.2 10.5 %collective-permute-start = (f32[4,1,8,128]{3,2,1,0:T(8,128)S(1)}, f32[4,1,8,128]{3,2,1,0:T(8,128)S(1)}, u32[]{:S(2)}, u32[]{:S(2)}) collective-permute-start(f32[4,1,8,128]{3,2,1,0:T(8,128)S(1)} %get-tuple-element.31), channel_id=1, source_target_pairs={{0,16},{8,24},{1,17},{9,25},{2,18},{10,26},{3,19},{11,27},{4,20},{... | collective-permute-start | bytes 49160 | tf_op jit(solution)/shard_map/ppermute | solution.py:36
  7.1 6.4 %collective-permute-start.2 = (f32[4,2,8,128]{3,2,1,0:T(8,128)S(1)}, f32[4,2,8,128]{3,2,1,0:T(8,128)S(1)}, u32[]{:S(2)}, u32[]{:S(2)}) collective-permute-start(f32[4,2,8,128]{3,2,1,0:T(8,128)S(1)} %pad_maximum_fusion.3), channel_id=1, source_target_pairs={{8,0},{16,8},{24,16},{9,1},{17,9},{25,17},{10,2},{18,10},{26,18},{... | collective-permute-start | bytes 98312 | tf_op jit(solution)/shard_map/ppermute | solution.py:37
  8.4 4.4 %collective-permute-start.1 = (f32[4,2,8,128]{3,2,1,0:T(8,128)S(1)}, f32[4,2,8,128]{3,2,1,0:T(8,128)S(1)}, u32[]{:S(2)}, u32[]{:S(2)}) collective-permute-start(f32[4,2,8,128]{3,2,1,0:T(8,128)S(1)} %pad_maximum_fusion.3), channel_id=1, source_target_pairs={{0,8},{8,16},{16,24},{1,9},{9,17},{17,25},{2,10},{10,18},{18,26},{... | collective-permute-start | bytes 98312 | tf_op jit(solution)/shard_map/ppermute | solution.py:36
  11.4 5.6 %collective-permute-start.3 = (f32[4,1,8,128]{3,2,1,0:T(8,128)S(1)}, f32[4,1,8,128]{3,2,1,0:T(8,128)S(1)}, u32[]{:S(2)}, u32[]{:S(2)}) collective-permute-start(f32[4,1,8,128]{3,2,1,0:T(8,128)S(1)} %get-tuple-element.30), channel_id=1, source_target_pairs={{16,0},{24,8},{17,1},{25,9},{18,2},{26,10},{19,3},{27,11},{20,4},{... | collective-permute-start | bytes 49160 | tf_op jit(solution)/shard_map/ppermute | solution.py:37
  17.1 5.3 %collective-permute-start.4 = (f32[4,8,3,128]{3,2,1,0:T(4,128)S(1)}, f32[4,8,3,128]{3,2,1,0:T(4,128)S(1)}, u32[]{:S(2)}, u32[]{:S(2)}) collective-permute-start(f32[4,8,3,128]{3,2,1,0:T(4,128)S(1)} %get-tuple-element.28), channel_id=1, source_target_pairs={{0,1},{1,2},{2,3},{3,4},{4,5},{5,6},{6,7},{8,9},{9,10},{10,11},{11... | collective-permute-start | bytes 147464 | tf_op jit(solution)/shard_map/ppermute | solution.py:36
  20.5 6.2 %collective-permute-start.5 = (f32[4,8,3,128]{3,2,1,0:T(4,128)S(1)}, f32[4,8,3,128]{3,2,1,0:T(4,128)S(1)}, u32[]{:S(2)}, u32[]{:S(2)}) collective-permute-start(f32[4,8,3,128]{3,2,1,0:T(4,128)S(1)} %get-tuple-element.29), channel_id=1, source_target_pairs={{1,0},{2,1},{3,2},{4,3},{5,4},{6,5},{7,6},{9,8},{10,9},{11,10},{12... | collective-permute-start | bytes 147464 | tf_op jit(solution)/shard_map/ppermute | solution.py:37
  26.7 0.9 copy-start
  56.7 4.3 %collective-permute-start.7 = (f32[2,8,128]{2,1,0:T(8,128)S(1)}, f32[2,8,128]{2,1,0:T(8,128)S(1)}, u32[]{:S(2)}, u32[]{:S(2)}) collective-permute-start(f32[2,8,128]{2,1,0:T(8,128)S(1)} %products_0.1.refs_4_.refs_1_), channel_id=1, source_target_pairs={{8,0},{16,8},{24,16},{9,1},{17,9},{25,17},{10,2},{18,10},{26,18},{... | collective-permute-start | bytes 24584 | tf_op jit(solution)/shard_map/ppermute | solution.py:37
  58.0 3.8 %collective-permute-start.6 = (f32[2,8,128]{2,1,0:T(8,128)S(1)}, f32[2,8,128]{2,1,0:T(8,128)S(1)}, u32[]{:S(2)}, u32[]{:S(2)}) collective-permute-start(f32[2,8,128]{2,1,0:T(8,128)S(1)} %products_0.1.refs_4_.refs_1_), channel_id=1, source_target_pairs={{0,8},{8,16},{16,24},{1,9},{9,17},{17,25},{2,10},{10,18},{18,26},{... | collective-permute-start | bytes 24584 | tf_op jit(solution)/shard_map/ppermute | solution.py:36
  61.9 5.7 %collective-permute-start.8 = (f32[6,2,128]{2,1,0:T(2,128)S(1)}, f32[6,2,128]{2,1,0:T(2,128)S(1)}, u32[]{:S(2)}, u32[]{:S(2)}) collective-permute-start(f32[6,2,128]{2,1,0:T(2,128)S(1)} %get-tuple-element.34), channel_id=1, source_target_pairs={{0,1},{1,2},{2,3},{3,4},{4,5},{5,6},{6,7},{8,9},{9,10},{10,11},{11... | collective-permute-start | bytes 18440 | tf_op jit(solution)/shard_map/ppermute | solution.py:36
  66.3 5.5 %collective-permute-start.9 = (f32[6,2,128]{2,1,0:T(2,128)S(1)}, f32[6,2,128]{2,1,0:T(2,128)S(1)}, u32[]{:S(2)}, u32[]{:S(2)}) collective-permute-start(f32[6,2,128]{2,1,0:T(2,128)S(1)} %get-tuple-element.35), channel_id=1, source_target_pairs={{1,0},{2,1},{3,2},{4,3},{5,4},{6,5},{7,6},{9,8},{10,9},{11,10},{12... | collective-permute-start | bytes 18440 | tf_op jit(solution)/shard_map/ppermute | solution.py:37
  76.4 2.6 %collective-permute-start.10 = (f32[2,8,128]{2,1,0:T(8,128)S(1)}, f32[2,8,128]{2,1,0:T(8,128)S(1)}, u32[]{:S(2)}, u32[]{:S(2)}) collective-permute-start(f32[2,8,128]{2,1,0:T(8,128)S(1)} %get-tuple-element.20.refs_6_.refs_3_), channel_id=1, source_target_pairs={{0,8},{8,16},{16,24},{1,9},{9,17},{17,25},{2,10},{10,18},{18,26},{... | collective-permute-start | bytes 24584 | tf_op jit(solution)/shard_map/ppermute | solution.py:36
  77.7 5.4 %collective-permute-start.11 = (f32[2,8,128]{2,1,0:T(8,128)S(1)}, f32[2,8,128]{2,1,0:T(8,128)S(1)}, u32[]{:S(2)}, u32[]{:S(2)}) collective-permute-start(f32[2,8,128]{2,1,0:T(8,128)S(1)} %get-tuple-element.20.refs_6_.refs_3_), channel_id=1, source_target_pairs={{8,0},{16,8},{24,16},{9,1},{17,9},{25,17},{10,2},{18,10},{26,18},{... | collective-permute-start | bytes 24584 | tf_op jit(solution)/shard_map/ppermute | solution.py:37
  83.1 4.7 %collective-permute-start.12 = (f32[6,2,128]{2,1,0:T(2,128)S(1)}, f32[6,2,128]{2,1,0:T(2,128)S(1)}, u32[]{:S(2)}, u32[]{:S(2)}) collective-permute-start(f32[6,2,128]{2,1,0:T(2,128)S(1)} %get-tuple-element.32), channel_id=1, source_target_pairs={{0,1},{1,2},{2,3},{3,4},{4,5},{5,6},{6,7},{8,9},{9,10},{10,11},{11... | collective-permute-start | bytes 18440 | tf_op jit(solution)/shard_map/ppermute | solution.py:36
  86.5 5.5 %collective-permute-start.13 = (f32[6,2,128]{2,1,0:T(2,128)S(1)}, f32[6,2,128]{2,1,0:T(2,128)S(1)}, u32[]{:S(2)}, u32[]{:S(2)}) collective-permute-start(f32[6,2,128]{2,1,0:T(2,128)S(1)} %get-tuple-element.33), channel_id=1, source_target_pairs={{1,0},{2,1},{3,2},{4,3},{5,4},{6,5},{7,6},{9,8},{10,9},{11,10},{12... | collective-permute-start | bytes 18440 | tf_op jit(solution)/shard_map/ppermute | solution.py:37
  96.7 2.7 %collective-permute-start.16 = (f32[24,128]{1,0:T(8,128)S(1)}, f32[24,128]{1,0:T(8,128)S(1)}, u32[]{:S(2)}, u32[]{:S(2)}) collective-permute-start(f32[24,128]{1,0:T(8,128)S(1)} %get-tuple-element.22), channel_id=1, source_target_pairs={{0,24},{8,0},{16,8},{24,16},{1,25},{9,1},{17,9},{25,17},{2,26},{10... | collective-permute-start | bytes 36872 | tf_op jit(solution)/shard_map/ppermute | solution.py:60
  96.7 4.4 %collective-permute-start.15 = (f32[24,128]{1,0:T(8,128)S(1)}, f32[24,128]{1,0:T(8,128)S(1)}, u32[]{:S(2)}, u32[]{:S(2)}) collective-permute-start(f32[24,128]{1,0:T(8,128)S(1)} %get-tuple-element.22), channel_id=1, source_target_pairs={{0,16},{8,24},{16,0},{24,8},{1,17},{9,25},{17,1},{25,9},{2,18},{10... | collective-permute-start | bytes 36872 | tf_op jit(solution)/shard_map/ppermute | solution.py:60
  99.3 3.1 %collective-permute-start.14 = (f32[24,128]{1,0:T(8,128)S(1)}, f32[24,128]{1,0:T(8,128)S(1)}, u32[]{:S(2)}, u32[]{:S(2)}) collective-permute-start(f32[24,128]{1,0:T(8,128)S(1)} %get-tuple-element.22), channel_id=1, source_target_pairs={{0,8},{8,16},{16,24},{24,0},{1,9},{9,17},{17,25},{25,1},{2,10},{10... | collective-permute-start | bytes 36872 | tf_op jit(solution)/shard_map/ppermute | solution.py:60
  102.5 4.9 %collective-permute-start.19 = (f32[24,128]{1,0:T(8,128)S(1)}, f32[24,128]{1,0:T(8,128)S(1)}, u32[]{:S(2)}, u32[]{:S(2)}) collective-permute-start(f32[24,128]{1,0:T(8,128)S(1)} %add_add_fusion.1), channel_id=1, source_target_pairs={{0,3},{1,0},{2,1},{3,2},{4,7},{5,4},{6,5},{7,6},{8,11},{9,8},{10,9... | collective-permute-start | bytes 36872 | tf_op jit(solution)/shard_map/ppermute | solution.py:60
  105.9 3.7 %collective-permute-start.18 = (f32[24,128]{1,0:T(8,128)S(1)}, f32[24,128]{1,0:T(8,128)S(1)}, u32[]{:S(2)}, u32[]{:S(2)}) collective-permute-start(f32[24,128]{1,0:T(8,128)S(1)} %add_add_fusion.1), channel_id=1, source_target_pairs={{0,2},{1,3},{2,0},{3,1},{4,6},{5,7},{6,4},{7,5},{8,10},{9,11},{10,... | collective-permute-start | bytes 36872 | tf_op jit(solution)/shard_map/ppermute | solution.py:60
  106.4 4.7 %collective-permute-start.17 = (f32[24,128]{1,0:T(8,128)S(1)}, f32[24,128]{1,0:T(8,128)S(1)}, u32[]{:S(2)}, u32[]{:S(2)}) collective-permute-start(f32[24,128]{1,0:T(8,128)S(1)} %add_add_fusion.1), channel_id=1, source_target_pairs={{0,1},{1,2},{2,3},{3,0},{4,5},{5,6},{6,7},{7,4},{8,9},{9,10},{10,1... | collective-permute-start | bytes 36872 | tf_op jit(solution)/shard_map/ppermute | solution.py:60
  111.0 4.6 %collective-permute-start.20 = (f32[24,128]{1,0:T(8,128)S(1)}, f32[24,128]{1,0:T(8,128)S(1)}, u32[]{:S(2)}, u32[]{:S(2)}) collective-permute-start(f32[24,128]{1,0:T(8,128)S(1)} %add_add_fusion), channel_id=1, source_target_pairs={{0,4},{1,5},{2,6},{3,7},{4,0},{5,1},{6,2},{7,3},{8,12},{9,13},{10,... | collective-permute-start | bytes 36872 | tf_op jit(solution)/shard_map/ppermute | solution.py:60
  116.6 1.3 %collective-permute-start.23 = (f32[8,128]{1,0:T(8,128)S(1)}, f32[8,128]{1,0:T(8,128)S(1)}, u32[]{:S(2)}, u32[]{:S(2)}) collective-permute-start(f32[8,128]{1,0:T(8,128)S(1)} %get-tuple-element.27), channel_id=1, source_target_pairs={{0,24},{8,0},{16,8},{24,16},{1,25},{9,1},{17,9},{25,17},{2,26},{10... | collective-permute-start | bytes 12296 | tf_op jit(solution)/shard_map/ppermute | solution.py:60
  116.6 3.6 %collective-permute-start.22 = (f32[8,128]{1,0:T(8,128)S(1)}, f32[8,128]{1,0:T(8,128)S(1)}, u32[]{:S(2)}, u32[]{:S(2)}) collective-permute-start(f32[8,128]{1,0:T(8,128)S(1)} %get-tuple-element.27), channel_id=1, source_target_pairs={{0,16},{8,24},{16,0},{24,8},{1,17},{9,25},{17,1},{25,9},{2,18},{10... | collective-permute-start | bytes 12296 | tf_op jit(solution)/shard_map/ppermute | solution.py:60
  117.1 3.1 %collective-permute-start.21 = (f32[8,128]{1,0:T(8,128)S(1)}, f32[8,128]{1,0:T(8,128)S(1)}, u32[]{:S(2)}, u32[]{:S(2)}) collective-permute-start(f32[8,128]{1,0:T(8,128)S(1)} %get-tuple-element.27), channel_id=1, source_target_pairs={{0,8},{8,16},{16,24},{24,0},{1,9},{9,17},{17,25},{25,1},{2,10},{10... | collective-permute-start | bytes 12296 | tf_op jit(solution)/shard_map/ppermute | solution.py:60
  120.2 3.7 %collective-permute-start.26 = (f32[8,128]{1,0:T(8,128)S(1)}, f32[8,128]{1,0:T(8,128)S(1)}, u32[]{:S(2)}, u32[]{:S(2)}) collective-permute-start(f32[8,128]{1,0:T(8,128)S(1)} %maximum_maximum_fusion.1), channel_id=1, source_target_pairs={{0,3},{1,0},{2,1},{3,2},{4,7},{5,4},{6,5},{7,6},{8,11},{9,8},{10,9... | collective-permute-start | bytes 12296 | tf_op jit(solution)/shard_map/ppermute | solution.py:60
  120.3 3.7 %collective-permute-start.25 = (f32[8,128]{1,0:T(8,128)S(1)}, f32[8,128]{1,0:T(8,128)S(1)}, u32[]{:S(2)}, u32[]{:S(2)}) collective-permute-start(f32[8,128]{1,0:T(8,128)S(1)} %maximum_maximum_fusion.1), channel_id=1, source_target_pairs={{0,2},{1,3},{2,0},{3,1},{4,6},{5,7},{6,4},{7,5},{8,10},{9,11},{10,... | collective-permute-start | bytes 12296 | tf_op jit(solution)/shard_map/ppermute | solution.py:60
  121.8 4.5 %collective-permute-start.24 = (f32[8,128]{1,0:T(8,128)S(1)}, f32[8,128]{1,0:T(8,128)S(1)}, u32[]{:S(2)}, u32[]{:S(2)}) collective-permute-start(f32[8,128]{1,0:T(8,128)S(1)} %maximum_maximum_fusion.1), channel_id=1, source_target_pairs={{0,1},{1,2},{2,3},{3,0},{4,5},{5,6},{6,7},{7,4},{8,9},{9,10},{10,1... | collective-permute-start | bytes 12296 | tf_op jit(solution)/shard_map/ppermute | solution.py:60
  126.3 4.5 %collective-permute-start.27 = (f32[8,128]{1,0:T(8,128)S(1)}, f32[8,128]{1,0:T(8,128)S(1)}, u32[]{:S(2)}, u32[]{:S(2)}) collective-permute-start(f32[8,128]{1,0:T(8,128)S(1)} %maximum_maximum_fusion), channel_id=1, source_target_pairs={{0,4},{1,5},{2,6},{3,7},{4,0},{5,1},{6,2},{7,3},{8,12},{9,13},{10,... | collective-permute-start | bytes 12296 | tf_op jit(solution)/shard_map/ppermute | solution.py:60

commit v3 on v2

--- a/solution.py
+++ b/solution.py
@@ -2,7 +2,6 @@
 
 import jax
 import jax.numpy as jnp
-import numpy as np
 from jax import lax
 from jax.experimental import pallas as pl
 from jax.experimental.pallas import tpu as pltpu
@@ -49,7 +48,7 @@
         count = lax.axis_size(axis)
         window = 1
         while window < count:
-            radix = next(k for k in (4, 2, 3, count // window) if (count // window) % k == 0)
+            radix = next(k for k in (8, 4, 2, 3, count // window) if (count // window) % k == 0)
             got = [part]
             for k in range(1, radix):
                 group = radix * window
@@ -70,34 +69,41 @@
     return jnp.broadcast_to(row, (slots, slots)).T
 
 
-def loop_cells(row_from, row_to, col_from, col_to, visit):
+def loop_cells(row_from, row_to, col_from, col_to, visit, most=2):
+    count = col_to - col_from
+    unroll = max(k for k in range(1, most + 1) if count % k == 0)
+
     def outer(r, carry):
         def inner(c, carry):
             visit(r, c)
             return carry
-        return lax.fori_loop(col_from, col_to, inner, carry, unroll=min(2, col_to - col_from))
+        return lax.fori_loop(col_from, col_to, inner, carry, unroll=unroll)
     lax.fori_loop(row_from, row_to, outer, 0)
 
 
-def split_tables(slots):
+def write_tables(table_ref, kind):
     pairs = ((0, 0), (0, 1), (1, 0), (1, 1), (0, 2), (2, 0))
     left = [(0, 1.0), (1, 1.0), (2, 1.0), (3, 1.0), (3, 1.0), (3, 1.0)]
     right = [(3, 1.0), (3, 1.0), (3, 1.0), (0, 1.0), (1, 1.0), (2, 1.0)]
     for _ in range(2):
         left += [(p, 2.0) for p, _ in pairs]
         right += [(q, 1.0) for _, q in pairs]
-    table = np.zeros((8, SPLIT_ROWS, slots), np.float32)
-    for row, ((p, x), (q, y)) in enumerate(zip(left, right)):
-        table[p, row], table[4 + q, row] = x, y
-    return table
-
-
-def setup_kernel(f_ref, table_ref, dens_ref, w_ref, aux_ref, u_ref, full_ref, inv_ref, a_ref, b_ref):
+    for base, side in ((0, left), (4, right)):
+        for part in range(4):
+            value = jnp.zeros(kind.shape, jnp.float32)
+            for row, (p, scale) in enumerate(side):
+                if p == part:
+                    value = jnp.where(kind == row, scale, value)
+            table_ref[base + part] = value
+
+
+def setup_kernel(f_ref, dens_ref, w_ref, aux_ref, u_ref, full_ref, inv_ref, a_ref, b_ref, table_ref):
     _, rows_all, cols_all, slots = f_ref.shape
     halo = DEPTH + 2
     rows, cols = rows_all - 2 * halo, cols_all - 2 * halo
     span = cols + 2 * DEPTH
     kind = lax.broadcasted_iota(jnp.int32, (SPLIT_ROWS, slots), 0)
+    write_tables(table_ref, kind)
 
     def field(k, r, c):
         return f_ref[k, r, pl.ds(c, 1), :]
@@ -124,7 +130,7 @@
         a_ref[r * cols_all + c] = parts(own, 0)
         b_ref[r * cols_all + c] = parts(near, 4)
 
-    loop_cells(0, rows_all, 0, cols_all, factors)
+    loop_cells(0, rows_all, 0, cols_all, factors, 8)
 
     def density(keep, r, c):
         acc = jnp.zeros((slots, slots), jnp.float32)
@@ -187,7 +193,7 @@
             (1.0 - shift) * own - summed * aux_ref[1, r + skip, pl.ds(c + skip, 1), :]
         ) * (1.0 / SCALE)
 
-    loop_cells(0, rows, 0, cols, visit)
+    loop_cells(0, rows, 0, cols, visit, 5)
 
 
 def own_part(ref, rows, cols):
@@ -312,10 +318,11 @@
             pltpu.VMEM(padded.shape[1:], f32),
             pltpu.VMEM((cells, SPLIT_ROWS, slots), jnp.bfloat16),
             pltpu.VMEM((cells, SPLIT_ROWS, slots), jnp.bfloat16),
+            pltpu.VMEM((8, SPLIT_ROWS, slots), f32),
         ],
         compiler_params=LIMIT,
         name="setup",
-    )(padded, jnp.asarray(split_tables(slots)))
+    )(padded)
     kept = weight
     basis = [vector]
     wide = vector

time: 132 us -> 134 us (1.015)
  starting transfers between devices: 45.1 us -> 54.6 us
  Pallas kernels: 39.2 us -> 35.8 us
  waiting for transfers between devices: 42.3 us -> 38.9 us
    ppermute x14 -> x20, starting transfers between devices: 12.7 us -> 22.2 us  [combined(): got.append(lax.ppermute(part, axis, pairs))]
    ppermute x14 -> x20, waiting for transfers between devices: 20.6 us -> 17.1 us  [combined(): got.append(lax.ppermute(part, axis, pairs))]
    pallas_call x3, Pallas kernels: 10.5 us -> 7.36 us  [body(): pl.pallas_call(lambda *refs, a=first, n=count, z=last: products_kernel(a,...]
  transfers between devices with their start and end apart: 28 -> 34, of which waited for: 19 -> 18; matrix products, arithmetic and copies ran while one was open for 1% -> 1% of each run, Pallas kernels for 0% -> 0%
where the time goes in v3:
time: 134 us; the launch traced here: 133 us
  starting transfers between devices  54.6 us (41%)
  waiting for transfers between devices  38.9 us (29%)
  Pallas kernels  35.8 us (27%)
  other arithmetic  2.36 us (2%)
    pallas_call x1, Pallas kernels, body(): pl.pallas_call(setup_kernel, out_shape=(own, WEIGHT_SPACE((span_r * span_...  27.5 us
    ppermute x7, starting transfers between devices, extended(): lows.insert(0, lax.ppermute(tail, axis, up))  23.4 us
    ppermute x20, starting transfers between devices, combined(): got.append(lax.ppermute(part, axis, pairs))  22.2 us
    ppermute x7, waiting for transfers between devices, extended(): highs.append(lax.ppermute(head, axis, down))  20.3 us
    ppermute x20, waiting for transfers between devices, combined(): got.append(lax.ppermute(part, axis, pairs))  17.1 us
    ppermute x7, starting transfers between devices, extended(): highs.append(lax.ppermute(head, axis, down))  9.04 us
    pallas_call x3, Pallas kernels, body(): pl.pallas_call(lambda *refs, a=first, n=count, z=last: products_kernel(a,...  7.36 us
  transfers between devices with their start and end apart: 34, of which 18 were waited for; matrix products, arithmetic and copies ran while one was open for 1% of the time, Pallas kernels for 0%

profile of v3, /device:TPU:0, one launch (start us, length us, event | category | flops | bytes accessed | tf_op | source)
XLA Modules:
  0.0 133.3 jit_solution(2924105298714462048)
XLA Ops:
  2.2 4.9 %collective-permute-start = (f32[4,1,8,128]{3,2,1,0:T(8,128)S(1)}, f32[4,1,8,128]{3,2,1,0:T(8,128)S(1)}, u32[]{:S(2)}, u32[]{:S(2)}) collective-permute-start(f32[4,1,8,128]{3,2,1,0:T(8,128)S(1)} %get-tuple-element.31), channel_id=1, source_target_pairs={{0,16},{8,24},{1,17},{9,25},{2,18},{10,26},{3,19},{11,27},{4,20},{... | collective-permute-start | bytes 49160 | tf_op jit(solution)/shard_map/ppermute | solution.py:35
  8.4 3.0 %collective-permute-start.1 = (f32[4,2,8,128]{3,2,1,0:T(8,128)S(1)}, f32[4,2,8,128]{3,2,1,0:T(8,128)S(1)}, u32[]{:S(2)}, u32[]{:S(2)}) collective-permute-start(f32[4,2,8,128]{3,2,1,0:T(8,128)S(1)} %pad_maximum_fusion.3), channel_id=1, source_target_pairs={{0,8},{8,16},{16,24},{1,9},{9,17},{17,25},{2,10},{10,18},{18,26},{... | collective-permute-start | bytes 98312 | tf_op jit(solution)/shard_map/ppermute | solution.py:35
  13.5 3.6 %collective-permute-done.3 = f32[4,1,8,128]{3,2,1,0:T(8,128)S(1)} collective-permute-done((f32[4,1,8,128]{3,2,1,0:T(8,128)S(1)}, f32[4,1,8,128]{3,2,1,0:T(8,128)S(1)}, u32[]{:S(2)}, u32[]{:S(2)}) %collective-permute-start.3) | collective-permute-done | bytes 16416 | tf_op jit(solution)/shard_map/ppermute | solution.py:36
  17.1 3.4 %collective-permute-start.4 = (f32[4,8,3,128]{3,2,1,0:T(4,128)S(1)}, f32[4,8,3,128]{3,2,1,0:T(4,128)S(1)}, u32[]{:S(2)}, u32[]{:S(2)}) collective-permute-start(f32[4,8,3,128]{3,2,1,0:T(4,128)S(1)} %get-tuple-element.28), channel_id=1, source_target_pairs={{0,1},{1,2},{2,3},{3,4},{4,5},{5,6},{6,7},{8,9},{9,10},{10,11},{11... | collective-permute-start | bytes 147464 | tf_op jit(solution)/shard_map/ppermute | solution.py:35
  20.5 1.3 collective-permute-start.5
  22.3 4.3 %collective-permute-done.5 = f32[4,8,3,128]{3,2,1,0:T(4,128)S(1)} collective-permute-done((f32[4,8,3,128]{3,2,1,0:T(4,128)S(1)}, f32[4,8,3,128]{3,2,1,0:T(4,128)S(1)}, u32[]{:S(2)}, u32[]{:S(2)}) %collective-permute-start.5) | collective-permute-done | bytes 49184 | tf_op jit(solution)/shard_map/ppermute | solution.py:36
  26.7 27.5 %setup.1 = (f32[2,8,128]{2,1,0:T(8,128)}, f32[40,9,128,128]{3,2,1,0:T(8,128)S(1)}, f32[2,4,10,128]{3,2,1,0:T(8,128)S(1)}, f32[4,10,128]{2,1,0:T(8,128)S(1)}) custom-call(f32[4,8,14,128]{3,2,1,0:T(8,128)S(1)} %pad_maximum_fusion.f_ref), custom_call_target="tpu_custom_call" | custom-call | tf_op jit(solution)/shard_map/setup/pallas_call | solution.py:308
  56.4 3.0 %collective-permute-start.6 = (f32[2,8,128]{2,1,0:T(8,128)S(1)}, f32[2,8,128]{2,1,0:T(8,128)S(1)}, u32[]{:S(2)}, u32[]{:S(2)}) collective-permute-start(f32[2,8,128]{2,1,0:T(8,128)S(1)} %products_0.1.refs_4_.refs_1_), channel_id=1, source_target_pairs={{0,8},{8,16},{16,24},{1,9},{9,17},{17,25},{2,10},{10,18},{18,26},{... | collective-permute-start | bytes 24584 | tf_op jit(solution)/shard_map/ppermute | solution.py:35
  60.3 4.3 %collective-permute-start.8 = (f32[6,2,128]{2,1,0:T(2,128)S(1)}, f32[6,2,128]{2,1,0:T(2,128)S(1)}, u32[]{:S(2)}, u32[]{:S(2)}) collective-permute-start(f32[6,2,128]{2,1,0:T(2,128)S(1)} %get-tuple-element.34), channel_id=1, source_target_pairs={{0,1},{1,2},{2,3},{3,4},{4,5},{5,6},{6,7},{8,9},{9,10},{10,11},{11... | collective-permute-start | bytes 18440 | tf_op jit(solution)/shard_map/ppermute | solution.py:35
  66.0 4.2 %collective-permute-done.9 = f32[6,2,128]{2,1,0:T(2,128)S(1)} collective-permute-done((f32[6,2,128]{2,1,0:T(2,128)S(1)}, f32[6,2,128]{2,1,0:T(2,128)S(1)}, u32[]{:S(2)}, u32[]{:S(2)}) %collective-permute-start.9) | collective-permute-done | bytes 6176 | tf_op jit(solution)/shard_map/ppermute | solution.py:36
  70.2 3.2 %products_1.1 = (f32[2,8,128]{2,1,0:T(8,128)S(1)}, f32[2,8,128]{2,1,0:T(8,128)S(1)}) custom-call(f32[40,9,128,128]{3,2,1,0:T(8,128)S(1)} %get-tuple-element.17.refs_0_, f32[2,4,10,128]{3,2,1,0:T(8,128)S(1)} %get-tuple-element.18.refs_1_.aux_ref, f32[6,12,128]{2,1,0:T(8,128)S(1)} %pad_maximum_fusion.1.refs_2_), custom_call_target="tpu_custom_call" | custom-call | tf_op jit(solution)/shard_map/products_1/pallas_call | solution.py:343
  74.7 1.3 collective-permute-start.11
  76.0 4.1 %collective-permute-done.11 = f32[2,8,128]{2,1,0:T(8,128)S(1)} collective-permute-done((f32[2,8,128]{2,1,0:T(8,128)S(1)}, f32[2,8,128]{2,1,0:T(8,128)S(1)}, u32[]{:S(2)}, u32[]{:S(2)}) %collective-permute-start.11) | collective-permute-done | bytes 8224 | tf_op jit(solution)/shard_map/ppermute | solution.py:36
  80.1 3.4 %collective-permute-start.12 = (f32[6,2,128]{2,1,0:T(2,128)S(1)}, f32[6,2,128]{2,1,0:T(2,128)S(1)}, u32[]{:S(2)}, u32[]{:S(2)}) collective-permute-start(f32[6,2,128]{2,1,0:T(2,128)S(1)} %get-tuple-element.32), channel_id=1, source_target_pairs={{0,1},{1,2},{2,3},{3,4},{4,5},{5,6},{6,7},{8,9},{9,10},{10,11},{11... | collective-permute-start | bytes 18440 | tf_op jit(solution)/shard_map/ppermute | solution.py:35
  84.9 4.2 %collective-permute-done.13 = f32[6,2,128]{2,1,0:T(2,128)S(1)} collective-permute-done((f32[6,2,128]{2,1,0:T(2,128)S(1)}, f32[6,2,128]{2,1,0:T(2,128)S(1)}, u32[]{:S(2)}, u32[]{:S(2)}) %collective-permute-start.13) | collective-permute-done | bytes 6176 | tf_op jit(solution)/shard_map/ppermute | solution.py:36
  89.1 3.2 %products_3.1 = (f32[2,8,128]{2,1,0:T(8,128)S(1)}, f32[2,8,128]{2,1,0:T(8,128)S(1)}, f32[24,128]{1,0:T(8,128)S(1)}) custom-call(f32[40,9,128,128]{3,2,1,0:T(8,128)S(1)} %get-tuple-element.17.refs_0_, f32[2,4,10,128]{3,2,1,0:T(8,128)S(1)} %get-tuple-element.18.refs_1_.aux_ref, f32[6,12,128]{2,1,0:T(8,128)S(1)} %pad_maximum_fusion.2.refs_2_, ...), custom_call_target="tpu_custom_call" | custom-call | tf_op jit(solution)/shard_map/products_3/pallas_call | solution.py:343
  92.4 2.6 %collective-permute-start.15 = (f32[24,128]{1,0:T(8,128)S(1)}, f32[24,128]{1,0:T(8,128)S(1)}, u32[]{:S(2)}, u32[]{:S(2)}) collective-permute-start(f32[24,128]{1,0:T(8,128)S(1)} %get-tuple-element.22), channel_id=1, source_target_pairs={{0,16},{8,24},{16,0},{24,8},{1,17},{9,25},{17,1},{25,9},{2,18},{10... | collective-permute-start | bytes 36872 | tf_op jit(solution)/shard_map/ppermute | solution.py:59
  95.0 1.8 %collective-permute-done.15 = f32[24,128]{1,0:T(8,128)S(1)} collective-permute-done((f32[24,128]{1,0:T(8,128)S(1)}, f32[24,128]{1,0:T(8,128)S(1)}, u32[]{:S(2)}, u32[]{:S(2)}) %collective-permute-start.15) | collective-permute-done | bytes 12320 | tf_op jit(solution)/shard_map/ppermute | solution.py:59
  96.8 1.3 collective-permute-done.14
  98.2 4.6 %collective-permute-start.22 = (f32[24,128]{1,0:T(8,128)S(1)}, f32[24,128]{1,0:T(8,128)S(1)}, u32[]{:S(2)}, u32[]{:S(2)}) collective-permute-start(f32[24,128]{1,0:T(8,128)S(1)} %add_add_fusion.1), channel_id=1, source_target_pairs={{0,6},{1,7},{2,0},{3,1},{4,2},{5,3},{6,4},{7,5},{8,14},{9,15},{10,... | collective-permute-start | bytes 36872 | tf_op jit(solution)/shard_map/ppermute | solution.py:59
  104.3 2.1 %collective-permute-start.19 = (f32[24,128]{1,0:T(8,128)S(1)}, f32[24,128]{1,0:T(8,128)S(1)}, u32[]{:S(2)}, u32[]{:S(2)}) collective-permute-start(f32[24,128]{1,0:T(8,128)S(1)} %add_add_fusion.1), channel_id=1, source_target_pairs={{0,3},{1,4},{2,5},{3,6},{4,7},{5,0},{6,1},{7,2},{8,11},{9,12},{10,... | collective-permute-start | bytes 36872 | tf_op jit(solution)/shard_map/ppermute | solution.py:59
  106.4 2.5 %collective-permute-start.18 = (f32[24,128]{1,0:T(8,128)S(1)}, f32[24,128]{1,0:T(8,128)S(1)}, u32[]{:S(2)}, u32[]{:S(2)}) collective-permute-start(f32[24,128]{1,0:T(8,128)S(1)} %add_add_fusion.1), channel_id=1, source_target_pairs={{0,2},{1,3},{2,4},{3,5},{4,6},{5,7},{6,0},{7,1},{8,10},{9,11},{10,... | collective-permute-start | bytes 36872 | tf_op jit(solution)/shard_map/ppermute | solution.py:59
  108.9 1.3 %collective-permute-done.19 = f32[24,128]{1,0:T(8,128)S(1)} collective-permute-done((f32[24,128]{1,0:T(8,128)S(1)}, f32[24,128]{1,0:T(8,128)S(1)}, u32[]{:S(2)}, u32[]{:S(2)}) %collective-permute-start.19) | collective-permute-done | bytes 12320 | tf_op jit(solution)/shard_map/ppermute | solution.py:59
  110.2 1.6 %collective-permute-done.18 = f32[24,128]{1,0:T(8,128)S(1)} collective-permute-done((f32[24,128]{1,0:T(8,128)S(1)}, f32[24,128]{1,0:T(8,128)S(1)}, u32[]{:S(2)}, u32[]{:S(2)}) %collective-permute-start.18) | collective-permute-done | bytes 12320 | tf_op jit(solution)/shard_map/ppermute | solution.py:59
  111.9 3.4 %collective-permute-done.17 = f32[24,128]{1,0:T(8,128)S(1)} collective-permute-done((f32[24,128]{1,0:T(8,128)S(1)}, f32[24,128]{1,0:T(8,128)S(1)}, u32[]{:S(2)}, u32[]{:S(2)}) %collective-permute-start.17) | collective-permute-done | bytes 12320 | tf_op jit(solution)/shard_map/ppermute | solution.py:59
  117.5 2.3 %collective-permute-done.25 = f32[8,128]{1,0:T(8,128)S(1)} collective-permute-done((f32[8,128]{1,0:T(8,128)S(1)}, f32[8,128]{1,0:T(8,128)S(1)}, u32[]{:S(2)}, u32[]{:S(2)}) %collective-permute-start.25) | collective-permute-done | bytes 4128 | tf_op jit(solution)/shard_map/ppermute | solution.py:59
  120.0 1.4 %collective-permute-start.31 = (f32[8,128]{1,0:T(8,128)S(1)}, f32[8,128]{1,0:T(8,128)S(1)}, u32[]{:S(2)}, u32[]{:S(2)}) collective-permute-start(f32[8,128]{1,0:T(8,128)S(1)} %maximum_maximum_fusion.1), channel_id=1, source_target_pairs={{0,5},{1,6},{2,7},{3,0},{4,1},{5,2},{6,3},{7,4},{8,13},{9,14},{10,... | collective-permute-start | bytes 12296 | tf_op jit(solution)/shard_map/ppermute | solution.py:59
  121.3 3.0 %collective-permute-start.30 = (f32[8,128]{1,0:T(8,128)S(1)}, f32[8,128]{1,0:T(8,128)S(1)}, u32[]{:S(2)}, u32[]{:S(2)}) collective-permute-start(f32[8,128]{1,0:T(8,128)S(1)} %maximum_maximum_fusion.1), channel_id=1, source_target_pairs={{0,4},{1,5},{2,6},{3,7},{4,0},{5,1},{6,2},{7,3},{8,12},{9,13},{10,... | collective-permute-start | bytes 12296 | tf_op jit(solution)/shard_map/ppermute | solution.py:59
  124.3 2.0 %collective-permute-start.28 = (f32[8,128]{1,0:T(8,128)S(1)}, f32[8,128]{1,0:T(8,128)S(1)}, u32[]{:S(2)}, u32[]{:S(2)}) collective-permute-start(f32[8,128]{1,0:T(8,128)S(1)} %maximum_maximum_fusion.1), channel_id=1, source_target_pairs={{0,2},{1,3},{2,4},{3,5},{4,6},{5,7},{6,0},{7,1},{8,10},{9,11},{10,... | collective-permute-start | bytes 12296 | tf_op jit(solution)/shard_map/ppermute | solution.py:59
  126.3 1.5 %collective-permute-start.27 = (f32[8,128]{1,0:T(8,128)S(1)}, f32[8,128]{1,0:T(8,128)S(1)}, u32[]{:S(2)}, u32[]{:S(2)}) collective-permute-start(f32[8,128]{1,0:T(8,128)S(1)} %maximum_maximum_fusion.1), channel_id=1, source_target_pairs={{0,1},{1,2},{2,3},{3,4},{4,5},{5,6},{6,7},{7,0},{8,9},{9,10},{10,1... | collective-permute-start | bytes 12296 | tf_op jit(solution)/shard_map/ppermute | solution.py:59
  127.8 1.9 %collective-permute-done.29 = f32[8,128]{1,0:T(8,128)S(1)} collective-permute-done((f32[8,128]{1,0:T(8,128)S(1)}, f32[8,128]{1,0:T(8,128)S(1)}, u32[]{:S(2)}, u32[]{:S(2)}) %collective-permute-start.29) | collective-permute-done | bytes 4128 | tf_op jit(solution)/shard_map/ppermute | solution.py:59
  129.8 2.8 %collective-permute-done.27 = f32[8,128]{1,0:T(8,128)S(1)} collective-permute-done((f32[8,128]{1,0:T(8,128)S(1)}, f32[8,128]{1,0:T(8,128)S(1)}, u32[]{:S(2)}, u32[]{:S(2)}) %collective-permute-start.27) | collective-permute-done | bytes 4128 | tf_op jit(solution)/shard_map/ppermute | solution.py:59
  (63 shorter events, 17.3 us)
Async XLA Ops:
  2.2 10.5 %collective-permute-start = (f32[4,1,8,128]{3,2,1,0:T(8,128)S(1)}, f32[4,1,8,128]{3,2,1,0:T(8,128)S(1)}, u32[]{:S(2)}, u32[]{:S(2)}) collective-permute-start(f32[4,1,8,128]{3,2,1,0:T(8,128)S(1)} %get-tuple-element.31), channel_id=1, source_target_pairs={{0,16},{8,24},{1,17},{9,25},{2,18},{10,26},{3,19},{11,27},{4,20},{... | collective-permute-start | bytes 49160 | tf_op jit(solution)/shard_map/ppermute | solution.py:35
  7.1 6.4 %collective-permute-start.2 = (f32[4,2,8,128]{3,2,1,0:T(8,128)S(1)}, f32[4,2,8,128]{3,2,1,0:T(8,128)S(1)}, u32[]{:S(2)}, u32[]{:S(2)}) collective-permute-start(f32[4,2,8,128]{3,2,1,0:T(8,128)S(1)} %pad_maximum_fusion.3), channel_id=1, source_target_pairs={{8,0},{16,8},{24,16},{9,1},{17,9},{25,17},{10,2},{18,10},{26,18},{... | collective-permute-start | bytes 98312 | tf_op jit(solution)/shard_map/ppermute | solution.py:36
  8.4 4.4 %collective-permute-start.1 = (f32[4,2,8,128]{3,2,1,0:T(8,128)S(1)}, f32[4,2,8,128]{3,2,1,0:T(8,128)S(1)}, u32[]{:S(2)}, u32[]{:S(2)}) collective-permute-start(f32[4,2,8,128]{3,2,1,0:T(8,128)S(1)} %pad_maximum_fusion.3), channel_id=1, source_target_pairs={{0,8},{8,16},{16,24},{1,9},{9,17},{17,25},{2,10},{10,18},{18,26},{... | collective-permute-start | bytes 98312 | tf_op jit(solution)/shard_map/ppermute | solution.py:35
  11.4 5.6 %collective-permute-start.3 = (f32[4,1,8,128]{3,2,1,0:T(8,128)S(1)}, f32[4,1,8,128]{3,2,1,0:T(8,128)S(1)}, u32[]{:S(2)}, u32[]{:S(2)}) collective-permute-start(f32[4,1,8,128]{3,2,1,0:T(8,128)S(1)} %get-tuple-element.30), channel_id=1, source_target_pairs={{16,0},{24,8},{17,1},{25,9},{18,2},{26,10},{19,3},{27,11},{20,4},{... | collective-permute-start | bytes 49160 | tf_op jit(solution)/shard_map/ppermute | solution.py:36
  17.1 5.3 %collective-permute-start.4 = (f32[4,8,3,128]{3,2,1,0:T(4,128)S(1)}, f32[4,8,3,128]{3,2,1,0:T(4,128)S(1)}, u32[]{:S(2)}, u32[]{:S(2)}) collective-permute-start(f32[4,8,3,128]{3,2,1,0:T(4,128)S(1)} %get-tuple-element.28), channel_id=1, source_target_pairs={{0,1},{1,2},{2,3},{3,4},{4,5},{5,6},{6,7},{8,9},{9,10},{10,11},{11... | collective-permute-start | bytes 147464 | tf_op jit(solution)/shard_map/ppermute | solution.py:35
  20.5 6.2 %collective-permute-start.5 = (f32[4,8,3,128]{3,2,1,0:T(4,128)S(1)}, f32[4,8,3,128]{3,2,1,0:T(4,128)S(1)}, u32[]{:S(2)}, u32[]{:S(2)}) collective-permute-start(f32[4,8,3,128]{3,2,1,0:T(4,128)S(1)} %get-tuple-element.29), channel_id=1, source_target_pairs={{1,0},{2,1},{3,2},{4,3},{5,4},{6,5},{7,6},{9,8},{10,9},{11,10},{12... | collective-permute-start | bytes 147464 | tf_op jit(solution)/shard_map/ppermute | solution.py:36
  55.1 4.3 %collective-permute-start.7 = (f32[2,8,128]{2,1,0:T(8,128)S(1)}, f32[2,8,128]{2,1,0:T(8,128)S(1)}, u32[]{:S(2)}, u32[]{:S(2)}) collective-permute-start(f32[2,8,128]{2,1,0:T(8,128)S(1)} %products_0.1.refs_4_.refs_1_), channel_id=1, source_target_pairs={{8,0},{16,8},{24,16},{9,1},{17,9},{25,17},{10,2},{18,10},{26,18},{... | collective-permute-start | bytes 24584 | tf_op jit(solution)/shard_map/ppermute | solution.py:36
  56.4 3.8 %collective-permute-start.6 = (f32[2,8,128]{2,1,0:T(8,128)S(1)}, f32[2,8,128]{2,1,0:T(8,128)S(1)}, u32[]{:S(2)}, u32[]{:S(2)}) collective-permute-start(f32[2,8,128]{2,1,0:T(8,128)S(1)} %products_0.1.refs_4_.refs_1_), channel_id=1, source_target_pairs={{0,8},{8,16},{16,24},{1,9},{9,17},{17,25},{2,10},{10,18},{18,26},{... | collective-permute-start | bytes 24584 | tf_op jit(solution)/shard_map/ppermute | solution.py:35
  60.3 5.7 %collective-permute-start.8 = (f32[6,2,128]{2,1,0:T(2,128)S(1)}, f32[6,2,128]{2,1,0:T(2,128)S(1)}, u32[]{:S(2)}, u32[]{:S(2)}) collective-permute-start(f32[6,2,128]{2,1,0:T(2,128)S(1)} %get-tuple-element.34), channel_id=1, source_target_pairs={{0,1},{1,2},{2,3},{3,4},{4,5},{5,6},{6,7},{8,9},{9,10},{10,11},{11... | collective-permute-start | bytes 18440 | tf_op jit(solution)/shard_map/ppermute | solution.py:35
  64.6 5.5 %collective-permute-start.9 = (f32[6,2,128]{2,1,0:T(2,128)S(1)}, f32[6,2,128]{2,1,0:T(2,128)S(1)}, u32[]{:S(2)}, u32[]{:S(2)}) collective-permute-start(f32[6,2,128]{2,1,0:T(2,128)S(1)} %get-tuple-element.35), channel_id=1, source_target_pairs={{1,0},{2,1},{3,2},{4,3},{5,4},{6,5},{7,6},{9,8},{10,9},{11,10},{12... | collective-permute-start | bytes 18440 | tf_op jit(solution)/shard_map/ppermute | solution.py:36
  74.7 5.4 %collective-permute-start.11 = (f32[2,8,128]{2,1,0:T(8,128)S(1)}, f32[2,8,128]{2,1,0:T(8,128)S(1)}, u32[]{:S(2)}, u32[]{:S(2)}) collective-permute-start(f32[2,8,128]{2,1,0:T(8,128)S(1)} %get-tuple-element.20.refs_6_.refs_3_), channel_id=1, source_target_pairs={{8,0},{16,8},{24,16},{9,1},{17,9},{25,17},{10,2},{18,10},{26,18},{... | collective-permute-start | bytes 24584 | tf_op jit(solution)/shard_map/ppermute | solution.py:36
  80.1 4.7 %collective-permute-start.12 = (f32[6,2,128]{2,1,0:T(2,128)S(1)}, f32[6,2,128]{2,1,0:T(2,128)S(1)}, u32[]{:S(2)}, u32[]{:S(2)}) collective-permute-start(f32[6,2,128]{2,1,0:T(2,128)S(1)} %get-tuple-element.32), channel_id=1, source_target_pairs={{0,1},{1,2},{2,3},{3,4},{4,5},{5,6},{6,7},{8,9},{9,10},{10,11},{11... | collective-permute-start | bytes 18440 | tf_op jit(solution)/shard_map/ppermute | solution.py:35
  83.5 5.5 %collective-permute-start.13 = (f32[6,2,128]{2,1,0:T(2,128)S(1)}, f32[6,2,128]{2,1,0:T(2,128)S(1)}, u32[]{:S(2)}, u32[]{:S(2)}) collective-permute-start(f32[6,2,128]{2,1,0:T(2,128)S(1)} %get-tuple-element.33), channel_id=1, source_target_pairs={{1,0},{2,1},{3,2},{4,3},{5,4},{6,5},{7,6},{9,8},{10,9},{11,10},{12... | collective-permute-start | bytes 18440 | tf_op jit(solution)/shard_map/ppermute | solution.py:36
  92.3 2.7 %collective-permute-start.16 = (f32[24,128]{1,0:T(8,128)S(1)}, f32[24,128]{1,0:T(8,128)S(1)}, u32[]{:S(2)}, u32[]{:S(2)}) collective-permute-start(f32[24,128]{1,0:T(8,128)S(1)} %get-tuple-element.22), channel_id=1, source_target_pairs={{0,24},{8,0},{16,8},{24,16},{1,25},{9,1},{17,9},{25,17},{2,26},{10... | collective-permute-start | bytes 36872 | tf_op jit(solution)/shard_map/ppermute | solution.py:59
  92.4 4.4 %collective-permute-start.15 = (f32[24,128]{1,0:T(8,128)S(1)}, f32[24,128]{1,0:T(8,128)S(1)}, u32[]{:S(2)}, u32[]{:S(2)}) collective-permute-start(f32[24,128]{1,0:T(8,128)S(1)} %get-tuple-element.22), channel_id=1, source_target_pairs={{0,16},{8,24},{16,0},{24,8},{1,17},{9,25},{17,1},{25,9},{2,18},{10... | collective-permute-start | bytes 36872 | tf_op jit(solution)/shard_map/ppermute | solution.py:59
  95.0 3.1 %collective-permute-start.14 = (f32[24,128]{1,0:T(8,128)S(1)}, f32[24,128]{1,0:T(8,128)S(1)}, u32[]{:S(2)}, u32[]{:S(2)}) collective-permute-start(f32[24,128]{1,0:T(8,128)S(1)} %get-tuple-element.22), channel_id=1, source_target_pairs={{0,8},{8,16},{16,24},{24,0},{1,9},{9,17},{17,25},{25,1},{2,10},{10... | collective-permute-start | bytes 36872 | tf_op jit(solution)/shard_map/ppermute | solution.py:59
  98.1 8.3 %collective-permute-start.23 = (f32[24,128]{1,0:T(8,128)S(1)}, f32[24,128]{1,0:T(8,128)S(1)}, u32[]{:S(2)}, u32[]{:S(2)}) collective-permute-start(f32[24,128]{1,0:T(8,128)S(1)} %add_add_fusion.1), channel_id=1, source_target_pairs={{0,7},{1,0},{2,1},{3,2},{4,3},{5,4},{6,5},{7,6},{8,15},{9,8},{10,9... | collective-permute-start | bytes 36872 | tf_op jit(solution)/shard_map/ppermute | solution.py:59
  98.2 10.7 %collective-permute-start.22 = (f32[24,128]{1,0:T(8,128)S(1)}, f32[24,128]{1,0:T(8,128)S(1)}, u32[]{:S(2)}, u32[]{:S(2)}) collective-permute-start(f32[24,128]{1,0:T(8,128)S(1)} %add_add_fusion.1), channel_id=1, source_target_pairs={{0,6},{1,7},{2,0},{3,1},{4,2},{5,3},{6,4},{7,5},{8,14},{9,15},{10,... | collective-permute-start | bytes 36872 | tf_op jit(solution)/shard_map/ppermute | solution.py:59
  102.8 6.1 %collective-permute-start.21 = (f32[24,128]{1,0:T(8,128)S(1)}, f32[24,128]{1,0:T(8,128)S(1)}, u32[]{:S(2)}, u32[]{:S(2)}) collective-permute-start(f32[24,128]{1,0:T(8,128)S(1)} %add_add_fusion.1), channel_id=1, source_target_pairs={{0,5},{1,6},{2,7},{3,0},{4,1},{5,2},{6,3},{7,4},{8,13},{9,14},{10,... | collective-permute-start | bytes 36872 | tf_op jit(solution)/shard_map/ppermute | solution.py:59
  103.1 5.8 %collective-permute-start.20 = (f32[24,128]{1,0:T(8,128)S(1)}, f32[24,128]{1,0:T(8,128)S(1)}, u32[]{:S(2)}, u32[]{:S(2)}) collective-permute-start(f32[24,128]{1,0:T(8,128)S(1)} %add_add_fusion.1), channel_id=1, source_target_pairs={{0,4},{1,5},{2,6},{3,7},{4,0},{5,1},{6,2},{7,3},{8,12},{9,13},{10,... | collective-permute-start | bytes 36872 | tf_op jit(solution)/shard_map/ppermute | solution.py:59
  104.3 6.0 %collective-permute-start.19 = (f32[24,128]{1,0:T(8,128)S(1)}, f32[24,128]{1,0:T(8,128)S(1)}, u32[]{:S(2)}, u32[]{:S(2)}) collective-permute-start(f32[24,128]{1,0:T(8,128)S(1)} %add_add_fusion.1), channel_id=1, source_target_pairs={{0,3},{1,4},{2,5},{3,6},{4,7},{5,0},{6,1},{7,2},{8,11},{9,12},{10,... | collective-permute-start | bytes 36872 | tf_op jit(solution)/shard_map/ppermute | solution.py:59
  106.4 5.5 %collective-permute-start.18 = (f32[24,128]{1,0:T(8,128)S(1)}, f32[24,128]{1,0:T(8,128)S(1)}, u32[]{:S(2)}, u32[]{:S(2)}) collective-permute-start(f32[24,128]{1,0:T(8,128)S(1)} %add_add_fusion.1), channel_id=1, source_target_pairs={{0,2},{1,3},{2,4},{3,5},{4,6},{5,7},{6,0},{7,1},{8,10},{9,11},{10,... | collective-permute-start | bytes 36872 | tf_op jit(solution)/shard_map/ppermute | solution.py:59
  108.9 6.4 %collective-permute-start.17 = (f32[24,128]{1,0:T(8,128)S(1)}, f32[24,128]{1,0:T(8,128)S(1)}, u32[]{:S(2)}, u32[]{:S(2)}) collective-permute-start(f32[24,128]{1,0:T(8,128)S(1)} %add_add_fusion.1), channel_id=1, source_target_pairs={{0,1},{1,2},{2,3},{3,4},{4,5},{5,6},{6,7},{7,0},{8,9},{9,10},{10,1... | collective-permute-start | bytes 36872 | tf_op jit(solution)/shard_map/ppermute | solution.py:59
  116.2 3.6 %collective-permute-start.25 = (f32[8,128]{1,0:T(8,128)S(1)}, f32[8,128]{1,0:T(8,128)S(1)}, u32[]{:S(2)}, u32[]{:S(2)}) collective-permute-start(f32[8,128]{1,0:T(8,128)S(1)} %get-tuple-element.27), channel_id=1, source_target_pairs={{0,16},{8,24},{16,0},{24,8},{1,17},{9,25},{17,1},{25,9},{2,18},{10... | collective-permute-start | bytes 12296 | tf_op jit(solution)/shard_map/ppermute | solution.py:59
  116.8 3.0 %collective-permute-start.24 = (f32[8,128]{1,0:T(8,128)S(1)}, f32[8,128]{1,0:T(8,128)S(1)}, u32[]{:S(2)}, u32[]{:S(2)}) collective-permute-start(f32[8,128]{1,0:T(8,128)S(1)} %get-tuple-element.27), channel_id=1, source_target_pairs={{0,8},{8,16},{16,24},{24,0},{1,9},{9,17},{17,25},{25,1},{2,10},{10... | collective-permute-start | bytes 12296 | tf_op jit(solution)/shard_map/ppermute | solution.py:59
  119.9 4.4 %collective-permute-start.33 = (f32[8,128]{1,0:T(8,128)S(1)}, f32[8,128]{1,0:T(8,128)S(1)}, u32[]{:S(2)}, u32[]{:S(2)}) collective-permute-start(f32[8,128]{1,0:T(8,128)S(1)} %maximum_maximum_fusion.1), channel_id=1, source_target_pairs={{0,7},{1,0},{2,1},{3,2},{4,3},{5,4},{6,5},{7,6},{8,15},{9,8},{10,9... | collective-permute-start | bytes 12296 | tf_op jit(solution)/shard_map/ppermute | solution.py:59
  119.9 6.4 %collective-permute-start.32 = (f32[8,128]{1,0:T(8,128)S(1)}, f32[8,128]{1,0:T(8,128)S(1)}, u32[]{:S(2)}, u32[]{:S(2)}) collective-permute-start(f32[8,128]{1,0:T(8,128)S(1)} %maximum_maximum_fusion.1), channel_id=1, source_target_pairs={{0,6},{1,7},{2,0},{3,1},{4,2},{5,3},{6,4},{7,5},{8,14},{9,15},{10,... | collective-permute-start | bytes 12296 | tf_op jit(solution)/shard_map/ppermute | solution.py:59
  120.0 7.8 %collective-permute-start.31 = (f32[8,128]{1,0:T(8,128)S(1)}, f32[8,128]{1,0:T(8,128)S(1)}, u32[]{:S(2)}, u32[]{:S(2)}) collective-permute-start(f32[8,128]{1,0:T(8,128)S(1)} %maximum_maximum_fusion.1), channel_id=1, source_target_pairs={{0,5},{1,6},{2,7},{3,0},{4,1},{5,2},{6,3},{7,4},{8,13},{9,14},{10,... | collective-permute-start | bytes 12296 | tf_op jit(solution)/shard_map/ppermute | solution.py:59
  121.3 6.5 %collective-permute-start.30 = (f32[8,128]{1,0:T(8,128)S(1)}, f32[8,128]{1,0:T(8,128)S(1)}, u32[]{:S(2)}, u32[]{:S(2)}) collective-permute-start(f32[8,128]{1,0:T(8,128)S(1)} %maximum_maximum_fusion.1), channel_id=1, source_target_pairs={{0,4},{1,5},{2,6},{3,7},{4,0},{5,1},{6,2},{7,3},{8,12},{9,13},{10,... | collective-permute-start | bytes 12296 | tf_op jit(solution)/shard_map/ppermute | solution.py:59
  124.3 5.4 %collective-permute-start.29 = (f32[8,128]{1,0:T(8,128)S(1)}, f32[8,128]{1,0:T(8,128)S(1)}, u32[]{:S(2)}, u32[]{:S(2)}) collective-permute-start(f32[8,128]{1,0:T(8,128)S(1)} %maximum_maximum_fusion.1), channel_id=1, source_target_pairs={{0,3},{1,4},{2,5},{3,6},{4,7},{5,0},{6,1},{7,2},{8,11},{9,12},{10,... | collective-permute-start | bytes 12296 | tf_op jit(solution)/shard_map/ppermute | solution.py:59
  124.3 5.5 %collective-permute-start.28 = (f32[8,128]{1,0:T(8,128)S(1)}, f32[8,128]{1,0:T(8,128)S(1)}, u32[]{:S(2)}, u32[]{:S(2)}) collective-permute-start(f32[8,128]{1,0:T(8,128)S(1)} %maximum_maximum_fusion.1), channel_id=1, source_target_pairs={{0,2},{1,3},{2,4},{3,5},{4,6},{5,7},{6,0},{7,1},{8,10},{9,11},{10,... | collective-permute-start | bytes 12296 | tf_op jit(solution)/shard_map/ppermute | solution.py:59
  126.3 6.3 %collective-permute-start.27 = (f32[8,128]{1,0:T(8,128)S(1)}, f32[8,128]{1,0:T(8,128)S(1)}, u32[]{:S(2)}, u32[]{:S(2)}) collective-permute-start(f32[8,128]{1,0:T(8,128)S(1)} %maximum_maximum_fusion.1), channel_id=1, source_target_pairs={{0,1},{1,2},{2,3},{3,4},{4,5},{5,6},{6,7},{7,0},{8,9},{9,10},{10,1... | collective-permute-start | bytes 12296 | tf_op jit(solution)/shard_map/ppermute | solution.py:59
  (2 other events, 3.9 us)

commit v4 on v3

--- a/solution.py
+++ b/solution.py
@@ -48,7 +48,7 @@
         count = lax.axis_size(axis)
         window = 1
         while window < count:
-            radix = next(k for k in (8, 4, 2, 3, count // window) if (count // window) % k == 0)
+            radix = next(k for k in (4, 2, 3, count // window) if (count // window) % k == 0)
             got = [part]
             for k in range(1, radix):
                 group = radix * window
@@ -173,7 +173,7 @@
         aux_ref[1, r0, pl.ds(c0, 1), :] = occupied / diagonal
         u_ref[r0, pl.ds(c0, 1), :] = field(3, r, c) / diagonal
 
-    loop_cells(2, rows_all - 2, 2, cols_all - 2, weights)
+    loop_cells(2, rows_all - 2, 2, cols_all - 2, weights, 5)
     dens_ref[...] = full_ref[halo:halo + rows, halo:halo + cols, :]
 
 

time: 134 us -> 126 us (0.940)
  starting transfers between devices: 54.6 us -> 45.1 us
  waiting for transfers between devices: 38.9 us -> 42.4 us
  Pallas kernels: 35.8 us -> 34.3 us
    ppermute x20 -> x14, starting transfers between devices: 22.2 us -> 12.6 us  [combined(): got.append(lax.ppermute(part, axis, pairs))]
    ppermute x20 -> x14, waiting for transfers between devices: 17.1 us -> 20.6 us  [combined(): got.append(lax.ppermute(part, axis, pairs))]
    pallas_call x1, Pallas kernels: 27.5 us -> 26 us  [body(): pl.pallas_call(setup_kernel, out_shape=(own, WEIGHT_SPACE((span_r * span_...]
  transfers between devices with their start and end apart: 34 -> 28, of which waited for: 18 -> 19; matrix products, arithmetic and copies ran while one was open for 1% -> 1% of each run, Pallas kernels for 0% -> 0%
where the time goes in v4:
time: 126 us
  starting transfers between devices  45.1 us (36%)
  waiting for transfers between devices  42.4 us (34%)
  Pallas kernels  34.3 us (27%)
  other arithmetic  2.36 us (2%)
    pallas_call x1, Pallas kernels, body(): pl.pallas_call(setup_kernel, out_shape=(own, WEIGHT_SPACE((span_r * span_...  26 us
    ppermute x7, starting transfers between devices, extended(): lows.insert(0, lax.ppermute(tail, axis, up))  23.4 us
    ppermute x14, waiting for transfers between devices, combined(): got.append(lax.ppermute(part, axis, pairs))  20.6 us
    ppermute x7, waiting for transfers between devices, extended(): highs.append(lax.ppermute(head, axis, down))  20.3 us
    ppermute x14, starting transfers between devices, combined(): got.append(lax.ppermute(part, axis, pairs))  12.6 us
    ppermute x7, starting transfers between devices, extended(): highs.append(lax.ppermute(head, axis, down))  9.04 us
    pallas_call x3, Pallas kernels, body(): pl.pallas_call(lambda *refs, a=first, n=count, z=last: products_kernel(a,...  7.36 us
  transfers between devices with their start and end apart: 28, of which 19 were waited for; matrix products, arithmetic and copies ran while one was open for 1% of the time, Pallas kernels for 0%

profile of v4, /device:TPU:0, one launch (start us, length us, event | category | flops | bytes accessed | tf_op | source)
XLA Modules:
  0.0 125.6 jit_solution(16723197117584584299)
XLA Ops:
  2.2 4.9 %collective-permute-start = (f32[4,1,8,128]{3,2,1,0:T(8,128)S(1)}, f32[4,1,8,128]{3,2,1,0:T(8,128)S(1)}, u32[]{:S(2)}, u32[]{:S(2)}) collective-permute-start(f32[4,1,8,128]{3,2,1,0:T(8,128)S(1)} %get-tuple-element.31), channel_id=1, source_target_pairs={{0,16},{8,24},{1,17},{9,25},{2,18},{10,26},{3,19},{11,27},{4,20},{... | collective-permute-start | bytes 49160 | tf_op jit(solution)/shard_map/ppermute | solution.py:35
  7.1 1.3 %collective-permute-start.2 = (f32[4,2,8,128]{3,2,1,0:T(8,128)S(1)}, f32[4,2,8,128]{3,2,1,0:T(8,128)S(1)}, u32[]{:S(2)}, u32[]{:S(2)}) collective-permute-start(f32[4,2,8,128]{3,2,1,0:T(8,128)S(1)} %pad_maximum_fusion.3), channel_id=1, source_target_pairs={{8,0},{16,8},{24,16},{9,1},{17,9},{25,17},{10,2},{18,10},{26,18},{... | collective-permute-start | bytes 98312 | tf_op jit(solution)/shard_map/ppermute | solution.py:36
  8.4 3.0 %collective-permute-start.1 = (f32[4,2,8,128]{3,2,1,0:T(8,128)S(1)}, f32[4,2,8,128]{3,2,1,0:T(8,128)S(1)}, u32[]{:S(2)}, u32[]{:S(2)}) collective-permute-start(f32[4,2,8,128]{3,2,1,0:T(8,128)S(1)} %pad_maximum_fusion.3), channel_id=1, source_target_pairs={{0,8},{8,16},{16,24},{1,9},{9,17},{17,25},{2,10},{10,18},{18,26},{... | collective-permute-start | bytes 98312 | tf_op jit(solution)/shard_map/ppermute | solution.py:35
  11.4 1.3 %collective-permute-start.3 = (f32[4,1,8,128]{3,2,1,0:T(8,128)S(1)}, f32[4,1,8,128]{3,2,1,0:T(8,128)S(1)}, u32[]{:S(2)}, u32[]{:S(2)}) collective-permute-start(f32[4,1,8,128]{3,2,1,0:T(8,128)S(1)} %get-tuple-element.30), channel_id=1, source_target_pairs={{16,0},{24,8},{17,1},{25,9},{18,2},{26,10},{19,3},{27,11},{20,4},{... | collective-permute-start | bytes 49160 | tf_op jit(solution)/shard_map/ppermute | solution.py:36
  13.5 3.6 %collective-permute-done.3 = f32[4,1,8,128]{3,2,1,0:T(8,128)S(1)} collective-permute-done((f32[4,1,8,128]{3,2,1,0:T(8,128)S(1)}, f32[4,1,8,128]{3,2,1,0:T(8,128)S(1)}, u32[]{:S(2)}, u32[]{:S(2)}) %collective-permute-start.3) | collective-permute-done | bytes 16416 | tf_op jit(solution)/shard_map/ppermute | solution.py:36
  17.1 3.4 %collective-permute-start.4 = (f32[4,8,3,128]{3,2,1,0:T(4,128)S(1)}, f32[4,8,3,128]{3,2,1,0:T(4,128)S(1)}, u32[]{:S(2)}, u32[]{:S(2)}) collective-permute-start(f32[4,8,3,128]{3,2,1,0:T(4,128)S(1)} %get-tuple-element.28), channel_id=1, source_target_pairs={{0,1},{1,2},{2,3},{3,4},{4,5},{5,6},{6,7},{8,9},{9,10},{10,11},{11... | collective-permute-start | bytes 147464 | tf_op jit(solution)/shard_map/ppermute | solution.py:35
  20.5 1.3 %collective-permute-start.5 = (f32[4,8,3,128]{3,2,1,0:T(4,128)S(1)}, f32[4,8,3,128]{3,2,1,0:T(4,128)S(1)}, u32[]{:S(2)}, u32[]{:S(2)}) collective-permute-start(f32[4,8,3,128]{3,2,1,0:T(4,128)S(1)} %get-tuple-element.29), channel_id=1, source_target_pairs={{1,0},{2,1},{3,2},{4,3},{5,4},{6,5},{7,6},{9,8},{10,9},{11,10},{12... | collective-permute-start | bytes 147464 | tf_op jit(solution)/shard_map/ppermute | solution.py:36
  22.3 4.3 %collective-permute-done.5 = f32[4,8,3,128]{3,2,1,0:T(4,128)S(1)} collective-permute-done((f32[4,8,3,128]{3,2,1,0:T(4,128)S(1)}, f32[4,8,3,128]{3,2,1,0:T(4,128)S(1)}, u32[]{:S(2)}, u32[]{:S(2)}) %collective-permute-start.5) | collective-permute-done | bytes 49184 | tf_op jit(solution)/shard_map/ppermute | solution.py:36
  26.7 26.0 %setup.1 = (f32[2,8,128]{2,1,0:T(8,128)}, f32[40,9,128,128]{3,2,1,0:T(8,128)S(1)}, f32[2,4,10,128]{3,2,1,0:T(8,128)S(1)}, f32[4,10,128]{2,1,0:T(8,128)S(1)}) custom-call(f32[4,8,14,128]{3,2,1,0:T(8,128)S(1)} %pad_maximum_fusion.f_ref), custom_call_target="tpu_custom_call" | custom-call | tf_op jit(solution)/shard_map/setup/pallas_call | solution.py:308
  53.6 1.3 %collective-permute-start.7 = (f32[2,8,128]{2,1,0:T(8,128)S(1)}, f32[2,8,128]{2,1,0:T(8,128)S(1)}, u32[]{:S(2)}, u32[]{:S(2)}) collective-permute-start(f32[2,8,128]{2,1,0:T(8,128)S(1)} %products_0.1.refs_4_.refs_1_), channel_id=1, source_target_pairs={{8,0},{16,8},{24,16},{9,1},{17,9},{25,17},{10,2},{18,10},{26,18},{... | collective-permute-start | bytes 24584 | tf_op jit(solution)/shard_map/ppermute | solution.py:36
  54.9 3.0 %collective-permute-start.6 = (f32[2,8,128]{2,1,0:T(8,128)S(1)}, f32[2,8,128]{2,1,0:T(8,128)S(1)}, u32[]{:S(2)}, u32[]{:S(2)}) collective-permute-start(f32[2,8,128]{2,1,0:T(8,128)S(1)} %products_0.1.refs_4_.refs_1_), channel_id=1, source_target_pairs={{0,8},{8,16},{16,24},{1,9},{9,17},{17,25},{2,10},{10,18},{18,26},{... | collective-permute-start | bytes 24584 | tf_op jit(solution)/shard_map/ppermute | solution.py:35
  58.8 4.3 %collective-permute-start.8 = (f32[6,2,128]{2,1,0:T(2,128)S(1)}, f32[6,2,128]{2,1,0:T(2,128)S(1)}, u32[]{:S(2)}, u32[]{:S(2)}) collective-permute-start(f32[6,2,128]{2,1,0:T(2,128)S(1)} %get-tuple-element.34), channel_id=1, source_target_pairs={{0,1},{1,2},{2,3},{3,4},{4,5},{5,6},{6,7},{8,9},{9,10},{10,11},{11... | collective-permute-start | bytes 18440 | tf_op jit(solution)/shard_map/ppermute | solution.py:35
  63.1 1.3 %collective-permute-start.9 = (f32[6,2,128]{2,1,0:T(2,128)S(1)}, f32[6,2,128]{2,1,0:T(2,128)S(1)}, u32[]{:S(2)}, u32[]{:S(2)}) collective-permute-start(f32[6,2,128]{2,1,0:T(2,128)S(1)} %get-tuple-element.35), channel_id=1, source_target_pairs={{1,0},{2,1},{3,2},{4,3},{5,4},{6,5},{7,6},{9,8},{10,9},{11,10},{12... | collective-permute-start | bytes 18440 | tf_op jit(solution)/shard_map/ppermute | solution.py:36
  64.5 4.2 %collective-permute-done.9 = f32[6,2,128]{2,1,0:T(2,128)S(1)} collective-permute-done((f32[6,2,128]{2,1,0:T(2,128)S(1)}, f32[6,2,128]{2,1,0:T(2,128)S(1)}, u32[]{:S(2)}, u32[]{:S(2)}) %collective-permute-start.9) | collective-permute-done | bytes 6176 | tf_op jit(solution)/shard_map/ppermute | solution.py:36
  68.7 3.2 %products_1.1 = (f32[2,8,128]{2,1,0:T(8,128)S(1)}, f32[2,8,128]{2,1,0:T(8,128)S(1)}) custom-call(f32[40,9,128,128]{3,2,1,0:T(8,128)S(1)} %get-tuple-element.17.refs_0_, f32[2,4,10,128]{3,2,1,0:T(8,128)S(1)} %get-tuple-element.18.refs_1_.aux_ref, f32[6,12,128]{2,1,0:T(8,128)S(1)} %pad_maximum_fusion.1.refs_2_), custom_call_target="tpu_custom_call" | custom-call | tf_op jit(solution)/shard_map/products_1/pallas_call | solution.py:343
  73.2 1.3 %collective-permute-start.11 = (f32[2,8,128]{2,1,0:T(8,128)S(1)}, f32[2,8,128]{2,1,0:T(8,128)S(1)}, u32[]{:S(2)}, u32[]{:S(2)}) collective-permute-start(f32[2,8,128]{2,1,0:T(8,128)S(1)} %get-tuple-element.20.refs_6_.refs_3_), channel_id=1, source_target_pairs={{8,0},{16,8},{24,16},{9,1},{17,9},{25,17},{10,2},{18,10},{26,18},{... | collective-permute-start | bytes 24584 | tf_op jit(solution)/shard_map/ppermute | solution.py:36
  74.5 4.1 %collective-permute-done.11 = f32[2,8,128]{2,1,0:T(8,128)S(1)} collective-permute-done((f32[2,8,128]{2,1,0:T(8,128)S(1)}, f32[2,8,128]{2,1,0:T(8,128)S(1)}, u32[]{:S(2)}, u32[]{:S(2)}) %collective-permute-start.11) | collective-permute-done | bytes 8224 | tf_op jit(solution)/shard_map/ppermute | solution.py:36
  78.6 3.4 %collective-permute-start.12 = (f32[6,2,128]{2,1,0:T(2,128)S(1)}, f32[6,2,128]{2,1,0:T(2,128)S(1)}, u32[]{:S(2)}, u32[]{:S(2)}) collective-permute-start(f32[6,2,128]{2,1,0:T(2,128)S(1)} %get-tuple-element.32), channel_id=1, source_target_pairs={{0,1},{1,2},{2,3},{3,4},{4,5},{5,6},{6,7},{8,9},{9,10},{10,11},{11... | collective-permute-start | bytes 18440 | tf_op jit(solution)/shard_map/ppermute | solution.py:35
  83.3 4.2 %collective-permute-done.13 = f32[6,2,128]{2,1,0:T(2,128)S(1)} collective-permute-done((f32[6,2,128]{2,1,0:T(2,128)S(1)}, f32[6,2,128]{2,1,0:T(2,128)S(1)}, u32[]{:S(2)}, u32[]{:S(2)}) %collective-permute-start.13) | collective-permute-done | bytes 6176 | tf_op jit(solution)/shard_map/ppermute | solution.py:36
  87.6 3.2 %products_3.1 = (f32[2,8,128]{2,1,0:T(8,128)S(1)}, f32[2,8,128]{2,1,0:T(8,128)S(1)}, f32[24,128]{1,0:T(8,128)S(1)}) custom-call(f32[40,9,128,128]{3,2,1,0:T(8,128)S(1)} %get-tuple-element.17.refs_0_, f32[2,4,10,128]{3,2,1,0:T(8,128)S(1)} %get-tuple-element.18.refs_1_.aux_ref, f32[6,12,128]{2,1,0:T(8,128)S(1)} %pad_maximum_fusion.2.refs_2_, ...), custom_call_target="tpu_custom_call" | custom-call | tf_op jit(solution)/shard_map/products_3/pallas_call | solution.py:343
  90.9 2.6 %collective-permute-start.15 = (f32[24,128]{1,0:T(8,128)S(1)}, f32[24,128]{1,0:T(8,128)S(1)}, u32[]{:S(2)}, u32[]{:S(2)}) collective-permute-start(f32[24,128]{1,0:T(8,128)S(1)} %get-tuple-element.22), channel_id=1, source_target_pairs={{0,16},{8,24},{16,0},{24,8},{1,17},{9,25},{17,1},{25,9},{2,18},{10... | collective-permute-start | bytes 36872 | tf_op jit(solution)/shard_map/ppermute | solution.py:59
  93.4 1.8 %collective-permute-done.15 = f32[24,128]{1,0:T(8,128)S(1)} collective-permute-done((f32[24,128]{1,0:T(8,128)S(1)}, f32[24,128]{1,0:T(8,128)S(1)}, u32[]{:S(2)}, u32[]{:S(2)}) %collective-permute-start.15) | collective-permute-done | bytes 12320 | tf_op jit(solution)/shard_map/ppermute | solution.py:59
  95.2 1.3 %collective-permute-done.14 = f32[24,128]{1,0:T(8,128)S(1)} collective-permute-done((f32[24,128]{1,0:T(8,128)S(1)}, f32[24,128]{1,0:T(8,128)S(1)}, u32[]{:S(2)}, u32[]{:S(2)}) %collective-permute-start.14) | collective-permute-done | bytes 12320 | tf_op jit(solution)/shard_map/ppermute | solution.py:59
  96.6 3.5 %collective-permute-start.19 = (f32[24,128]{1,0:T(8,128)S(1)}, f32[24,128]{1,0:T(8,128)S(1)}, u32[]{:S(2)}, u32[]{:S(2)}) collective-permute-start(f32[24,128]{1,0:T(8,128)S(1)} %add_add_fusion.1), channel_id=1, source_target_pairs={{0,3},{1,0},{2,1},{3,2},{4,7},{5,4},{6,5},{7,6},{8,11},{9,8},{10,9... | collective-permute-start | bytes 36872 | tf_op jit(solution)/shard_map/ppermute | solution.py:59
  101.4 2.3 %collective-permute-done.18 = f32[24,128]{1,0:T(8,128)S(1)} collective-permute-done((f32[24,128]{1,0:T(8,128)S(1)}, f32[24,128]{1,0:T(8,128)S(1)}, u32[]{:S(2)}, u32[]{:S(2)}) %collective-permute-start.18) | collective-permute-done | bytes 12320 | tf_op jit(solution)/shard_map/ppermute | solution.py:59
  103.7 1.4 %collective-permute-done.17 = f32[24,128]{1,0:T(8,128)S(1)} collective-permute-done((f32[24,128]{1,0:T(8,128)S(1)}, f32[24,128]{1,0:T(8,128)S(1)}, u32[]{:S(2)}, u32[]{:S(2)}) %collective-permute-start.17) | collective-permute-done | bytes 12320 | tf_op jit(solution)/shard_map/ppermute | solution.py:59
  106.4 3.3 %collective-permute-done.20 = f32[24,128]{1,0:T(8,128)S(1)} collective-permute-done((f32[24,128]{1,0:T(8,128)S(1)}, f32[24,128]{1,0:T(8,128)S(1)}, u32[]{:S(2)}, u32[]{:S(2)}) %collective-permute-start.20) | collective-permute-done | bytes 12320 | tf_op jit(solution)/shard_map/ppermute | solution.py:59
  112.0 2.3 %collective-permute-done.22 = f32[8,128]{1,0:T(8,128)S(1)} collective-permute-done((f32[8,128]{1,0:T(8,128)S(1)}, f32[8,128]{1,0:T(8,128)S(1)}, u32[]{:S(2)}, u32[]{:S(2)}) %collective-permute-start.22) | collective-permute-done | bytes 4128 | tf_op jit(solution)/shard_map/ppermute | solution.py:59
  114.4 1.5 %collective-permute-start.25 = (f32[8,128]{1,0:T(8,128)S(1)}, f32[8,128]{1,0:T(8,128)S(1)}, u32[]{:S(2)}, u32[]{:S(2)}) collective-permute-start(f32[8,128]{1,0:T(8,128)S(1)} %maximum_maximum_fusion.1), channel_id=1, source_target_pairs={{0,2},{1,3},{2,0},{3,1},{4,6},{5,7},{6,4},{7,5},{8,10},{9,11},{10,... | collective-permute-start | bytes 12296 | tf_op jit(solution)/shard_map/ppermute | solution.py:59
  115.9 1.9 %collective-permute-start.24 = (f32[8,128]{1,0:T(8,128)S(1)}, f32[8,128]{1,0:T(8,128)S(1)}, u32[]{:S(2)}, u32[]{:S(2)}) collective-permute-start(f32[8,128]{1,0:T(8,128)S(1)} %maximum_maximum_fusion.1), channel_id=1, source_target_pairs={{0,1},{1,2},{2,3},{3,0},{4,5},{5,6},{6,7},{7,4},{8,9},{9,10},{10,1... | collective-permute-start | bytes 12296 | tf_op jit(solution)/shard_map/ppermute | solution.py:59
  118.1 2.4 %collective-permute-done.24 = f32[8,128]{1,0:T(8,128)S(1)} collective-permute-done((f32[8,128]{1,0:T(8,128)S(1)}, f32[8,128]{1,0:T(8,128)S(1)}, u32[]{:S(2)}, u32[]{:S(2)}) %collective-permute-start.24) | collective-permute-done | bytes 4128 | tf_op jit(solution)/shard_map/ppermute | solution.py:59
  120.7 4.2 %collective-permute-done.27 = f32[8,128]{1,0:T(8,128)S(1)} collective-permute-done((f32[8,128]{1,0:T(8,128)S(1)}, f32[8,128]{1,0:T(8,128)S(1)}, u32[]{:S(2)}, u32[]{:S(2)}) %collective-permute-start.27) | collective-permute-done | bytes 4128 | tf_op jit(solution)/shard_map/ppermute | solution.py:59
  (53 shorter events, 13.6 us)
Async XLA Ops:
  2.2 10.5 %collective-permute-start = (f32[4,1,8,128]{3,2,1,0:T(8,128)S(1)}, f32[4,1,8,128]{3,2,1,0:T(8,128)S(1)}, u32[]{:S(2)}, u32[]{:S(2)}) collective-permute-start(f32[4,1,8,128]{3,2,1,0:T(8,128)S(1)} %get-tuple-element.31), channel_id=1, source_target_pairs={{0,16},{8,24},{1,17},{9,25},{2,18},{10,26},{3,19},{11,27},{4,20},{... | collective-permute-start | bytes 49160 | tf_op jit(solution)/shard_map/ppermute | solution.py:35
  7.1 6.4 %collective-permute-start.2 = (f32[4,2,8,128]{3,2,1,0:T(8,128)S(1)}, f32[4,2,8,128]{3,2,1,0:T(8,128)S(1)}, u32[]{:S(2)}, u32[]{:S(2)}) collective-permute-start(f32[4,2,8,128]{3,2,1,0:T(8,128)S(1)} %pad_maximum_fusion.3), channel_id=1, source_target_pairs={{8,0},{16,8},{24,16},{9,1},{17,9},{25,17},{10,2},{18,10},{26,18},{... | collective-permute-start | bytes 98312 | tf_op jit(solution)/shard_map/ppermute | solution.py:36
  8.4 4.4 %collective-permute-start.1 = (f32[4,2,8,128]{3,2,1,0:T(8,128)S(1)}, f32[4,2,8,128]{3,2,1,0:T(8,128)S(1)}, u32[]{:S(2)}, u32[]{:S(2)}) collective-permute-start(f32[4,2,8,128]{3,2,1,0:T(8,128)S(1)} %pad_maximum_fusion.3), channel_id=1, source_target_pairs={{0,8},{8,16},{16,24},{1,9},{9,17},{17,25},{2,10},{10,18},{18,26},{... | collective-permute-start | bytes 98312 | tf_op jit(solution)/shard_map/ppermute | solution.py:35
  11.4 5.6 %collective-permute-start.3 = (f32[4,1,8,128]{3,2,1,0:T(8,128)S(1)}, f32[4,1,8,128]{3,2,1,0:T(8,128)S(1)}, u32[]{:S(2)}, u32[]{:S(2)}) collective-permute-start(f32[4,1,8,128]{3,2,1,0:T(8,128)S(1)} %get-tuple-element.30), channel_id=1, source_target_pairs={{16,0},{24,8},{17,1},{25,9},{18,2},{26,10},{19,3},{27,11},{20,4},{... | collective-permute-start | bytes 49160 | tf_op jit(solution)/shard_map/ppermute | solution.py:36
  17.1 5.3 %collective-permute-start.4 = (f32[4,8,3,128]{3,2,1,0:T(4,128)S(1)}, f32[4,8,3,128]{3,2,1,0:T(4,128)S(1)}, u32[]{:S(2)}, u32[]{:S(2)}) collective-permute-start(f32[4,8,3,128]{3,2,1,0:T(4,128)S(1)} %get-tuple-element.28), channel_id=1, source_target_pairs={{0,1},{1,2},{2,3},{3,4},{4,5},{5,6},{6,7},{8,9},{9,10},{10,11},{11... | collective-permute-start | bytes 147464 | tf_op jit(solution)/shard_map/ppermute | solution.py:35
  20.5 6.2 %collective-permute-start.5 = (f32[4,8,3,128]{3,2,1,0:T(4,128)S(1)}, f32[4,8,3,128]{3,2,1,0:T(4,128)S(1)}, u32[]{:S(2)}, u32[]{:S(2)}) collective-permute-start(f32[4,8,3,128]{3,2,1,0:T(4,128)S(1)} %get-tuple-element.29), channel_id=1, source_target_pairs={{1,0},{2,1},{3,2},{4,3},{5,4},{6,5},{7,6},{9,8},{10,9},{11,10},{12... | collective-permute-start | bytes 147464 | tf_op jit(solution)/shard_map/ppermute | solution.py:36
  53.6 4.3 %collective-permute-start.7 = (f32[2,8,128]{2,1,0:T(8,128)S(1)}, f32[2,8,128]{2,1,0:T(8,128)S(1)}, u32[]{:S(2)}, u32[]{:S(2)}) collective-permute-start(f32[2,8,128]{2,1,0:T(8,128)S(1)} %products_0.1.refs_4_.refs_1_), channel_id=1, source_target_pairs={{8,0},{16,8},{24,16},{9,1},{17,9},{25,17},{10,2},{18,10},{26,18},{... | collective-permute-start | bytes 24584 | tf_op jit(solution)/shard_map/ppermute | solution.py:36
  54.9 3.8 %collective-permute-start.6 = (f32[2,8,128]{2,1,0:T(8,128)S(1)}, f32[2,8,128]{2,1,0:T(8,128)S(1)}, u32[]{:S(2)}, u32[]{:S(2)}) collective-permute-start(f32[2,8,128]{2,1,0:T(8,128)S(1)} %products_0.1.refs_4_.refs_1_), channel_id=1, source_target_pairs={{0,8},{8,16},{16,24},{1,9},{9,17},{17,25},{2,10},{10,18},{18,26},{... | collective-permute-start | bytes 24584 | tf_op jit(solution)/shard_map/ppermute | solution.py:35
  58.8 5.7 %collective-permute-start.8 = (f32[6,2,128]{2,1,0:T(2,128)S(1)}, f32[6,2,128]{2,1,0:T(2,128)S(1)}, u32[]{:S(2)}, u32[]{:S(2)}) collective-permute-start(f32[6,2,128]{2,1,0:T(2,128)S(1)} %get-tuple-element.34), channel_id=1, source_target_pairs={{0,1},{1,2},{2,3},{3,4},{4,5},{5,6},{6,7},{8,9},{9,10},{10,11},{11... | collective-permute-start | bytes 18440 | tf_op jit(solution)/shard_map/ppermute | solution.py:35
  63.1 5.5 %collective-permute-start.9 = (f32[6,2,128]{2,1,0:T(2,128)S(1)}, f32[6,2,128]{2,1,0:T(2,128)S(1)}, u32[]{:S(2)}, u32[]{:S(2)}) collective-permute-start(f32[6,2,128]{2,1,0:T(2,128)S(1)} %get-tuple-element.35), channel_id=1, source_target_pairs={{1,0},{2,1},{3,2},{4,3},{5,4},{6,5},{7,6},{9,8},{10,9},{11,10},{12... | collective-permute-start | bytes 18440 | tf_op jit(solution)/shard_map/ppermute | solution.py:36
  71.9 2.6 %collective-permute-start.10 = (f32[2,8,128]{2,1,0:T(8,128)S(1)}, f32[2,8,128]{2,1,0:T(8,128)S(1)}, u32[]{:S(2)}, u32[]{:S(2)}) collective-permute-start(f32[2,8,128]{2,1,0:T(8,128)S(1)} %get-tuple-element.20.refs_6_.refs_3_), channel_id=1, source_target_pairs={{0,8},{8,16},{16,24},{1,9},{9,17},{17,25},{2,10},{10,18},{18,26},{... | collective-permute-start | bytes 24584 | tf_op jit(solution)/shard_map/ppermute | solution.py:35
  73.2 5.4 %collective-permute-start.11 = (f32[2,8,128]{2,1,0:T(8,128)S(1)}, f32[2,8,128]{2,1,0:T(8,128)S(1)}, u32[]{:S(2)}, u32[]{:S(2)}) collective-permute-start(f32[2,8,128]{2,1,0:T(8,128)S(1)} %get-tuple-element.20.refs_6_.refs_3_), channel_id=1, source_target_pairs={{8,0},{16,8},{24,16},{9,1},{17,9},{25,17},{10,2},{18,10},{26,18},{... | collective-permute-start | bytes 24584 | tf_op jit(solution)/shard_map/ppermute | solution.py:36
  78.6 4.7 %collective-permute-start.12 = (f32[6,2,128]{2,1,0:T(2,128)S(1)}, f32[6,2,128]{2,1,0:T(2,128)S(1)}, u32[]{:S(2)}, u32[]{:S(2)}) collective-permute-start(f32[6,2,128]{2,1,0:T(2,128)S(1)} %get-tuple-element.32), channel_id=1, source_target_pairs={{0,1},{1,2},{2,3},{3,4},{4,5},{5,6},{6,7},{8,9},{9,10},{10,11},{11... | collective-permute-start | bytes 18440 | tf_op jit(solution)/shard_map/ppermute | solution.py:35
  82.0 5.5 %collective-permute-start.13 = (f32[6,2,128]{2,1,0:T(2,128)S(1)}, f32[6,2,128]{2,1,0:T(2,128)S(1)}, u32[]{:S(2)}, u32[]{:S(2)}) collective-permute-start(f32[6,2,128]{2,1,0:T(2,128)S(1)} %get-tuple-element.33), channel_id=1, source_target_pairs={{1,0},{2,1},{3,2},{4,3},{5,4},{6,5},{7,6},{9,8},{10,9},{11,10},{12... | collective-permute-start | bytes 18440 | tf_op jit(solution)/shard_map/ppermute | solution.py:36
  90.8 2.7 %collective-permute-start.16 = (f32[24,128]{1,0:T(8,128)S(1)}, f32[24,128]{1,0:T(8,128)S(1)}, u32[]{:S(2)}, u32[]{:S(2)}) collective-permute-start(f32[24,128]{1,0:T(8,128)S(1)} %get-tuple-element.22), channel_id=1, source_target_pairs={{0,24},{8,0},{16,8},{24,16},{1,25},{9,1},{17,9},{25,17},{2,26},{10... | collective-permute-start | bytes 36872 | tf_op jit(solution)/shard_map/ppermute | solution.py:59
  90.9 4.4 %collective-permute-start.15 = (f32[24,128]{1,0:T(8,128)S(1)}, f32[24,128]{1,0:T(8,128)S(1)}, u32[]{:S(2)}, u32[]{:S(2)}) collective-permute-start(f32[24,128]{1,0:T(8,128)S(1)} %get-tuple-element.22), channel_id=1, source_target_pairs={{0,16},{8,24},{16,0},{24,8},{1,17},{9,25},{17,1},{25,9},{2,18},{10... | collective-permute-start | bytes 36872 | tf_op jit(solution)/shard_map/ppermute | solution.py:59
  93.4 3.1 %collective-permute-start.14 = (f32[24,128]{1,0:T(8,128)S(1)}, f32[24,128]{1,0:T(8,128)S(1)}, u32[]{:S(2)}, u32[]{:S(2)}) collective-permute-start(f32[24,128]{1,0:T(8,128)S(1)} %get-tuple-element.22), channel_id=1, source_target_pairs={{0,8},{8,16},{16,24},{24,0},{1,9},{9,17},{17,25},{25,1},{2,10},{10... | collective-permute-start | bytes 36872 | tf_op jit(solution)/shard_map/ppermute | solution.py:59
  96.6 4.9 %collective-permute-start.19 = (f32[24,128]{1,0:T(8,128)S(1)}, f32[24,128]{1,0:T(8,128)S(1)}, u32[]{:S(2)}, u32[]{:S(2)}) collective-permute-start(f32[24,128]{1,0:T(8,128)S(1)} %add_add_fusion.1), channel_id=1, source_target_pairs={{0,3},{1,0},{2,1},{3,2},{4,7},{5,4},{6,5},{7,6},{8,11},{9,8},{10,9... | collective-permute-start | bytes 36872 | tf_op jit(solution)/shard_map/ppermute | solution.py:59
  100.0 3.7 %collective-permute-start.18 = (f32[24,128]{1,0:T(8,128)S(1)}, f32[24,128]{1,0:T(8,128)S(1)}, u32[]{:S(2)}, u32[]{:S(2)}) collective-permute-start(f32[24,128]{1,0:T(8,128)S(1)} %add_add_fusion.1), channel_id=1, source_target_pairs={{0,2},{1,3},{2,0},{3,1},{4,6},{5,7},{6,4},{7,5},{8,10},{9,11},{10,... | collective-permute-start | bytes 36872 | tf_op jit(solution)/shard_map/ppermute | solution.py:59
  100.5 4.7 %collective-permute-start.17 = (f32[24,128]{1,0:T(8,128)S(1)}, f32[24,128]{1,0:T(8,128)S(1)}, u32[]{:S(2)}, u32[]{:S(2)}) collective-permute-start(f32[24,128]{1,0:T(8,128)S(1)} %add_add_fusion.1), channel_id=1, source_target_pairs={{0,1},{1,2},{2,3},{3,0},{4,5},{5,6},{6,7},{7,4},{8,9},{9,10},{10,1... | collective-permute-start | bytes 36872 | tf_op jit(solution)/shard_map/ppermute | solution.py:59
  105.2 4.6 %collective-permute-start.20 = (f32[24,128]{1,0:T(8,128)S(1)}, f32[24,128]{1,0:T(8,128)S(1)}, u32[]{:S(2)}, u32[]{:S(2)}) collective-permute-start(f32[24,128]{1,0:T(8,128)S(1)} %add_add_fusion), channel_id=1, source_target_pairs={{0,4},{1,5},{2,6},{3,7},{4,0},{5,1},{6,2},{7,3},{8,12},{9,13},{10,... | collective-permute-start | bytes 36872 | tf_op jit(solution)/shard_map/ppermute | solution.py:59
  110.7 1.3 %collective-permute-start.23 = (f32[8,128]{1,0:T(8,128)S(1)}, f32[8,128]{1,0:T(8,128)S(1)}, u32[]{:S(2)}, u32[]{:S(2)}) collective-permute-start(f32[8,128]{1,0:T(8,128)S(1)} %get-tuple-element.27), channel_id=1, source_target_pairs={{0,24},{8,0},{16,8},{24,16},{1,25},{9,1},{17,9},{25,17},{2,26},{10... | collective-permute-start | bytes 12296 | tf_op jit(solution)/shard_map/ppermute | solution.py:59
  110.7 3.6 %collective-permute-start.22 = (f32[8,128]{1,0:T(8,128)S(1)}, f32[8,128]{1,0:T(8,128)S(1)}, u32[]{:S(2)}, u32[]{:S(2)}) collective-permute-start(f32[8,128]{1,0:T(8,128)S(1)} %get-tuple-element.27), channel_id=1, source_target_pairs={{0,16},{8,24},{16,0},{24,8},{1,17},{9,25},{17,1},{25,9},{2,18},{10... | collective-permute-start | bytes 12296 | tf_op jit(solution)/shard_map/ppermute | solution.py:59
  111.2 3.1 %collective-permute-start.21 = (f32[8,128]{1,0:T(8,128)S(1)}, f32[8,128]{1,0:T(8,128)S(1)}, u32[]{:S(2)}, u32[]{:S(2)}) collective-permute-start(f32[8,128]{1,0:T(8,128)S(1)} %get-tuple-element.27), channel_id=1, source_target_pairs={{0,8},{8,16},{16,24},{24,0},{1,9},{9,17},{17,25},{25,1},{2,10},{10... | collective-permute-start | bytes 12296 | tf_op jit(solution)/shard_map/ppermute | solution.py:59
  114.3 3.7 %collective-permute-start.26 = (f32[8,128]{1,0:T(8,128)S(1)}, f32[8,128]{1,0:T(8,128)S(1)}, u32[]{:S(2)}, u32[]{:S(2)}) collective-permute-start(f32[8,128]{1,0:T(8,128)S(1)} %maximum_maximum_fusion.1), channel_id=1, source_target_pairs={{0,3},{1,0},{2,1},{3,2},{4,7},{5,4},{6,5},{7,6},{8,11},{9,8},{10,9... | collective-permute-start | bytes 12296 | tf_op jit(solution)/shard_map/ppermute | solution.py:59
  114.4 3.7 %collective-permute-start.25 = (f32[8,128]{1,0:T(8,128)S(1)}, f32[8,128]{1,0:T(8,128)S(1)}, u32[]{:S(2)}, u32[]{:S(2)}) collective-permute-start(f32[8,128]{1,0:T(8,128)S(1)} %maximum_maximum_fusion.1), channel_id=1, source_target_pairs={{0,2},{1,3},{2,0},{3,1},{4,6},{5,7},{6,4},{7,5},{8,10},{9,11},{10,... | collective-permute-start | bytes 12296 | tf_op jit(solution)/shard_map/ppermute | solution.py:59
  115.9 4.5 %collective-permute-start.24 = (f32[8,128]{1,0:T(8,128)S(1)}, f32[8,128]{1,0:T(8,128)S(1)}, u32[]{:S(2)}, u32[]{:S(2)}) collective-permute-start(f32[8,128]{1,0:T(8,128)S(1)} %maximum_maximum_fusion.1), channel_id=1, source_target_pairs={{0,1},{1,2},{2,3},{3,0},{4,5},{5,6},{6,7},{7,4},{8,9},{9,10},{10,1... | collective-permute-start | bytes 12296 | tf_op jit(solution)/shard_map/ppermute | solution.py:59
  120.5 4.5 %collective-permute-start.27 = (f32[8,128]{1,0:T(8,128)S(1)}, f32[8,128]{1,0:T(8,128)S(1)}, u32[]{:S(2)}, u32[]{:S(2)}) collective-permute-start(f32[8,128]{1,0:T(8,128)S(1)} %maximum_maximum_fusion), channel_id=1, source_target_pairs={{0,4},{1,5},{2,6},{3,7},{4,0},{5,1},{6,2},{7,3},{8,12},{9,13},{10,... | collective-permute-start | bytes 12296 | tf_op jit(solution)/shard_map/ppermute | solution.py:59
